TPU v7x, 32 devices: a whole 2x2x4 slice. The times are simulated.
32 devices in a mesh: shard: 4 (over y, x), ctx: 4 (over z), tp: 2 (over core).
Axes of the slice: x: 2, y: 2, z: 4, core: 2. Of those that a mesh axis runs over, the one named last changes fastest.
Arguments:
- frames: bfloat16 [4, 2048, 768], P('shard', 'ctx'), may hold values from -6 to 6
- lengths: int32 [4], P('shard'), may hold values from 512 to 2048, as said below
- cotangent: bfloat16 [4, 2048, 768], P('shard', 'ctx'), may hold values from -6 to 6
- ln1_gain: float32 [768], replicated, may hold values from 0.5 to 1.5
- ln1_bias: float32 [768], replicated, may hold values from -1 to 1
- w_query: bfloat16 [768, 768], P(('shard', 'ctx'), 'tp'), may hold values from -0.3125 to 0.3125
- b_query: float32 [768], P('tp'), may hold values from -1 to 1
- w_key: bfloat16 [768, 768], P(('shard', 'ctx'), 'tp'), may hold values from -0.3125 to 0.3125
- w_value: bfloat16 [768, 768], P(('shard', 'ctx'), 'tp'), may hold values from -0.21875 to 0.21875
- b_value: float32 [768], P('tp'), may hold values from -1 to 1
- w_out: bfloat16 [768, 768], P('tp', ('shard', 'ctx')), may hold values from -1.25 to 1.25
- b_out: float32 [768], replicated, may hold values from -1 to 1
- ln2_gain: float32 [768], replicated, may hold values from 0.5 to 1.5
- ln2_bias: float32 [768], replicated, may hold values from -1 to 1
- w_up: bfloat16 [768, 3072], P(('shard', 'ctx'), 'tp'), may hold values from -0.21875 to 0.21875
- b_up: float32 [3072], P('tp'), may hold values from -1 to 1
- w_down: bfloat16 [3072, 768], P('tp', ('shard', 'ctx')), may hold values from -0.109375 to 0.109375
- b_down: float32 [768], replicated, may hold values from -1 to 1
Outputs:
- output: bfloat16 [4, 2048, 768], P('shard', 'ctx')
- grad_input: float32 [4, 2048, 768], P('shard', 'ctx')
- grad_ln1_gain: float32 [768], replicated
- grad_ln1_bias: float32 [768], replicated
- grad_w_query: float32 [768, 768], P(('shard', 'ctx'), 'tp')
- grad_b_query: float32 [768], P('tp')
- grad_w_key: float32 [768, 768], P(('shard', 'ctx'), 'tp')
- grad_w_value: float32 [768, 768], P(('shard', 'ctx'), 'tp')
- grad_b_value: float32 [768], P('tp')
- grad_w_out: float32 [768, 768], P('tp', ('shard', 'ctx'))
- grad_b_out: float32 [768], replicated
- grad_ln2_gain: float32 [768], replicated
- grad_ln2_bias: float32 [768], replicated
- grad_w_up: float32 [768, 3072], P(('shard', 'ctx'), 'tp')
- grad_b_up: float32 [3072], P('tp')
- grad_w_down: float32 [3072, 768], P('tp', ('shard', 'ctx'))
- grad_b_down: float32 [768], replicated
Inputs may be any that keep to these rules, and one draw needn't show every extreme that they name: lengths[s] is the number of live frames at the start of slot s, at least 512; at least one slot has exactly 2048.
All inputs are finite; a program needn't handle non-finite values.
Results may differ from a plain program's by a relative error of at most 0.018.
Values may be sent and summed in bfloat16 or wider, within the bound.
A program may use at most 128 MiB of HBM per device.

v0:
```python
import math

import jax
import jax.numpy as jnp
from jax import lax
from jax.sharding import PartitionSpec as P

HD = 64


EPSILON = 1e-05
INV_ROOT_TWO = 0.7071067811865476
INV_ROOT_TAU = 0.3989422804014327


def norm_rows(values, gain, shift):
    centred = values - jnp.mean(values, axis=-1, keepdims=True)
    inverse = lax.rsqrt(jnp.mean(centred * centred, axis=-1, keepdims=True) + EPSILON)
    normed = centred * inverse
    return (normed * gain + shift, normed, inverse)


def norm_back(grad_rows, normed, inverse, gain):
    scaled = grad_rows * gain
    inner = (
        scaled
        - jnp.mean(scaled, axis=-1, keepdims=True)
        - normed * jnp.mean(scaled * normed, axis=-1, keepdims=True)
    )
    return (inner * inverse, jnp.sum(grad_rows * normed, axis=0), jnp.sum(grad_rows, axis=0))


def gelu_slope(values):
    return (
        0.5 * (1.0 + lax.erf(values * INV_ROOT_TWO))
        + values * jnp.exp(-0.5 * values * values) * INV_ROOT_TAU
    )


def pair_scores(queries, block_keys, score_scale):
    return (
        jnp.einsum("qhd,khd->hqk", queries, block_keys, preferred_element_type=jnp.float32)
        * score_scale
    )


def live_weights(scores, query_live, key_live, log_totals):
    both_live = query_live[None, :, None] & key_live[None, None, :]
    return jnp.where(both_live, jnp.exp(scores - log_totals[:, :, None]), 0.0)


def in_blocks(array, block_rows):
    return array.reshape((array.shape[0] // block_rows, block_rows) + array.shape[1:])


def slot_forward(queries, slot_keys, slot_values, query_live, key_live, key_block, score_scale):
    seg_rows, head_count, head_dim = queries.shape
    key_starts = jnp.arange(slot_keys.shape[0] // key_block, dtype=jnp.int32) * key_block
    blocks = (
        in_blocks(slot_keys, key_block),
        in_blocks(slot_values, key_block),
        in_blocks(key_live, key_block),
        key_starts,
    )
    start_state = (
        jnp.full((head_count, seg_rows), -jnp.inf, jnp.float32),
        jnp.zeros((head_count, seg_rows), jnp.float32),
    )

    def totals_step(carried, scan_item):
        block_keys, block_values, block_live, block_start = scan_item
        running_max, running_sum = carried
        scores = jnp.where(
            block_live[None, None, :], pair_scores(queries, block_keys, score_scale), -jnp.inf
        )
        new_max = jnp.maximum(running_max, jnp.max(scores, axis=-1))
        new_sum = running_sum * jnp.exp(running_max - new_max) + jnp.sum(
            jnp.exp(scores - new_max[:, :, None]), axis=-1
        )
        return ((new_max, new_sum), None)

    def whole_slot(ignored):
        final_state, unused = lax.scan(totals_step, start_state, blocks)
        log_totals = final_state[0] + jnp.log(final_state[1])

        def output_step(output_sum, scan_item):
            block_keys, block_values, block_live, block_start = scan_item
            weights_here = live_weights(
                pair_scores(queries, block_keys, score_scale), query_live, block_live, log_totals
            ).astype(jnp.bfloat16)
            return (
                output_sum
                + jnp.einsum(
                    "hqk,khd->qhd", weights_here, block_values, preferred_element_type=jnp.float32
                ),
                None,
            )

        attended, unused_too = lax.scan(
            output_step, jnp.zeros((seg_rows, head_count, head_dim), jnp.float32), blocks
        )
        return (log_totals, attended)

    return whole_slot(0)


def slot_back(
    queries,
    grad_att,
    log_totals,
    delta,
    slot_keys,
    slot_values,
    query_live,
    key_live,
    key_block,
    score_scale,
):
    seg_rows, head_count, head_dim = queries.shape
    key_starts = jnp.arange(slot_keys.shape[0] // key_block, dtype=jnp.int32) * key_block
    blocks = (
        in_blocks(slot_keys, key_block),
        in_blocks(slot_values, key_block),
        in_blocks(key_live, key_block),
        key_starts,
    )

    def grad_step(grad_query, scan_item):
        block_keys, block_values, block_live, block_start = scan_item
        partial_value = grad_query
        weights_full = live_weights(
            pair_scores(queries, block_keys, score_scale), query_live, block_live, log_totals
        )
        grad_probs = jnp.einsum(
            "qhd,khd->hqk", grad_att, block_values, preferred_element_type=jnp.float32
        )
        grad_scores = (weights_full * (grad_probs - delta[:, :, None])).astype(jnp.bfloat16)
        partial_value = (
            partial_value
            + jnp.einsum(
                "hqk,khd->qhd", grad_scores, block_keys, preferred_element_type=jnp.float32
            )
            * score_scale
        )
        grad_value = jnp.einsum(
            "hqk,qhd->khd",
            weights_full.astype(jnp.bfloat16),
            grad_att,
            preferred_element_type=jnp.float32,
        )
        grad_key = (
            jnp.einsum("hqk,qhd->khd", grad_scores, queries, preferred_element_type=jnp.float32)
            * score_scale
        )
        return (partial_value, (grad_key, grad_value))

    def whole_slot(ignored):
        grad_query, key_parts = lax.scan(
            grad_step, jnp.zeros((seg_rows, head_count, head_dim), jnp.float32), blocks
        )
        return (
            grad_query,
            key_parts[0].reshape(slot_keys.shape),
            key_parts[1].reshape(slot_keys.shape),
        )

    return whole_slot(0)


def per_device(
    frames,
    lengths,
    cotangent,
    ln1_gain,
    ln1_bias,
    w_query,
    b_query,
    w_key,
    w_value,
    b_value,
    w_out,
    b_out,
    ln2_gain,
    ln2_bias,
    w_up,
    b_up,
    w_down,
    b_down,
):
    slot_count, seg_rows, model_width = frames.shape
    row_count = slot_count * seg_rows
    head_cols = w_query.shape[1]
    head_count = head_cols // HD
    seq_length = seg_rows * lax.axis_size("ctx")
    seg_start = lax.axis_index("ctx") * seg_rows
    score_scale = HD ** (-0.5)
    key_block = math.gcd(seq_length, 512)
    positions = seg_start + jnp.arange(seg_rows, dtype=jnp.int32)
    query_live = positions[None, :] < lengths[:, None]
    key_live = jnp.arange(seq_length, dtype=jnp.int32)[None, :] < lengths[:, None]
    live_rows = query_live.astype(jnp.float32).reshape(row_count, 1)
    weight_query, weight_key, weight_value, weight_out = (
        lax.all_gather(w_query, ("shard", "ctx"), axis=0, tiled=True),
        lax.all_gather(w_key, ("shard", "ctx"), axis=0, tiled=True),
        lax.all_gather(w_value, ("shard", "ctx"), axis=0, tiled=True),
        lax.all_gather(w_out, ("shard", "ctx"), axis=1, tiled=True),
    )
    frames_flat = frames.astype(jnp.float32).reshape(row_count, model_width)
    first, normed_one, inverse_one = norm_rows(frames_flat, ln1_gain, ln1_bias)
    first_low = first.astype(jnp.bfloat16)
    queries = (
        jnp.dot(first_low, weight_query, preferred_element_type=jnp.float32) + b_query
    ).astype(jnp.bfloat16)
    keys_local = jnp.dot(first_low, weight_key, preferred_element_type=jnp.float32).astype(
        jnp.bfloat16
    )
    values_local = (
        jnp.dot(first_low, weight_value, preferred_element_type=jnp.float32) + b_value
    ).astype(jnp.bfloat16)
    keys_all, values_all = (
        lax.all_gather(
            keys_local.reshape(slot_count, seg_rows, head_cols), "ctx", axis=1, tiled=True
        ),
        lax.all_gather(
            values_local.reshape(slot_count, seg_rows, head_cols), "ctx", axis=1, tiled=True
        ),
    )
    query_heads = queries.reshape(slot_count, seg_rows, head_count, HD)
    key_heads = keys_all.reshape(slot_count, seq_length, head_count, HD)
    value_heads = values_all.reshape(slot_count, seq_length, head_count, HD)
    slot = 0
    log_totals, attended_slot = slot_forward(
        query_heads[slot],
        key_heads[slot],
        value_heads[slot],
        query_live[slot],
        key_live[slot],
        key_block,
        score_scale,
    )
    totals_list = [log_totals]
    attended_list = [attended_slot]
    attended = jnp.stack(attended_list).reshape(row_count, head_cols)
    attended_low = attended.astype(jnp.bfloat16)
    attn_sum = lax.psum(
        jnp.dot(attended_low, weight_out, preferred_element_type=jnp.float32).astype(jnp.bfloat16),
        "tp",
    ).astype(jnp.float32)
    hidden = frames_flat + attn_sum + b_out
    weight_up, weight_down = (
        lax.all_gather(w_up, ("shard", "ctx"), axis=0, tiled=True),
        lax.all_gather(w_down, ("shard", "ctx"), axis=1, tiled=True),
    )
    second, normed_two, inverse_two = norm_rows(hidden, ln2_gain, ln2_bias)
    second_low = second.astype(jnp.bfloat16)
    upper = jnp.dot(second_low, weight_up, preferred_element_type=jnp.float32) + b_up
    activated = jax.nn.gelu(upper, approximate=False).astype(jnp.bfloat16)
    mlp_sum = lax.psum(
        jnp.dot(activated, weight_down, preferred_element_type=jnp.float32).astype(jnp.bfloat16),
        "tp",
    ).astype(jnp.float32)
    output = (
        (live_rows * (hidden + mlp_sum + b_down))
        .astype(jnp.bfloat16)
        .reshape(slot_count, seg_rows, model_width)
    )
    grad_out = live_rows * cotangent.astype(jnp.float32).reshape(row_count, model_width)
    grad_out_low = grad_out.astype(jnp.bfloat16)
    grad_b_down = jnp.sum(grad_out, axis=0)
    grad_w_down = jnp.einsum(
        "rf,rd->fd", activated, grad_out_low, preferred_element_type=jnp.float32
    )
    grad_act = jnp.einsum(
        "rd,fd->rf", grad_out_low, weight_down, preferred_element_type=jnp.float32
    )
    grad_upper = (grad_act * gelu_slope(upper)).astype(jnp.bfloat16)
    grad_b_up = jnp.sum(grad_upper.astype(jnp.float32), axis=0)
    grad_w_up = jnp.einsum("rd,rf->df", second_low, grad_upper, preferred_element_type=jnp.float32)
    grad_second = lax.psum(
        jnp.einsum("rf,df->rd", grad_upper, weight_up, preferred_element_type=jnp.float32).astype(
            jnp.bfloat16
        ),
        "tp",
    ).astype(jnp.float32)
    grad_norm_two, grad_ln2_gain, grad_ln2_bias = norm_back(
        grad_second, normed_two, inverse_two, ln2_gain
    )
    grad_hidden = grad_out + grad_norm_two
    grad_hidden_low = grad_hidden.astype(jnp.bfloat16)
    grad_b_out = jnp.sum(grad_hidden_low.astype(jnp.float32), axis=0)
    grad_w_out = jnp.einsum(
        "rc,rd->cd", attended_low, grad_hidden_low, preferred_element_type=jnp.float32
    )
    grad_att = jnp.einsum(
        "rd,cd->rc", grad_hidden_low, weight_out, preferred_element_type=jnp.float32
    ).astype(jnp.bfloat16)
    delta = jnp.sum(
        (grad_att.astype(jnp.float32) * attended).reshape(row_count, head_count, HD), axis=-1
    )
    delta_heads = delta.reshape(slot_count, seg_rows, head_count)
    grad_att_heads = grad_att.reshape(slot_count, seg_rows, head_count, HD)
    slot = 0
    grad_query_slot, key_part, value_part = slot_back(
        query_heads[slot],
        grad_att_heads[slot],
        totals_list[slot],
        delta_heads[slot].T,
        key_heads[slot],
        value_heads[slot],
        query_live[slot],
        key_live[slot],
        key_block,
        score_scale,
    )
    grad_query_list = [grad_query_slot]
    key_part_list = [key_part.reshape(seq_length, head_cols)]
    value_part_list = [value_part.reshape(seq_length, head_cols)]
    grad_keys, grad_values = (
        lax.psum_scatter(
            jnp.stack(key_part_list).astype(jnp.bfloat16), "ctx", scatter_dimension=1, tiled=True
        ).astype(jnp.float32),
        lax.psum_scatter(
            jnp.stack(value_part_list).astype(jnp.bfloat16), "ctx", scatter_dimension=1, tiled=True
        ).astype(jnp.float32),
    )
    grad_query_low = jnp.stack(grad_query_list).reshape(row_count, head_cols).astype(jnp.bfloat16)
    grad_key_low = grad_keys.reshape(row_count, head_cols).astype(jnp.bfloat16)
    grad_value_low = grad_values.reshape(row_count, head_cols).astype(jnp.bfloat16)
    grad_b_query = jnp.sum(grad_query_low.astype(jnp.float32), axis=0)
    grad_b_value = jnp.sum(grad_value_low.astype(jnp.float32), axis=0)
    grad_w_query = jnp.einsum(
        "rd,rc->dc", first_low, grad_query_low, preferred_element_type=jnp.float32
    )
    grad_w_key = jnp.einsum(
        "rd,rc->dc", first_low, grad_key_low, preferred_element_type=jnp.float32
    )
    grad_w_value = jnp.einsum(
        "rd,rc->dc", first_low, grad_value_low, preferred_element_type=jnp.float32
    )
    first_terms = jnp.einsum(
        "rc,dc->rd", grad_query_low, weight_query, preferred_element_type=jnp.float32
    )
    first_terms = first_terms + jnp.einsum(
        "rc,dc->rd", grad_key_low, weight_key, preferred_element_type=jnp.float32
    )
    first_terms = first_terms + jnp.einsum(
        "rc,dc->rd", grad_value_low, weight_value, preferred_element_type=jnp.float32
    )
    grad_first = lax.psum(first_terms.astype(jnp.bfloat16), "tp").astype(jnp.float32)
    grad_norm_one, grad_ln1_gain, grad_ln1_bias = norm_back(
        grad_first, normed_one, inverse_one, ln1_gain
    )
    grad_input = (grad_hidden + grad_norm_one).reshape(slot_count, seg_rows, model_width)
    shard_grads = (
        lax.psum_scatter(grad_w_query, ("shard", "ctx"), scatter_dimension=0, tiled=True),
        lax.psum_scatter(grad_w_key, ("shard", "ctx"), scatter_dimension=0, tiled=True),
        lax.psum_scatter(grad_w_value, ("shard", "ctx"), scatter_dimension=0, tiled=True),
        lax.psum_scatter(grad_w_out, ("shard", "ctx"), scatter_dimension=1, tiled=True),
        lax.psum_scatter(grad_w_up, ("shard", "ctx"), scatter_dimension=0, tiled=True),
        lax.psum_scatter(grad_w_down, ("shard", "ctx"), scatter_dimension=1, tiled=True),
    )
    small_sums = lax.psum(
        (
            grad_ln1_gain,
            grad_ln1_bias,
            grad_b_query,
            grad_b_value,
            grad_b_out,
            grad_ln2_gain,
            grad_ln2_bias,
            grad_b_up,
            grad_b_down,
        ),
        ("shard", "ctx"),
    )
    return (
        output,
        grad_input,
        small_sums[0],
        small_sums[1],
        shard_grads[0],
        small_sums[2],
        shard_grads[1],
        shard_grads[2],
        small_sums[3],
        shard_grads[3],
        small_sums[4],
        small_sums[5],
        small_sums[6],
        shard_grads[4],
        small_sums[7],
        shard_grads[5],
        small_sums[8],
    )


def solution(mesh):
    in_specs = (
        P("shard", "ctx", None),
        P("shard"),
        P("shard", "ctx", None),
        P(),
        P(),
        P(("shard", "ctx"), "tp"),
        P("tp"),
        P(("shard", "ctx"), "tp"),
        P(("shard", "ctx"), "tp"),
        P("tp"),
        P("tp", ("shard", "ctx")),
        P(),
        P(),
        P(),
        P(("shard", "ctx"), "tp"),
        P("tp"),
        P("tp", ("shard", "ctx")),
        P(),
    )
    out_specs = (
        P("shard", "ctx", None),
        P("shard", "ctx", None),
        P(),
        P(),
        P(("shard", "ctx"), "tp"),
        P("tp"),
        P(("shard", "ctx"), "tp"),
        P(("shard", "ctx"), "tp"),
        P("tp"),
        P("tp", ("shard", "ctx")),
        P(),
        P(),
        P(),
        P(("shard", "ctx"), "tp"),
        P("tp"),
        P("tp", ("shard", "ctx")),
        P(),
    )
    return jax.shard_map(
        per_device, mesh=mesh, in_specs=in_specs, out_specs=out_specs, check_vma=False
    )
```

profile of v0, /device:TPU:17, one launch (start us, length us, event | category | flops | bytes accessed | tf_op | source)
XLA Modules:
  0.0 1362.5 jit_solution(5138225697504081990)
XLA Ops:
  11.0 34.0 %all_gather.26 = bf16[768,384]{1,0:T(8,128)(2,1)S(1)} all-gather(bf16[48,384]{1,0:T(8,128)(2,1)S(1)} %copy-done.28), channel_id=1, replica_groups=mesh['shard'=4,'ctx'=4,'tp'=2] {'shard','ctx'}, dimensions={0}, use_global_device_ids=true | all-gather | bytes 626688 | tf_op jit(solution)/shard_map/all_gather | solution.py:204
  47.4 42.9 %all_gather.24 = bf16[768,384]{1,0:T(8,128)(2,1)S(1)} all-gather(bf16[48,384]{1,0:T(8,128)(2,1)S(1)} %copy-done.29), channel_id=1, replica_groups=mesh['shard'=4,'ctx'=4,'tp'=2] {'shard','ctx'}, dimensions={0}, use_global_device_ids=true | all-gather | bytes 626688 | tf_op jit(solution)/shard_map/all_gather | solution.py:205
  93.2 40.1 %all_gather.28 = bf16[768,384]{1,0:T(8,128)(2,1)S(1)} all-gather(bf16[48,384]{1,0:T(8,128)(2,1)S(1)} %copy-done.30), channel_id=1, replica_groups=mesh['shard'=4,'ctx'=4,'tp'=2] {'shard','ctx'}, dimensions={0}, use_global_device_ids=true | all-gather | bytes 626688 | tf_op jit(solution)/shard_map/all_gather | solution.py:203
  135.8 39.9 %all_gather.29 = bf16[384,768]{0,1:T(8,128)(2,1)} all-gather(bf16[384,48]{0,1:T(8,128)(2,1)S(1)} %copy-done.31), channel_id=1, replica_groups=mesh['shard'=4,'ctx'=4,'tp'=2] {'shard','ctx'}, dimensions={1}, use_global_device_ids=true | all-gather | bytes 626688 | tf_op jit(solution)/shard_map/all_gather | solution.py:206
  187.3 11.9 while.39
  199.8 33.8 %while.40 = (s32[]{:T(128)}, f32[512,6,64]{0,2,1:T(8,128)}, bf16[4,512,6,64]{1,3,2,0:T(8,128)(2,1)}, pred[4,512]{1,0:T(4,128)(4,1)S(1)}, bf16[4,512,6,64]{1,0,3,...) while((s32[]{:T(128)}, f32[512,6,64]{0,2,1:T(8,128)}, ...), condition=%wide.region_7.8_spmd.clone, body=%wide.region_6.7_spmd.clone.sunk | while | flops 409601024 | bytes 4737683 | solution.py:99
  203.5 4.5 fusion.195
  211.8 4.7 fusion.195
  220.3 4.7 fusion.195
  228.8 4.7 fusion.195
  239.5 46.6 %all-reduce.6.cloned.1.call-done = bf16[512,768]{1,0:T(8,128)(2,1)} async-done(((bf16[512,768]{1,0:T(8,128)(2,1)}), bf16[512,768]{1,0:T(8,128)(2,1)}) %all-reduce.6.cloned.1.call-update) | async-done | bytes 786448 | tf_op jit(solution)/shard_map/psum | solution.py:245
  289.3 41.3 %all-gather.7.cloned.1.call-done = bf16[768,1536]{1,0:T(8,128)(2,1)} async-done(((bf16[48,1536]{1,0:T(8,128)(2,1)}), bf16[768,1536]{1,0:T(8,128)(2,1)}) %all-gather.7.cloned.1.call-update) | async-done | bytes 2359312 | tf_op jit(solution)/shard_map/all_gather | solution.py:251
  330.5 11.2 fusion.63
  341.7 52.6 %all-gather.9.cloned.1.call-done = bf16[1536,768]{0,1:T(8,128)(2,1)} async-done(((bf16[1536,48]{0,1:T(8,128)(2,1)}), bf16[1536,768]{0,1:T(8,128)(2,1)}) %all-gather.9.cloned.1.call-update) | async-done | bytes 2359312 | tf_op jit(solution)/shard_map/all_gather | solution.py:252
  394.4 5.7 convert_reduce_fusion
  403.9 19.8 %all-reduce.8.cloned.1.call-done = bf16[512,768]{1,0:T(8,128)(2,1)} async-done(((bf16[512,768]{1,0:T(8,128)(2,1)}), bf16[512,768]{1,0:T(8,128)(2,1)}) %all-reduce.8.cloned.1.call-update) | async-done | bytes 786448 | tf_op jit(solution)/shard_map/psum | solution.py:279
  432.6 44.0 %while.41 = (s32[]{:T(128)}, f32[512,6,64]{0,2,1:T(8,128)S(1)}, bf16[4,512,6,64]{1,3,2,0:T(8,128)(2,1)}, bf16[4,512,6,64]{1,3,2,0:T(8,128)(2,1)}, bf16[4,512,6,6...) while((s32[]{:T(128)}, f32[512,6,64]{0,2,1:T(8,128)S(1)}, ...), condition=%wide.region_17.18_spmd.clone, body=%wide.region_16.17_spmd.clone.sunk | while | flops 1023411200 | bytes 61877120 | solution.py:158
  458.3 3.6 fusion.207
  469.3 3.6 fusion.207
  488.1 4.2 convolution_convert_fusion.1
  494.0 22.6 %reduce-scatter.9.cloned.1.call-done = bf16[1,512,384]{1,2,0:T(8,128)(2,1)} async-done(((bf16[1,2048,384]{1,2,0:T(8,128)(2,1)}), bf16[1,512,384]{1,2,0:T(8,128)(2,1)}) %reduce-scatter.9.cloned.1.call-update) | async-done | bytes 393232 | tf_op jit(solution)/shard_map/reduce_scatter | solution.py:319
  519.5 33.5 %reduce-scatter.11.cloned.1.call-done = bf16[1,512,384]{1,2,0:T(8,128)(2,1)} async-done(((bf16[1,2048,384]{1,2,0:T(8,128)(2,1)}), bf16[1,512,384]{1,2,0:T(8,128)(2,1)}) %reduce-scatter.11.cloned.1.call-update) | async-done | bytes 393232 | tf_op jit(solution)/shard_map/reduce_scatter | solution.py:322
  567.2 5.2 fusion.128
  572.4 5.4 fusion.121
  582.0 58.6 %all-reduce = (f32[768]{0:T(1024)}, f32[768]{0:T(1024)}, f32[384]{0:T(512)}, f32[384]{0:T(512)}, f32[768]{0:T(1024)}, /*index=5*/f32[768]{0:T(1024)}, f32[768]{0:T(1024)}, f32[1536]{0:T(1024)}, f32[768]{0:T(1024)}) all-reduce(f32[768]{0:T(1024)S(1)} %get-tuple-element.321, ...), channel_id=1, replica_groups=mesh['shard'=4,'ctx'=4,'tp'=2] {'shard','ctx'}, use_global_device_ids=true, to_apply=%region_24.25 | all-reduce | flops 6912 | bytes 55296 | tf_op jit(solution)/shard_map/psum | solution.py:362
  640.6 3.7 fusion.93
  644.3 39.5 %reduce-scatter.19.cloned.1.call-done = f32[384,48]{0,1:T(8,128)} async-done(((f32[384,768]{0,1:T(8,128)}), f32[384,48]{0,1:T(8,128)}) %reduce-scatter.19.cloned.1.call-update) | async-done | bytes 73744 | tf_op jit(solution)/shard_map/reduce_scatter | solution.py:358
  683.8 128.9 %reduce-scatter.13.cloned.1.call-done = f32[48,384]{1,0:T(8,128)} async-done(((f32[768,384]{1,0:T(8,128)}), f32[48,384]{1,0:T(8,128)}) %reduce-scatter.13.cloned.1.call-update) | async-done | bytes 73744 | tf_op jit(solution)/shard_map/reduce_scatter | solution.py:355
  812.7 128.9 %reduce-scatter.17.cloned.1.call-done = f32[48,384]{1,0:T(8,128)} async-done(((f32[768,384]{1,0:T(8,128)}), f32[48,384]{1,0:T(8,128)}) %reduce-scatter.17.cloned.1.call-update) | async-done | bytes 73744 | tf_op jit(solution)/shard_map/reduce_scatter | solution.py:357
  941.6 128.9 %reduce-scatter.15.cloned.1.call-done = f32[48,384]{1,0:T(8,128)} async-done(((f32[768,384]{1,0:T(8,128)}), f32[48,384]{1,0:T(8,128)}) %reduce-scatter.15.cloned.1.call-update) | async-done | bytes 73744 | tf_op jit(solution)/shard_map/reduce_scatter | solution.py:356
  1070.5 142.5 %reduce-scatter.21.cloned.1.call-done = f32[48,1536]{1,0:T(8,128)} async-done(((f32[768,1536]{1,0:T(8,128)}), f32[48,1536]{1,0:T(8,128)}) %reduce-scatter.21.cloned.1.call-update) | async-done | bytes 294928 | tf_op jit(solution)/shard_map/reduce_scatter | solution.py:359
  1213.0 141.8 %reduce-scatter.23.cloned.1.call-done = f32[1536,48]{0,1:T(8,128)} async-done(((f32[1536,768]{0,1:T(8,128)}), f32[1536,48]{0,1:T(8,128)}) %reduce-scatter.23.cloned.1.call-update) | async-done | bytes 294928 | tf_op jit(solution)/shard_map/reduce_scatter | solution.py:360
  (289 shorter events, 141.5 us)
Async XLA Ops:
  8.0 37.8 %copy-start = (bf16[1,512,768]{2,1,0:T(8,128)(2,1)S(1)}, bf16[1,512,768]{2,1,0:T(8,128)(2,1)}, u32[]{:S(2)}) copy-start(bf16[1,512,768]{2,1,0:T(8,128)(2,1)} %param.24) | copy-start | bytes 2359300
  8.0 37.8 %copy-start.37 = (f32[768]{0:T(1024)S(1)}, f32[768]{0:T(1024)}, u32[]{:S(2)}) copy-start(f32[768]{0:T(1024)} %param.27) | copy-start | bytes 9220
  8.1 37.8 %copy-start.45 = (f32[768]{0:T(1024)S(1)}, f32[768]{0:T(1024)}, u32[]{:S(2)}) copy-start(f32[768]{0:T(1024)} %param.28) | copy-start | bytes 9220
  8.1 167.6 %all-gather.13.cloned.1.call-start = ((), (), s32[]{:S(2)}) async-start(), calls=%async_computation.21 | async-start | bytes 1966080 | tf_op jit(solution)/shard_map/all_gather | solution.py:221
  11.0 122.3 %copy-start.34 = (f32[512]{0:T(512)}, f32[512]{0:T(512)S(1)}, u32[]{:S(2)}) copy-start(f32[512]{0:T(512)S(1)} %add_rsqrt_fusion.1) | copy-start | bytes 6148
  45.8 45.2 %copy-start.47 = (f32[384]{0:T(512)S(1)}, f32[384]{0:T(512)}, u32[]{:S(2)}) copy-start(f32[384]{0:T(512)} %param.33) | copy-start | bytes 4612
  47.3 132.5 %all-gather.11.cloned.1.call-start = ((), (), s32[]{:S(2)}) async-start(), calls=%async_computation.20 | async-start | bytes 1966080 | tf_op jit(solution)/shard_map/all_gather | solution.py:224
  91.0 42.3 %copy-start.48 = (f32[384]{0:T(512)S(1)}, f32[384]{0:T(512)}, u32[]{:S(2)}) copy-start(f32[384]{0:T(512)} %param.30) | copy-start | bytes 4612
  92.5 193.6 %all-reduce.6.cloned.1.call-start = ((), (), s32[]{:S(2)}) async-start(), calls=%async_computation.8 | async-start | bytes 1572864 | tf_op jit(solution)/shard_map/psum | solution.py:245
  235.5 50.6 %copy-start.27 = (f32[768]{0:T(1024)S(1)}, f32[768]{0:T(1024)}, u32[]{:S(2)}) copy-start(f32[768]{0:T(1024)} %param.35) | copy-start | bytes 9220
  238.1 92.4 %all-gather.7.cloned.1.call-start = ((), (), s32[]{:S(2)}) async-start(), calls=%async_computation.9 | async-start | bytes 2506752 | tf_op jit(solution)/shard_map/all_gather | solution.py:251
  238.7 155.7 %all-gather.9.cloned.1.call-start = ((), (), s32[]{:S(2)}) async-start(), calls=%async_computation.10 | async-start | bytes 2506752 | tf_op jit(solution)/shard_map/all_gather | solution.py:252
  239.3 184.4 %all-reduce.8.cloned.1.call-start = ((), (), s32[]{:S(2)}) async-start(), calls=%async_computation.11 | async-start | bytes 1572864 | tf_op jit(solution)/shard_map/psum | solution.py:279
  394.4 7.0 copy-start.44
  403.7 112.9 %reduce-scatter.9.cloned.1.call-start = ((), (), s32[]{:S(2)}) async-start(), calls=%async_computation.12 | async-start | bytes 1966080 | tf_op jit(solution)/shard_map/reduce_scatter | solution.py:319
  436.3 3.6 copy-start.20
  447.3 3.6 copy-start.20
  458.3 3.6 copy-start.20
  469.3 3.6 copy-start.20
  481.6 71.4 %reduce-scatter.11.cloned.1.call-start = ((), (), s32[]{:S(2)}) async-start(), calls=%async_computation.13 | async-start | bytes 1966080 | tf_op jit(solution)/shard_map/reduce_scatter | solution.py:322
  486.7 93.2 %all-reduce.10.cloned.1.call-start = ((), (), s32[]{:S(2)}) async-start(), calls=%async_computation.22 | async-start | bytes 3145728 | tf_op jit(solution)/shard_map/psum | solution.py:258
  493.0 26.5 %copy-start.24 = (bf16[512,6,64]{0,2,1:T(8,128)(2,1)}, bf16[512,6,64]{0,2,1:T(8,128)(2,1)S(1)}, u32[]{:S(2)}) copy-start(bf16[512,6,64]{0,2,1:T(8,128)(2,1)S(1)} %get-tuple-element.397) | copy-start | bytes 1179652
  494.0 59.0 %copy-start.14 = (bf16[768,384]{1,0:T(8,128)(2,1)S(1)}, bf16[768,384]{1,0:T(8,128)(2,1)}, u32[]{:S(2)}) copy-start(bf16[768,384]{1,0:T(8,128)(2,1)} %copy-done.13) | copy-start | bytes 1769476
  553.0 3.2 copy-start.9
  556.2 127.6 %reduce-scatter.19.cloned.1.call-start = ((), (), s32[]{:S(2)}) async-start(), calls=%async_computation.17 | async-start | bytes 1253376 | tf_op jit(solution)/shard_map/reduce_scatter | solution.py:358
  559.2 253.5 %reduce-scatter.13.cloned.1.call-start = ((), (), s32[]{:S(2)}) async-start(), calls=%async_computation.14 | async-start | bytes 1253376 | tf_op jit(solution)/shard_map/reduce_scatter | solution.py:355
  561.9 379.7 %reduce-scatter.17.cloned.1.call-start = ((), (), s32[]{:S(2)}) async-start(), calls=%async_computation.16 | async-start | bytes 1253376 | tf_op jit(solution)/shard_map/reduce_scatter | solution.py:357
  564.0 3.2 copy-start.6
  564.0 3.2 copy-start.33
  564.0 506.5 %reduce-scatter.15.cloned.1.call-start = ((), (), s32[]{:S(2)}) async-start(), calls=%async_computation.15 | async-start | bytes 1253376 | tf_op jit(solution)/shard_map/reduce_scatter | solution.py:356
  567.1 645.9 %reduce-scatter.21.cloned.1.call-start = ((), (), s32[]{:S(2)}) async-start(), calls=%async_computation.18 | async-start | bytes 5013504 | tf_op jit(solution)/shard_map/reduce_scatter | solution.py:359
  572.4 782.4 %reduce-scatter.23.cloned.1.call-start = ((), (), s32[]{:S(2)}) async-start(), calls=%async_computation.19 | async-start | bytes 5013504 | tf_op jit(solution)/shard_map/reduce_scatter | solution.py:360
  (54 other events, 94.9 us)
Sparse Core Ops, SparseCore 0:
  47.4 50.1 all-gather.12
  99.8 51.2 all-gather.10
  238.2 47.7 all-reduce.5
  403.8 19.8 all-reduce.7
  481.7 34.7 reduce-scatter.8
  518.7 34.2 reduce-scatter.10
  556.3 21.1 all-reduce.9
Sparse Core Ops, SparseCore 1:
  241.7 88.7 all-gather.6
  333.5 60.8 all-gather.8
  562.7 121.1 reduce-scatter.18
  689.8 122.8 reduce-scatter.12
  818.7 122.8 reduce-scatter.16
  947.6 122.8 reduce-scatter.14
  1076.9 136.0 reduce-scatter.20
  1218.6 136.1 reduce-scatter.22
where the time goes:
time: 1370 us; the launch traced here: 1360 us
  waiting for transfers between devices  928 us (68%)
  blocking collectives  215 us (16%)
  matrix products  113 us (8%)
  local copies, waits for them, and re-layouts  50 us (4%)
  other arithmetic  37 us (3%)
  between operations  17.1 us (1%)
    reduce_scatter x1, waiting for transfers between devices, per_device(): lax.psum_scatter(grad_w_up, ('shard', 'ctx'), scatter_dimension=0, tiled=...  142 us
    reduce_scatter x1, waiting for transfers between devices, per_device(): lax.psum_scatter(grad_w_down, ('shard', 'ctx'), scatter_dimension=1, tile...  142 us
    reduce_scatter x1, waiting for transfers between devices, per_device(): lax.psum_scatter(grad_w_value, ('shard', 'ctx'), scatter_dimension=0, til...  129 us
    reduce_scatter x1, waiting for transfers between devices, per_device(): lax.psum_scatter(grad_w_key, ('shard', 'ctx'), scatter_dimension=0, tiled...  129 us
    reduce_scatter x1, waiting for transfers between devices, per_device(): lax.psum_scatter(grad_w_query, ('shard', 'ctx'), scatter_dimension=0, til...  129 us
    psum x1, blocking collectives, per_device(): lax.psum((grad_ln1_gain, grad_ln1_bias, grad_b_query, grad_b_value, grad_...  58.6 us
    all_gather x1, waiting for transfers between devices, per_device(): lax.all_gather(w_down, ('shard', 'ctx'), axis=1, tiled=True)  52.6 us
    psum x1, waiting for transfers between devices, per_device(): lax.psum(jnp.dot(attended_low, weight_out, preferred_element_type=jnp.flo...  46.6 us
  transfers between devices with their start and end apart: 15, of which 12 were waited for; matrix products, arithmetic and copies ran while one was open for 5% of the time, Pallas kernels for 0%

commit v1 on v0

--- a/solution.py
+++ b/solution.py
@@ -1,8 +1,11 @@
+import functools
 import math
 
 import jax
 import jax.numpy as jnp
 from jax import lax
+from jax.experimental import pallas as pl
+from jax.experimental.pallas import tpu as pltpu
 from jax.sharding import PartitionSpec as P
 
 HD = 64
@@ -167,7 +170,7 @@
     return whole_slot(0)
 
 
-def per_device(
+def plain_layer(
     frames,
     lengths,
     cotangent,
@@ -394,6 +397,973 @@
     )
 
 
+MESH = pl.DeviceIdType.MESH
+F32 = jnp.float32
+BF16 = jnp.bfloat16
+NEG = -1e30
+LIVE_LANE = 192
+
+
+def nn(left, right):
+    return jnp.dot(left, right, preferred_element_type=F32)
+
+
+def nt(left, right):
+    return lax.dot_general(left, right, (((1,), (1,)), ((), ())), preferred_element_type=F32)
+
+
+def flip(values):
+    return values.astype(F32).T.astype(BF16)
+
+
+def layer_kernel(
+    dims,
+    frames,
+    cot,
+    lengths,
+    vecs,
+    b_up,
+    wqkv_own,
+    bias_own,
+    wf_own,
+    out_o,
+    gin_o,
+    gf_o,
+    go_o,
+    gq_o,
+    sums_o,
+    ss,
+    rs,
+    ls,
+    a_all,
+    a_t,
+    wqkv,
+    bias_all,
+    wf,
+    wo_sib,
+    k_tr,
+    v_tr,
+    k_n,
+    v_n,
+    q_n,
+    q_t,
+    lse,
+    att_f,
+    att_s,
+    att_r,
+    hid,
+    z_all,
+    z_t,
+    g_n,
+    g_t,
+    act,
+    gup,
+    part_s,
+    part_r,
+    gz_s,
+    gz_r,
+    ghl_t,
+    gatt_r,
+    gatt_t,
+    wg,
+    wg_r,
+    wg_zr,
+    og_x,
+    og_r,
+    og_z,
+    og_zr,
+    dk_t,
+    dv_t,
+    dq_f,
+    dkv_s,
+    dkv_r,
+    g_nat,
+    ga_s,
+    ga_r,
+    qg,
+    qg_r,
+    qg_p,
+    qg_z,
+    qg_zr,
+    sums,
+    sum_p,
+    sum_z,
+    sum_c,
+):
+    S, C, R, D, GP, HG, FH = dims
+    HF = R // 2
+    CH = C // 2
+    DB = D // (S * C)
+    PB = C * DB
+    s, z, c = lax.axis_index("shard"), lax.axis_index("ctx"), lax.axis_index("tp")
+    o = 1 - c
+    sib = (s, z, o)
+    owed = []
+    next_sem = [0]
+
+    def sems(count):
+        base = next_sem[0]
+        next_sem[0] = base + count
+        return base
+
+    def remote(src, dst, index, device):
+        return pltpu.make_async_remote_copy(
+            src_ref=src,
+            dst_ref=dst,
+            send_sem=ss.at[index],
+            recv_sem=rs.at[index],
+            device_id=device,
+            device_id_type=MESH,
+        )
+
+    def send(src, dst, index, device, when=None):
+        def go():
+            remote(src, dst, index, device).start()
+
+        if when is None:
+            go()
+        else:
+            pl.when(when)(go)
+        owed.append((src, dst, index, device, when))
+
+    def arrive(dst, index, when=None):
+        def go():
+            remote(dst, dst, index, sib).wait_recv()
+
+        if when is None:
+            go()
+        else:
+            pl.when(when)(go)
+
+    def plane(k):
+        return (lax.rem(s + k, S), z, c)
+
+    def column(k):
+        return (s, lax.rem(z + k, C), c)
+
+    def s_from(k):
+        return lax.rem(s + S - k, S)
+
+    def z_from(k):
+        return lax.rem(z + C - k, C)
+
+    def rows_of(block):
+        return pl.ds(pl.multiple_of(block * DB, 16), DB)
+
+    def half_rows(block, half):
+        return pl.ds(pl.multiple_of(block * R + half * HF, HF), HF)
+
+    def blk(block):
+        return pl.ds(pl.multiple_of(block * HF, HF), HF)
+
+    k_bias = sems(1)
+    k_q1 = sems(CH)
+    k_q2 = sems(S)
+    k_q3 = sems(1)
+    k_a = sems(2 * C)
+    k_as = sems(2 * C)
+    k_f = sems(2 * C)
+    k_fp0 = sems(S)
+    k_fp = sems(2 * C * S)
+    k_wo = sems(1)
+    k_att = sems(C)
+    k_n2 = sems(1)
+    k_part = sems(1)
+    k_gz = sems(1)
+    k_out = sems(1)
+    k_gatt = sems(C)
+    k_wg = sems(S)
+    k_wgz = sems(C)
+    k_ox = sems(1)
+    k_og = sems(S)
+    k_ogz = sems(C)
+    k_dkv = sems(1)
+    k_ga = sems(C)
+    k_qx = sems(1)
+    k_qp = sems(S)
+    k_qz = sems(CH)
+    k_gin = sems(1)
+    k_sp = sems(S)
+    k_sz = sems(C)
+    k_sc = sems(1)
+
+    barrier = pltpu.get_barrier_semaphore()
+    friends = [sib]
+    friends += [plane(k) for k in range(1, S)]
+    for k in range(1, C):
+        friends += [(s, lax.rem(z + k, C), c), (s, lax.rem(z + k, C), o)]
+    for friend in friends:
+        pl.semaphore_signal(barrier, inc=1, device_id=friend, device_id_type=MESH)
+
+    length = lengths[0]
+    lane = lax.broadcasted_iota(jnp.int32, (HF, GP), 1)
+
+    def head_lanes(count, h):
+        at = lax.broadcasted_iota(jnp.int32, (count, GP), 1)
+        return jnp.logical_and(at >= HD * h, at < HD * (h + 1))
+
+    def only_head(values, h, keep_live=False):
+        picked = head_lanes(values.shape[0], h)
+        if keep_live:
+            at = lax.broadcasted_iota(jnp.int32, values.shape, 1)
+            picked = jnp.logical_or(picked, at == LIVE_LANE)
+        return jnp.where(picked, values, jnp.zeros_like(values))
+
+    ln1_gain, ln1_bias, b_out, ln2_gain, ln2_bias, b_down = (
+        vecs[i : i + 1, :] for i in range(6)
+    )
+
+    def norm(values):
+        centred = values - jnp.mean(values, axis=-1, keepdims=True)
+        inverse = lax.rsqrt(jnp.mean(centred * centred, axis=-1, keepdims=True) + EPSILON)
+        return centred * inverse, inverse
+
+    def live_of(first, count):
+        at = z * R + first + lax.broadcasted_iota(jnp.int32, (count, 1), 0)
+        return (at < length).astype(F32)
+
+    def first_norm(i, carry):
+        at = pl.ds(pl.multiple_of(i * 64, 64), 64)
+        to = pl.ds(pl.multiple_of(z * R + i * 64, 64), 64)
+        normed, unused = norm(frames[at, :].astype(F32))
+        a_all[to, :] = (normed * ln1_gain + ln1_bias).astype(BF16)
+        g_n[at, :] = (cot[at, :].astype(F32) * live_of(i * 64, 64)).astype(BF16)
+        return carry
+
+    lax.fori_loop(0, R // 64, first_norm, 0)
+    sums[...] = jnp.zeros_like(sums)
+    pl.semaphore_wait(barrier, len(friends))
+
+    c_of_z = z // CH
+    for j in range(CH):
+        to_z = CH * c + j
+        same = jnp.logical_and(to_z == z, c_of_z == c)
+        for i in range(CH):
+            ok = jnp.logical_and(z - CH * c_of_z == i, jnp.logical_not(same))
+            here = wqkv.at[s, c_of_z, pl.ds(i * DB, DB), :]
+
+            def go(i=i, here=here, j=j, to_z=to_z):
+                pltpu.make_async_remote_copy(
+                    src_ref=wqkv_own.at[j],
+                    dst_ref=here,
+                    send_sem=ls.at[j],
+                    recv_sem=rs.at[k_q1 + i],
+                    device_id=(s, to_z, c_of_z),
+                    device_id_type=MESH,
+                ).start()
+
+            pl.when(ok)(go)
+
+        def keep(j=j):
+            wqkv[s, c, pl.ds(pl.multiple_of((z - CH * c) * DB, 16), DB), :] = wqkv_own[j]
+
+        pl.when(same)(keep)
+    send(bias_own, bias_all.at[c], k_bias, sib)
+    bias_all[c] = bias_own[...]
+    mine_rows = rows_of(s * C + z)
+    for k in range(1, S):
+        send(wf_own, wf.at[mine_rows, :], k_fp0 + k, plane(k))
+    can_right, can_left = z + 1 < C, z >= 1
+
+    def a_step(t):
+        send(
+            a_all.at[half_rows(jnp.maximum(z - t, 0), c), :],
+            a_all.at[half_rows(jnp.maximum(z - t, 0), c), :],
+            k_a + 2 * t,
+            (s, jnp.minimum(z + 1, C - 1), c),
+            jnp.logical_and(can_right, z - t >= 0),
+        )
+        send(
+            a_all.at[half_rows(jnp.minimum(z + t, C - 1), c), :],
+            a_all.at[half_rows(jnp.minimum(z + t, C - 1), c), :],
+            k_a + 2 * t + 1,
+            (s, jnp.maximum(z - 1, 0), c),
+            jnp.logical_and(can_left, z + t < C),
+        )
+
+    a_step(0)
+    wf[mine_rows, :] = wf_own[...]
+    key_at = lax.broadcasted_iota(jnp.int32, (GP - LIVE_LANE, C * R), 1)
+    first_row = lax.broadcasted_iota(jnp.int32, (GP - LIVE_LANE, C * R), 0) == 0
+    dead = jnp.where(jnp.logical_and(first_row, key_at >= length), NEG, 0.0)
+    k_tr[LIVE_LANE:, :] = dead.astype(BF16)
+    v_tr[LIVE_LANE:, :] = jnp.zeros((GP - LIVE_LANE, C * R), BF16)
+    for i in range(CH):
+        from_z = CH * c + i
+        same = jnp.logical_and(from_z == z, c_of_z == c)
+        arrive(wqkv.at[s, c, pl.ds(i * DB, DB), :], k_q1 + i, jnp.logical_not(same))
+    for k in range(1, S):
+        send(wqkv.at[s, c], wqkv.at[s, c], k_q2 + k, plane(k))
+    for k in range(1, S):
+        arrive(wqkv.at[s_from(k), c], k_q2 + k)
+    send(wqkv.at[:, c], wqkv.at[:, c], k_q3, sib)
+    arrive(bias_all.at[o], k_bias)
+    arrive(wqkv.at[:, o], k_q3)
+    bias_z = bias_all[c_of_z, z - CH * c_of_z]
+
+    def project(block, half, own):
+        at = half_rows(block, half)
+        rows = a_all[at, :]
+        width = 3 * GP if own else 2 * GP
+        weights = wqkv[:, :, :, :width].reshape(D, width)
+        made = nn(rows, weights) + bias_z[0:1, :width]
+        keys = made[:, :GP].astype(BF16)
+        values = made[:, GP : 2 * GP].astype(BF16)
+        k_n[at, :] = keys
+        v_n[at, :] = values
+        k_tr[:LIVE_LANE, at] = flip(keys)[:LIVE_LANE, :]
+        v_tr[:LIVE_LANE, at] = flip(values)[:LIVE_LANE, :]
+        if own:
+            queries = made[:, 2 * GP :].astype(BF16).astype(F32) * (HD**-0.5)
+            queries = jnp.where(lane == LIVE_LANE, 1.0, queries).astype(BF16)
+            q_n[blk(block), :] = queries
+            q_t[:, blk(block)] = flip(queries)
+            a_t[:, blk(block)] = flip(rows)
+
+    project(z, c, True)
+    project(z, o, False)
+    g_t[:, :HF] = flip(g_n[:HF, :])
+    g_t[:, HF:] = flip(g_n[HF:, :])
+
+    def f_step(t):
+        send(
+            wf.at[rows_of(s * C + jnp.maximum(z - t, 0)), :],
+            wf.at[rows_of(s * C + jnp.maximum(z - t, 0)), :],
+            k_f + 2 * t,
+            (s, jnp.minimum(z + 1, C - 1), c),
+            jnp.logical_and(can_right, z - t >= 0),
+        )
+        send(
+            wf.at[rows_of(s * C + jnp.minimum(z + t, C - 1)), :],
+            wf.at[rows_of(s * C + jnp.minimum(z + t, C - 1)), :],
+            k_f + 2 * t + 1,
+            (s, jnp.maximum(z - 1, 0), c),
+            jnp.logical_and(can_left, z + t < C),
+        )
+
+    def from_left(t):
+        return jnp.maximum(z - 1 - t, 0), z - 1 - t >= 0
+
+    def from_right(t):
+        return jnp.minimum(z + 1 + t, C - 1), z + 1 + t < C
+
+    def f_arrive(t):
+        for side, (block, ok) in enumerate((from_left(t), from_right(t))):
+            arrive(wf.at[rows_of(s * C + block), :], k_f + 2 * t + side, ok)
+        if t + 1 < C - 1:
+            f_step(t + 1)
+        for side, (block, ok) in enumerate((from_left(t), from_right(t))):
+            for k in range(1, S):
+                send(
+                    wf.at[rows_of(s * C + block), :],
+                    wf.at[rows_of(s * C + block), :],
+                    k_fp + (2 * t + side) * S + k,
+                    plane(k),
+                    ok,
+                )
+
+    for t in range(C - 1):
+        sides = (from_left(t), from_right(t))
+        for side, (block, ok) in enumerate(sides):
+            arrive(a_all.at[half_rows(block, c), :], k_a + 2 * t + side, ok)
+        if t + 1 < C - 1:
+            a_step(t + 1)
+        for side, (block, ok) in enumerate(sides):
+            send(
+                a_all.at[half_rows(block, c), :],
+                a_all.at[half_rows(block, c), :],
+                k_as + 2 * t + side,
+                sib,
+                ok,
+            )
+        if t == C - 3:
+            f_step(0)
+        for side, (block, ok) in enumerate(sides):
+
+            def come(block=block, t=t, side=side):
+                project(block, c, True)
+                remote(
+                    a_all.at[half_rows(block, o), :],
+                    a_all.at[half_rows(block, o), :],
+                    k_as + 2 * t + side,
+                    sib,
+                ).wait_recv()
+                project(block, o, False)
+
+            pl.when(ok)(come)
+
+    TQ = 128
+
+    def attend(block):
+        def step(i, carry):
+            at = pl.ds(pl.multiple_of(block * HF + i * TQ, TQ), TQ)
+            queries = q_n[at, :]
+            total = jnp.zeros((TQ, GP), F32)
+            for h in range(HG):
+                scores = nn(only_head(queries, h, True), k_tr[...])
+                top = jnp.max(scores, axis=-1, keepdims=True)
+                weights = jnp.exp(scores - top)
+                norm_sum = jnp.sum(weights, axis=-1, keepdims=True)
+                got = nn(weights.astype(BF16), v_n[...]) * (1.0 / norm_sum)
+                total = total + only_head(got, h)
+                lse[at, h : h + 1] = top + jnp.log(norm_sum)
+            att_f[at, :] = total
+            att_s[at, :] = total.astype(BF16)
+            return carry
+
+        lax.fori_loop(0, HF // TQ, step, 0)
+
+    for k in range(1, C):
+        block = lax.rem(z + k, C)
+        attend(block)
+        remote(att_s.at[blk(block), :], att_r.at[blk(z), :], k_att + k, column(k)).start()
+        f_arrive(k - 1)
+    attend(z)
+    att_r[blk(z), :] = att_s[blk(z), :]
+
+    for k in range(1, S):
+        arrive(wf.at[rows_of(s_from(k) * C + z), :], k_fp0 + k)
+        for t in range(C - 1):
+            for side, (block, ok) in enumerate((from_left(t), from_right(t))):
+                arrive(
+                    wf.at[rows_of(s_from(k) * C + block), :], k_fp + (2 * t + side) * S + k, ok
+                )
+    wo_cols = slice(2 * FH, 2 * FH + CH * GP)
+    send(wf.at[:, wo_cols], wo_sib, k_wo, sib)
+    for k in range(1, C):
+        arrive(att_r.at[blk(z_from(k)), :], k_att + k)
+        remote(att_s.at[blk(z), :], att_r.at[blk(z), :], k_att + k, column(k)).wait_send()
+    arrive(wo_sib, k_wo)
+
+    own_rows = pl.ds(pl.multiple_of(c * HF, HF), HF)
+    hidden = frames[own_rows, :].astype(F32) + b_out
+    for j in range(CH):
+        hidden = hidden + nt(
+            att_r[blk(CH * c + j), :], wf[:, 2 * FH + j * GP : 2 * FH + (j + 1) * GP]
+        )
+        hidden = hidden + nt(att_r[blk(CH * o + j), :], wo_sib[:, j * GP : (j + 1) * GP])
+    hid[...] = hidden
+    normed, unused = norm(hidden)
+    z_all[own_rows, :] = (normed * ln2_gain + ln2_bias).astype(BF16)
+    send(z_all.at[own_rows, :], z_all.at[own_rows, :], k_n2, sib)
+    other_rows = pl.ds(pl.multiple_of(o * HF, HF), HF)
+    z_t[:, own_rows] = flip(z_all[own_rows, :])
+    arrive(z_all.at[other_rows, :], k_n2)
+    z_t[:, other_rows] = flip(z_all[other_rows, :])
+
+    TF = 256
+
+    def units(i, carry):
+        cols = pl.ds(pl.multiple_of(i * TF, TF), TF)
+        down = pl.ds(pl.multiple_of(FH + i * TF, TF), TF)
+        upper = nn(z_all[...], wf[:, cols]) + b_up[:, cols]
+        cumulative = 0.5 * (1.0 + lax.erf(upper * INV_ROOT_TWO))
+        act[:, cols] = (upper * cumulative).astype(BF16)
+        slope = cumulative + upper * jnp.exp(-0.5 * upper * upper) * INV_ROOT_TAU
+        grad_units = (nn(g_n[...], wf[:, down]) * slope).astype(BF16)
+        gup[:, cols] = grad_units
+        return carry
+
+    lax.fori_loop(0, FH // TF, units, 0)
+
+    def z_grad(i, carry):
+        at = pl.ds(pl.multiple_of(i * 256, 256), 256)
+        gz_s[:, at] = nt(gup[other_rows, :], wf[at, :FH]).astype(BF16)
+        return carry
+
+    lax.fori_loop(0, D // 256, z_grad, 0)
+    send(gz_s, gz_r, k_gz, sib)
+
+    def down_part(i, carry):
+        at = pl.ds(pl.multiple_of(i * 256, 256), 256)
+        part_s[:, at] = nt(act[other_rows, :], wf[at, FH : 2 * FH]).astype(BF16)
+        return carry
+
+    lax.fori_loop(0, D // 256, down_part, 0)
+    send(part_s, part_r, k_part, sib)
+
+    def unit_grads(k):
+        at = pl.ds(pl.multiple_of(lax.rem(s + k, S) * PB, 64), PB)
+
+        def step(i, carry):
+            cols = pl.ds(pl.multiple_of(i * TF, TF), TF)
+            down = pl.ds(pl.multiple_of(FH + i * TF, TF), TF)
+            wg[at, cols] = nn(z_t[at, :], gup[:, cols]).astype(BF16)
+            wg[at, down] = nn(g_t[at, :], act[:, cols]).astype(BF16)
+            return carry
+
+        lax.fori_loop(0, FH // TF, step, 0)
+
+    for k in range(1, S):
+        unit_grads(k)
+        at = pl.ds(pl.multiple_of(lax.rem(s + k, S) * PB, 64), PB)
+        send(wg.at[at, :], wg_r.at[k - 1], k_wg + k, plane(k))
+
+    gz_rows = jnp.concatenate(
+        [nt(gup[own_rows, :], wf[i * 256 : (i + 1) * 256, :FH]) for i in range(D // 256)], axis=1
+    )
+    down_rows = jnp.concatenate(
+        [nt(act[own_rows, :], wf[i * 256 : (i + 1) * 256, FH : 2 * FH]) for i in range(D // 256)],
+        axis=1,
+    )
+    arrive(gz_r, k_gz)
+    grad_z = gz_rows + gz_r[...].astype(F32)
+    live_own = live_of(c * HF, HF)
+    normed, inverse = norm(hid[...])
+    scaled = grad_z * ln2_gain
+    inner = (
+        scaled
+        - jnp.mean(scaled, axis=-1, keepdims=True)
+        - normed * jnp.mean(scaled * normed, axis=-1, keepdims=True)
+    )
+    g_own = g_n[own_rows, :].astype(F32)
+    grad_hidden = g_own + inner * inverse
+    gin_o[own_rows, :] = grad_hidden
+    low = grad_hidden.astype(BF16)
+    sums[3:4, :] = jnp.sum(grad_z * normed, axis=0, keepdims=True)
+    sums[4:5, :] = jnp.sum(grad_z, axis=0, keepdims=True)
+    sums[5:6, :] = jnp.sum(g_own, axis=0, keepdims=True)
+    sums[2:3, :] = jnp.sum(low.astype(F32), axis=0, keepdims=True)
+    for j in range(CH):
+        att_s[blk(CH * c + j), :] = nn(
+            low, wf[:, 2 * FH + j * GP : 2 * FH + (j + 1) * GP]
+        ).astype(BF16)
+        att_s[blk(CH * o + j), :] = nn(low, wo_sib[:, j * GP : (j + 1) * GP]).astype(BF16)
+    for k in range(1, C):
+        send(att_s.at[blk(lax.rem(z + k, C)), :], gatt_r.at[blk(z), :], k_gatt + k, column(k))
+    gatt_r[blk(z), :] = att_s[blk(z), :]
+    ghl_t[...] = flip(low)
+    for j in range(CH):
+        og_x[0, :, j * GP : (j + 1) * GP] = nn(ghl_t[...], att_r[blk(CH * o + j), :]).astype(BF16)
+    remote(og_x.at[0], og_x.at[1], k_ox, sib).start()
+    arrive(part_r, k_part)
+    out_rows = live_own * (hid[...] + down_rows + part_r[...].astype(F32) + b_down)
+    out_o[own_rows, :] = out_rows.astype(BF16)
+    send(out_o.at[own_rows, :], out_o.at[own_rows, :], k_out, sib)
+    unit_grads(0)
+    for i in range(2):
+        sums[pl.ds(6 + 2 * c + i, 1), :] = jnp.sum(
+            gup[:, i * D : (i + 1) * D].astype(F32), axis=0, keepdims=True
+        )
+    arrive(og_x.at[1], k_ox)
+    remote(og_x.at[0], og_x.at[1], k_ox, sib).wait_send()
+    for j in range(CH):
+        cols = slice(j * GP, (j + 1) * GP)
+        own_part = nn(ghl_t[...], att_r[blk(CH * c + j), :])
+        og_x[0, :, cols] = (own_part + og_x[1, :, cols].astype(F32)).astype(BF16)
+    for k in range(1, S):
+        at = pl.ds(pl.multiple_of(lax.rem(s + k, S) * PB, 64), PB)
+        send(og_x.at[0, at, :], og_r.at[k - 1], k_og + k, plane(k))
+
+    dk_t[...] = jnp.zeros_like(dk_t)
+    dv_t[...] = jnp.zeros_like(dv_t)
+    TK = 512
+
+    def attend_back(block):
+        at = blk(block)
+        gatt_t[...] = flip(gatt_r[at, :])
+        product = gatt_r[at, :].astype(F32) * att_f[at, :]
+        deltas = []
+        for h in range(HG):
+            deltas.append(jnp.sum(only_head(product, h), axis=-1, keepdims=True))
+        dq_f[...] = jnp.zeros_like(dq_f)
+
+        def step(i, carry):
+            keys = pl.ds(pl.multiple_of(i * TK, TK), TK)
+            for h in range(HG):
+                head = slice(HD * h, HD * (h + 1))
+                scores = nn(only_head(q_n[at, :], h, True), k_tr[:, keys])
+                weights = jnp.exp(scores - lse[at, h : h + 1])
+                grads = nn(only_head(gatt_r[at, :], h), v_tr[:, keys])
+                grad_scores = (weights * (grads - deltas[h])).astype(BF16)
+                dv_t[head, keys] += nn(gatt_t[head, :], weights.astype(BF16))
+                dk_t[head, keys] += nn(q_t[head, at], grad_scores)
+                dq_f[...] += only_head(nn(grad_scores, k_n[keys, :]), h)
+            return carry
+
+        lax.fori_loop(0, C * R // TK, step, 0)
+        g_nat[at, 2 * GP :] = (dq_f[...] * (HD**-0.5)).astype(BF16)
+
+    def wg_reduce():
+        for k in range(1, S):
+            arrive(wg_r.at[k - 1], k_wg + k)
+        for j in range(C):
+            part = pl.ds(j * DB, DB)
+            own = pl.ds(pl.multiple_of(s * PB + j * DB, 16), DB)
+
+            def step(i, carry):
+                cols = pl.ds(pl.multiple_of(i * 512, 512), 512)
+                total = wg[own, cols].astype(F32)
+                for k in range(1, S):
+                    total = total + wg_r[k - 1, part, cols].astype(F32)
+                wg[own, cols] = total.astype(BF16)
+                return carry
+
+            lax.fori_loop(0, 2 * FH // 512, step, 0)
+        for k in range(1, C):
+            at = pl.ds(pl.multiple_of(s * PB + lax.rem(z + k, C) * DB, 16), DB)
+            send(wg.at[at, :], wg_zr.at[k - 1], k_wgz + k, column(k))
+
+    def og_reduce():
+        for k in range(1, S):
+            arrive(og_r.at[k - 1], k_og + k)
+        own = pl.ds(pl.multiple_of(s * PB, 64), PB)
+        total = og_x[0, own, :].astype(F32)
+        for k in range(1, S):
+            total = total + og_r[k - 1].astype(F32)
+        og_z[...] = total.astype(BF16)
+        for k in range(1, C):
+            at = pl.ds(pl.multiple_of(lax.rem(z + k, C) * DB, 16), DB)
+            send(og_z.at[at, :], og_zr.at[k - 1], k_ogz + k, column(k))
+
+    attend_back(z)
+    for k in range(1, C):
+        arrive(gatt_r.at[blk(z_from(k)), :], k_gatt + k)
+    attend_back(z_from(1))
+    for k in range(2, C):
+        attend_back(z_from(k))
+
+    for i in range(C):
+        cols = pl.ds(pl.multiple_of(i * R + o * HF, HF), HF)
+        dkv_s[i, 0] = dk_t[:, cols].astype(BF16)
+        dkv_s[i, 1] = dv_t[:, cols].astype(BF16)
+    send(dkv_s, dkv_r, k_dkv, sib)
+    wg_reduce()
+    arrive(dkv_r, k_dkv)
+
+    def finish(block):
+        cols = pl.ds(pl.multiple_of(block * R + c * HF, HF), HF)
+        at = blk(block)
+        keys_t = dk_t[:, cols] + dkv_r[block, 0].astype(F32)
+        values_t = dv_t[:, cols] + dkv_r[block, 1].astype(F32)
+        none = jnp.zeros((GP - LIVE_LANE, HF), F32)
+        g_nat[at, :GP] = jnp.concatenate([keys_t, none], axis=0).T.astype(BF16)
+        g_nat[at, GP : 2 * GP] = jnp.concatenate([values_t, none], axis=0).T.astype(BF16)
+        ga_s[at, :] = nt(g_nat[at, :], wqkv[...].reshape(D, 3 * GP)).astype(BF16)
+
+    for k in range(1, C):
+        block = lax.rem(z + k, C)
+        finish(block)
+        send(ga_s.at[blk(block), :], ga_r.at[k - 1], k_ga + k, column(k))
+    finish(z)
+    og_reduce()
+
+    for i in range(S):
+        got = nn(a_t[i * PB : (i + 1) * PB, :], g_nat[...])
+        qg[i] = got.reshape(2, CH * DB, 3 * GP).astype(BF16)
+    send(qg.at[:, o], qg_r, k_qx, sib)
+    sums[pl.ds(10 + z, 1), :] = jnp.sum(g_nat[...].astype(F32), axis=0, keepdims=True)
+    arrive(qg_r, k_qx)
+    for i in range(S):
+        qg_r[i] = (qg_r[i].astype(F32) + qg[i, c].astype(F32)).astype(BF16)
+    for k in range(1, S):
+        send(qg_r.at[lax.rem(s + k, S)], qg_p.at[k - 1], k_qp + k, plane(k))
+
+    own_block = blk(z)
+    for k in range(1, C):
+        arrive(ga_r.at[k - 1], k_ga + k)
+    grad_a = ga_s[own_block, :].astype(F32)
+    for k in range(1, C):
+        grad_a = grad_a + ga_r[k - 1].astype(F32)
+    normed, inverse = norm(frames[own_rows, :].astype(F32))
+    scaled = grad_a * ln1_gain
+    inner = (
+        scaled
+        - jnp.mean(scaled, axis=-1, keepdims=True)
+        - normed * jnp.mean(scaled * normed, axis=-1, keepdims=True)
+    )
+    sums[0:1, :] = jnp.sum(grad_a * normed, axis=0, keepdims=True)
+    sums[1:2, :] = jnp.sum(grad_a, axis=0, keepdims=True)
+    gin_o[own_rows, :] = gin_o[own_rows, :] + inner * inverse
+    send(gin_o.at[own_rows, :], gin_o.at[own_rows, :], k_gin, sib)
+    sum_p[s] = sums[...]
+    for k in range(1, S):
+        send(sum_p.at[s], sum_p.at[s], k_sp + k, plane(k))
+
+    for k in range(1, S):
+        arrive(qg_p.at[k - 1], k_qp + k)
+    total = qg_r[s].astype(F32)
+    for k in range(1, S):
+        total = total + qg_p[k - 1].astype(F32)
+    qg_z[...] = total.reshape(CH, DB, 3 * GP).astype(BF16)
+    for i in range(CH):
+        to_z = CH * c + i
+        same = jnp.logical_and(to_z == z, c_of_z == c)
+        for j in range(CH):
+            ok = jnp.logical_and(z - CH * c_of_z == j, jnp.logical_not(same))
+
+            def go(i=i, j=j, to_z=to_z):
+                pltpu.make_async_remote_copy(
+                    src_ref=qg_z.at[i],
+                    dst_ref=qg_zr.at[j],
+                    send_sem=ls.at[CH + i],
+                    recv_sem=rs.at[k_qz + j],
+                    device_id=(s, to_z, c_of_z),
+                    device_id_type=MESH,
+                ).start()
+
+            pl.when(ok)(go)
+
+        def keep(i=i):
+            qg_zr[z - CH * c] = qg_z[i]
+
+        pl.when(same)(keep)
+
+    for k in range(1, S):
+        arrive(sum_p.at[s_from(k)], k_sp + k)
+    total = sum_p[0]
+    for k in range(1, S):
+        total = total + sum_p[k]
+    sum_z[z] = total
+    for k in range(1, C):
+        send(sum_z.at[z], sum_z.at[z], k_sz + k, column(k))
+
+    def last(own, got, index, to):
+        for k in range(1, C):
+            arrive(got.at[k - 1], index + k)
+        total = own.astype(F32)
+        for k in range(1, C):
+            total = total + got[k - 1].astype(F32)
+        to[...] = total
+
+    last(wg[rows_of(s * C + z), :], wg_zr, k_wgz, gf_o)
+    last(og_z[pl.ds(pl.multiple_of(z * DB, 16), DB), :], og_zr, k_ogz, go_o)
+    for k in range(1, C):
+        arrive(sum_z.at[z_from(k)], k_sz + k)
+    total = sum_z[0]
+    for k in range(1, C):
+        total = total + sum_z[k]
+    sum_c[c] = total
+    send(sum_c.at[c], sum_c.at[c], k_sc, sib)
+    for j in range(CH):
+        same = jnp.logical_and(CH * c + j == z, c_of_z == c)
+        arrive(qg_zr.at[j], k_qz + j, jnp.logical_not(same))
+    gq_o[...] = qg_zr[...].astype(F32)
+    arrive(sum_c.at[o], k_sc)
+    sums_o[...] = sum_c[0] + sum_c[1]
+    arrive(out_o.at[other_rows, :], k_out)
+    arrive(gin_o.at[other_rows, :], k_gin)
+
+    for src, dst, index, device, when in owed:
+
+        def done(src=src, dst=dst, index=index, device=device):
+            remote(src, dst, index, device).wait_send()
+
+        if when is None:
+            done()
+        else:
+            pl.when(when)(done)
+    for j in range(CH):
+        same = jnp.logical_and(CH * c + j == z, c_of_z == c)
+
+        def done_weights(j=j):
+            pltpu.make_async_remote_copy(
+                src_ref=wqkv_own.at[j],
+                dst_ref=wqkv_own.at[j],
+                send_sem=ls.at[j],
+                recv_sem=rs.at[k_q1],
+                device_id=sib,
+                device_id_type=MESH,
+            ).wait_send()
+            pltpu.make_async_remote_copy(
+                src_ref=qg_z.at[j],
+                dst_ref=qg_z.at[j],
+                send_sem=ls.at[CH + j],
+                recv_sem=rs.at[k_qz],
+                device_id=sib,
+                device_id_type=MESH,
+            ).wait_send()
+
+        pl.when(jnp.logical_not(same))(done_weights)
+    assert next_sem[0] <= SEMS
+
+
+SEMS = 160
+
+
+def fits(frames, w_query, w_up):
+    shards, ctx, cores = (lax.axis_size(name) for name in ("shard", "ctx", "tp"))
+    slot_count, seg_rows, width = frames.shape
+    heads = w_query.shape[1] * cores // HD
+    return (
+        slot_count == 1
+        and cores == 2
+        and ctx % 2 == 0
+        and ctx > 2
+        and shards > 1
+        and heads == 3 * ctx
+        and width % (16 * shards * ctx) == 0
+        and width % 256 == 0
+        and seg_rows % 512 == 0
+        and w_up.shape[1] % 512 == 0
+        and w_up.shape[1] == 2 * width
+        and ctx * seg_rows <= 2048
+        and width <= 768
+        and w_up.shape[1] <= 1536
+    )
+
+
+def fast_layer(
+    frames,
+    lengths,
+    cotangent,
+    ln1_gain,
+    ln1_bias,
+    w_query,
+    b_query,
+    w_key,
+    w_value,
+    b_value,
+    w_out,
+    b_out,
+    ln2_gain,
+    ln2_bias,
+    w_up,
+    b_up,
+    w_down,
+    b_down,
+):
+    S, C = lax.axis_size("shard"), lax.axis_size("ctx")
+    unused, R, D = frames.shape
+    FH = w_up.shape[1]
+    HG, CH = 3, C // 2
+    G, GP = HG * HD, 256
+    DB = D // (S * C)
+    HF = R // 2
+    PB = C * DB
+    T = C * R
+
+    def grouped(array):
+        parts = array.reshape(array.shape[:-1] + (CH, G))
+        return jnp.pad(parts, [(0, 0)] * (parts.ndim - 1) + [(0, GP - G)])
+
+    wqkv = jnp.concatenate([grouped(w_key), grouped(w_value), grouped(w_query)], axis=-1)
+    wqkv = wqkv.transpose(1, 0, 2)
+    bias = jnp.concatenate(
+        [jnp.zeros((CH, GP), F32), grouped(b_value), grouped(b_query)], axis=-1
+    )
+    bias = jnp.broadcast_to(bias[:, None, :], (CH, 8, 3 * GP))
+    wf = jnp.concatenate([w_up, w_down.T, grouped(w_out.T).reshape(DB, CH * GP)], axis=1)
+    WF = wf.shape[1]
+    vecs = jnp.stack([ln1_gain, ln1_bias, b_out, ln2_gain, ln2_bias, b_down, b_down, b_down])
+    vmem = pl.BlockSpec(memory_space=pltpu.VMEM)
+    V = pltpu.VMEM
+    dims = (S, C, R, D, GP, HG, FH)
+    scratch = [
+        pltpu.SemaphoreType.DMA((SEMS,)),
+        pltpu.SemaphoreType.DMA((SEMS,)),
+        pltpu.SemaphoreType.DMA((2 * CH,)),
+        V((T, D), BF16),
+        V((D, C * HF), BF16),
+        V((S, 2, CH * DB, 3 * GP), BF16),
+        V((2, CH, 8, 3 * GP), F32),
+        V((D, WF), BF16),
+        V((D, CH * GP), BF16),
+        V((GP, T), BF16),
+        V((GP, T), BF16),
+        V((T, GP), BF16),
+        V((T, GP), BF16),
+        V((C * HF, GP), BF16),
+        V((GP, C * HF), BF16),
+        V((C * HF, 8), F32),
+        V((C * HF, GP), F32),
+        V((C * HF, GP), BF16),
+        V((C * HF, GP), BF16),
+        V((HF, D), F32),
+        V((R, D), BF16),
+        V((D, R), BF16),
+        V((R, D), BF16),
+        V((D, R), BF16),
+        V((R, FH), BF16),
+        V((R, FH), BF16),
+        V((HF, D), BF16),
+        V((HF, D), BF16),
+        V((HF, D), BF16),
+        V((HF, D), BF16),
+        V((D, HF), BF16),
+        V((C * HF, GP), BF16),
+        V((GP, HF), BF16),
+        V((D, 2 * FH), BF16),
+        V((S - 1, PB, 2 * FH), BF16),
+        V((C - 1, DB, 2 * FH), BF16),
+        V((2, D, CH * GP), BF16),
+        V((S - 1, PB, CH * GP), BF16),
+        V((PB, CH * GP), BF16),
+        V((C - 1, DB, CH * GP), BF16),
+        V((G, T), F32),
+        V((G, T), F32),
+        V((HF, GP), F32),
+        V((C, 2, G, HF), BF16),
+        V((C, 2, G, HF), BF16),
+        V((C * HF, 3 * GP), BF16),
+        V((C * HF, D), BF16),
+        V((C - 1, HF, D), BF16),
+        V((S, 2, CH * DB, 3 * GP), BF16),
+        V((S, CH * DB, 3 * GP), BF16),
+        V((S - 1, CH * DB, 3 * GP), BF16),
+        V((CH, DB, 3 * GP), BF16),
+        V((CH, DB, 3 * GP), BF16),
+        V((16, D), F32),
+        V((S, 16, D), F32),
+        V((C, 16, D), F32),
+        V((2, 16, D), F32),
+    ]
+    outs = (
+        jax.ShapeDtypeStruct((R, D), BF16),
+        jax.ShapeDtypeStruct((R, D), F32),
+        jax.ShapeDtypeStruct((DB, 2 * FH), F32),
+        jax.ShapeDtypeStruct((DB, CH * GP), F32),
+        jax.ShapeDtypeStruct((CH, DB, 3 * GP), F32),
+        jax.ShapeDtypeStruct((16, D), F32),
+    )
+    output, grad_input, gf, go, gq, sums = pl.pallas_call(
+        functools.partial(layer_kernel, dims),
+        out_shape=outs,
+        in_specs=[vmem, vmem, pl.BlockSpec(memory_space=pltpu.SMEM)] + [vmem] * 5,
+        out_specs=[vmem] * 6,
+        scratch_shapes=scratch,
+        compiler_params=pltpu.CompilerParams(
+            collective_id=0, has_side_effects=True, vmem_limit_bytes=63 << 20
+        ),
+    )(frames[0], cotangent[0], lengths, vecs, b_up.reshape(1, FH), wqkv, bias, wf)
+    c = lax.axis_index("tp")
+
+    def ungroup(array, start):
+        part = array[..., start : start + G]
+        return part
+
+    def heads_of(start):
+        return gq[:, :, start : start + G].transpose(1, 0, 2).reshape(DB, CH * G)
+
+    biases = lax.dynamic_slice_in_dim(sums, 10 + CH * c, CH, 0)
+    grad_b_up = lax.dynamic_slice_in_dim(sums, 6 + 2 * c, 2, 0).reshape(FH)
+    return (
+        output[None],
+        grad_input[None],
+        sums[0],
+        sums[1],
+        heads_of(2 * GP),
+        biases[:, 2 * GP : 2 * GP + G].reshape(CH * G),
+        heads_of(0),
+        heads_of(GP),
+        biases[:, GP : GP + G].reshape(CH * G),
+        go.reshape(DB, CH, GP)[:, :, :G].reshape(DB, CH * G).T,
+        sums[2],
+        sums[3],
+        sums[4],
+        gf[:, :FH],
+        grad_b_up,
+        gf[:, FH:].T,
+        sums[5],
+    )
+
+
+def per_device(frames, lengths, cotangent, *params):
+    if fits(frames, params[2], params[11]):
+        return fast_layer(frames, lengths, cotangent, *params)
+    return plain_layer(frames, lengths, cotangent, *params)
+
+
 def solution(mesh):
     in_specs = (
         P("shard", "ctx", None),

time: 1370 us -> 270 us (0.20)
  waiting for transfers between devices: 928 us -> 0 us
  Pallas kernels: 0 us -> 246 us
  blocking collectives: 215 us -> 0 us
  matrix products: 113 us -> 0 us
  other arithmetic: 37 us -> 2.43 us
  local copies, waits for them, and re-layouts: 50 us -> 18.1 us
  between operations: 17.1 us -> 1.59 us
    reduce_scatter x8 -> x0, waiting for transfers between devices: 767 us -> none  [the longest x1 142 us: per_device(): lax.psum_scatter(grad_w_up, ('shard', 'ctx'), scatter_dimension=0, tiled=...]
    pallas_call x0 -> x1, Pallas kernels: none -> 246 us  [fast_layer(): pl.pallas_call(functools.partial(layer_kernel, dims), out_shape=outs, in_...]
    all_gather x4 -> x0, blocking collectives: 157 us -> none  [the longest x1 42.9 us: per_device(): lax.all_gather(w_value, ('shard', 'ctx'), axis=0, tiled=True)]
    dot_general x46 -> x0, matrix products: 113 us -> none  [the longest x4 18.6 us: output_step(): jnp.einsum('hqk,khd->qhd', weights_here, block_values, preferred_element_...]
    all_gather x4 -> x0, waiting for transfers between devices: 93.9 us -> none  [the longest x1 52.6 us: per_device(): lax.all_gather(w_down, ('shard', 'ctx'), axis=1, tiled=True)]
    psum x3 -> x0, waiting for transfers between devices: 66.3 us -> none  [the longest x1 46.6 us: per_device(): lax.psum(jnp.dot(attended_low, weight_out, preferred_element_type=jnp.flo...]
    psum x1 -> x0, blocking collectives: 58.6 us -> none  [per_device(): lax.psum((grad_ln1_gain, grad_ln1_bias, grad_b_query, grad_b_value, grad_...]
    reduce_sum x14 -> x0, other arithmetic: 21 us -> none  [the longest x4 5.51 us: totals_step(): jnp.sum(jnp.exp(scores - new_max[:, :, None]), axis=-1)]
  transfers between devices with their start and end apart: 15 -> 0, of which waited for: 12 -> 0; matrix products, arithmetic and copies ran while one was open for 5% -> 0% of each run, Pallas kernels for 0% -> 0%
where the time goes in v1:
time: 270 us; the launch traced here: 268 us
  Pallas kernels  246 us (91%)
  local copies, waits for them, and re-layouts  18.1 us (7%)
    pallas_call x1, Pallas kernels, fast_layer(): pl.pallas_call(functools.partial(layer_kernel, dims), out_shape=outs, in_...  246 us

profile of v1, /device:TPU:17, one launch (start us, length us, event | category | flops | bytes accessed | tf_op | source)
XLA Modules:
  0.0 268.1 jit_solution(2705915511939873135)
XLA Ops:
  0.7 0.0 copy-start.11
  0.7 0.0 copy-start.12
  0.8 0.9 reshape.89
  1.7 1.7 pad_maximum_fusion.wf_own
  3.5 0.9 reshape.84
  4.4 0.9 reshape.85
  5.3 0.9 reshape.86
  6.1 0.7 fusion.6.wqkv_own
  6.8 0.1 reshape.87
  6.9 0.1 reshape.88
  7.0 0.6 broadcast_in_dim.16.bias_own
  7.8 0.7 stack.29.vecs
  8.4 0.6 reshape.83.b_up
  9.7 245.9 %shard_map.305 = (bf16[512,768]{1,0:T(8,128)(2,1)}, f32[512,768]{1,0:T(8,128)}, f32[48,3072]{1,0:T(8,128)}, f32[48,512]{1,0:T(8,128)}, f32[2,48,768]{2,1,0:T(8,128)}, /*index=5*/f32[16,768]{1,0:T(8,128)}) custom-call(bf16[512,768]{1,0:T(8,128)(2,1)} %bitcast.22, bf16[512,768]{1,0:T(8,128)(2,1)} %bitcast.23, s32[1]{0:T(128)S(6)} %copy.44.lengths, ...), custom_call_target="tpu_custom_call" | custom-call | tf_op jit(solution)/shard_map/pallas_call | solution.py:1319
  255.6 0.9 fusion.9
  256.5 0.7 reshape.92
  257.1 0.7 reshape.95
  257.8 0.7 constant_dynamic-slice_fusion
  258.5 0.6 reshape.98
  259.1 1.6 slice_reduce_fusion
  260.8 1.1 slice_bitcast_fusion.1
  261.8 0.1 copy.38
  261.9 0.8 reshape.91
  262.7 0.1 copy.39
  262.8 0.8 reshape.93
  263.5 0.1 copy.40
  263.6 0.8 reshape.94
  264.4 0.8 slice_bitcast_fusion
  265.2 0.1 reshape.96
  265.3 0.8 reshape.97
  266.0 0.9 copy.45
  266.9 1.1 copy.46
  (38 shorter events, 0.2 us)
Async XLA Ops:
  0.7 6.2 %copy-start.11 = (f32[384]{0:T(512)S(1)}, f32[384]{0:T(512)}, u32[]{:S(2)}) copy-start(f32[384]{0:T(512)} %param.27) | copy-start | bytes 4612
  0.7 6.3 %copy-start.12 = (f32[384]{0:T(512)S(1)}, f32[384]{0:T(512)}, u32[]{:S(2)}) copy-start(f32[384]{0:T(512)} %param.24) | copy-start | bytes 4612
  0.7 7.0 %copy-start.5 = (f32[768]{0:T(1024)S(1)}, f32[768]{0:T(1024)}, u32[]{:S(2)}) copy-start(f32[768]{0:T(1024)} %param.21) | copy-start | bytes 9220
  0.7 7.0 %copy-start.6 = (f32[768]{0:T(1024)S(1)}, f32[768]{0:T(1024)}, u32[]{:S(2)}) copy-start(f32[768]{0:T(1024)} %param.22) | copy-start | bytes 9220
  0.7 7.0 %copy-start.7 = (f32[768]{0:T(1024)S(1)}, f32[768]{0:T(1024)}, u32[]{:S(2)}) copy-start(f32[768]{0:T(1024)} %param.29) | copy-start | bytes 9220
  0.7 7.0 %copy-start.8 = (f32[768]{0:T(1024)S(1)}, f32[768]{0:T(1024)}, u32[]{:S(2)}) copy-start(f32[768]{0:T(1024)} %param.30) | copy-start | bytes 9220
  0.7 7.0 %copy-start.9 = (f32[768]{0:T(1024)S(1)}, f32[768]{0:T(1024)}, u32[]{:S(2)}) copy-start(f32[768]{0:T(1024)} %param.31) | copy-start | bytes 9220
  0.7 7.0 %copy-start.10 = (f32[768]{0:T(1024)S(1)}, f32[768]{0:T(1024)}, u32[]{:S(2)}) copy-start(f32[768]{0:T(1024)} %param.35) | copy-start | bytes 9220
  0.7 7.7 %copy-start.4 = (f32[1536]{0:T(1024)S(1)}, f32[1536]{0:T(1024)}, u32[]{:S(2)}) copy-start(f32[1536]{0:T(1024)} %param.33) | copy-start | bytes 18436
  255.6 8.8 %copy-start.2 = (f32[48,3072]{1,0:T(8,128)S(1)}, f32[48,3072]{1,0:T(8,128)}, u32[]{:S(2)}) copy-start(f32[48,3072]{1,0:T(8,128)} %get-tuple-element.28) | copy-start | bytes 1769476
  255.6 9.6 %copy-start.3 = (f32[48,512]{1,0:T(8,128)S(1)}, f32[48,512]{1,0:T(8,128)}, u32[]{:S(2)}) copy-start(f32[48,512]{1,0:T(8,128)} %get-tuple-element.27) | copy-start | bytes 294916
  260.8 5.3 %copy-start.1 = (bf16[512,768]{1,0:T(8,128)(2,1)S(1)}, bf16[512,768]{1,0:T(8,128)(2,1)}, u32[]{:S(2)}) copy-start(bf16[512,768]{1,0:T(8,128)(2,1)} %get-tuple-element.23) | copy-start | bytes 2359300
  264.4 2.6 copy-start

commit v2 on v1

--- a/solution.py
+++ b/solution.py
@@ -466,7 +466,9 @@
     gatt_r,
     gatt_t,
     wg,
-    wg_r,
+    wg_t,
+    wg_x,
+    wg_y,
     wg_zr,
     og_x,
     og_r,
@@ -475,22 +477,26 @@
     dk_t,
     dv_t,
     dq_f,
+    dlt,
     dkv_s,
     dkv_r,
-    g_nat,
-    ga_s,
     ga_r,
+    ga_f,
     qg,
     qg_r,
     qg_p,
     qg_z,
     qg_zr,
     sums,
+    pairs,
     sum_p,
     sum_z,
     sum_c,
 ):
     S, C, R, D, GP, HG, FH = dims
+    ga_s = a_all.at[pl.ds(0, C * R // 2), :]
+    g_nat = a_all.at[pl.ds(C * R // 2, C * R // 2), :]
+    WF = 2 * FH + C // 2 * GP
     HF = R // 2
     CH = C // 2
     DB = D // (S * C)
@@ -516,7 +522,7 @@
             device_id_type=MESH,
         )
 
-    def send(src, dst, index, device, when=None):
+    def send(src, dst, index, device, when=None, like=None):
         def go():
             remote(src, dst, index, device).start()
 
@@ -524,7 +530,18 @@
             go()
         else:
             pl.when(when)(go)
-        owed.append((src, dst, index, device, when))
+        owed.append((src if like is None else like, index, when))
+
+    def settle(entries):
+        for like, index, when in entries:
+
+            def done(like=like, index=index):
+                remote(like, like, index, sib).wait_send()
+
+            if when is None:
+                done()
+            else:
+                pl.when(when)(done)
 
     def arrive(dst, index, when=None):
         def go():
@@ -537,6 +554,11 @@
 
     def plane(k):
         return (lax.rem(s + k, S), z, c)
+
+    near_x = s + 1 - 2 * lax.rem(s, 2)
+    near_y = lax.rem(s + 2, 4)
+    far = near_y + 1 - 2 * lax.rem(s, 2)
+    to_x, to_y = (near_x, z, c), (near_y, z, c)
 
     def column(k):
         return (s, lax.rem(z + k, C), c)
@@ -563,8 +585,7 @@
     k_a = sems(2 * C)
     k_as = sems(2 * C)
     k_f = sems(2 * C)
-    k_fp0 = sems(S)
-    k_fp = sems(2 * C * S)
+    k_fp = sems(4 * 2 * C)
     k_wo = sems(1)
     k_att = sems(C)
     k_n2 = sems(1)
@@ -572,13 +593,13 @@
     k_gz = sems(1)
     k_out = sems(1)
     k_gatt = sems(C)
-    k_wg = sems(S)
+    k_wg = sems(6 * C)
     k_wgz = sems(C)
     k_ox = sems(1)
     k_og = sems(S)
     k_ogz = sems(C)
     k_dkv = sems(1)
-    k_ga = sems(C)
+    k_ga = sems(2 * C)
     k_qx = sems(1)
     k_qp = sems(S)
     k_qz = sems(CH)
@@ -622,15 +643,6 @@
         at = z * R + first + lax.broadcasted_iota(jnp.int32, (count, 1), 0)
         return (at < length).astype(F32)
 
-    def first_norm(i, carry):
-        at = pl.ds(pl.multiple_of(i * 64, 64), 64)
-        to = pl.ds(pl.multiple_of(z * R + i * 64, 64), 64)
-        normed, unused = norm(frames[at, :].astype(F32))
-        a_all[to, :] = (normed * ln1_gain + ln1_bias).astype(BF16)
-        g_n[at, :] = (cot[at, :].astype(F32) * live_of(i * 64, 64)).astype(BF16)
-        return carry
-
-    lax.fori_loop(0, R // 64, first_norm, 0)
     sums[...] = jnp.zeros_like(sums)
     pl.semaphore_wait(barrier, len(friends))
 
@@ -661,39 +673,124 @@
     send(bias_own, bias_all.at[c], k_bias, sib)
     bias_all[c] = bias_own[...]
     mine_rows = rows_of(s * C + z)
-    for k in range(1, S):
-        send(wf_own, wf.at[mine_rows, :], k_fp0 + k, plane(k))
     can_right, can_left = z + 1 < C, z >= 1
 
+    def line_step(view, t, index, like):
+        send(
+            view(jnp.maximum(z - t, 0)),
+            view(jnp.maximum(z - t, 0)),
+            index + 2 * t,
+            (s, jnp.minimum(z + 1, C - 1), c),
+            goes_right[t],
+            like,
+        )
+        send(
+            view(jnp.minimum(z + t, C - 1)),
+            view(jnp.minimum(z + t, C - 1)),
+            index + 2 * t + 1,
+            (s, jnp.maximum(z - 1, 0), c),
+            goes_left[t],
+            like,
+        )
+
+    goes_right = [jnp.logical_and(can_right, z - t >= 0) for t in range(C - 1)]
+    goes_left = [jnp.logical_and(can_left, z + t < C) for t in range(C - 1)]
+    like_f = wf.at[pl.ds(0, DB), :]
+    like_fh = wf.at[pl.ds(0, DB), pl.ds(0, WF // 2)]
+    like_a = a_all.at[pl.ds(0, HF), :]
+
+    def f_step(t):
+        line_step(lambda block: wf.at[rows_of(s * C + block), :], t, k_f, like_f)
+
     def a_step(t):
-        send(
-            a_all.at[half_rows(jnp.maximum(z - t, 0), c), :],
-            a_all.at[half_rows(jnp.maximum(z - t, 0), c), :],
-            k_a + 2 * t,
-            (s, jnp.minimum(z + 1, C - 1), c),
-            jnp.logical_and(can_right, z - t >= 0),
-        )
-        send(
-            a_all.at[half_rows(jnp.minimum(z + t, C - 1), c), :],
-            a_all.at[half_rows(jnp.minimum(z + t, C - 1), c), :],
-            k_a + 2 * t + 1,
-            (s, jnp.maximum(z - 1, 0), c),
-            jnp.logical_and(can_left, z + t < C),
-        )
-
+        line_step(lambda block: a_all.at[half_rows(block, c), :], t, k_a, like_a)
+
+    def from_left(t):
+        return jnp.maximum(z - 1 - t, 0), z - 1 - t >= 0
+
+    def from_right(t):
+        return jnp.minimum(z + 1 + t, C - 1), z + 1 + t < C
+
+    halves = (slice(0, WF // 2), slice(WF // 2, WF))
+
+    def row_of(shard, block):
+        return rows_of(shard * C + block)
+
+    labels_of = [
+        ((2 * t + 2,) + from_left(t), (2 * t + 3,) + from_right(t)) for t in range(C - 1)
+    ]
+    own_label = ((0, z, None),)
+    wo_cols = slice(2 * FH, 2 * FH + CH * GP)
+
+    def wo_pass(shard, block, ok, src=None):
+        def go():
+            at = row_of(shard, block)
+            view = wf.at[at, wo_cols] if src is None else src.at[:, wo_cols]
+            remote(view, wo_sib.at[at, :], k_wo, sib).start()
+
+        if ok is None:
+            go()
+        else:
+            pl.when(ok)(go)
+
+
+    def f_plane(labels, src=None):
+        for label, block, ok in labels:
+            at = wf.at[row_of(s, block), :]
+            send(src if src is not None else at, at, k_fp + 4 * label, to_x, ok, like_f)
+            send(src if src is not None else at, at, k_fp + 4 * label + 1, to_y, ok, like_f)
+            wo_pass(s, block, ok, src)
+
+    def f_relay(labels):
+        for label, block, ok in labels:
+            at_x, at_y = wf.at[row_of(near_x, block), :], wf.at[row_of(near_y, block), :]
+            arrive(at_x, k_fp + 4 * label, ok)
+            at = wf.at[row_of(near_x, block), halves[0]]
+            send(at, at, k_fp + 4 * label + 2, to_y, ok, like_fh)
+            arrive(at_y, k_fp + 4 * label + 1, ok)
+            at = wf.at[row_of(near_y, block), halves[1]]
+            send(at, at, k_fp + 4 * label + 3, to_x, ok, like_fh)
+            wo_pass(near_x, block, ok)
+            wo_pass(near_y, block, ok)
+
+    def f_finish(labels):
+        for label, block, ok in labels:
+            for i in (1, 0):
+                arrive(wf.at[row_of(far, block), halves[i]], k_fp + 4 * label + 2 + i, ok)
+                if i == 1:
+                    wo_pass(far, block, ok)
+
+    def f_arrive(t):
+        for side, (label, block, ok) in enumerate(labels_of[t]):
+            arrive(wf.at[row_of(s, block), :], k_f + 2 * t + side, ok)
+        f_plane(labels_of[t])
+
+    wf[mine_rows, :] = wf_own[...]
+    f_step(0)
+    def first_norm(i, carry):
+        at = pl.ds(pl.multiple_of(i * 64, 64), 64)
+        to = pl.ds(pl.multiple_of(z * R + i * 64, 64), 64)
+        normed, unused = norm(frames[at, :].astype(F32))
+        a_all[to, :] = (normed * ln1_gain + ln1_bias).astype(BF16)
+        g_n[at, :] = (cot[at, :].astype(F32) * live_of(i * 64, 64)).astype(BF16)
+        return carry
+
+    lax.fori_loop(0, R // 64, first_norm, 0)
     a_step(0)
-    wf[mine_rows, :] = wf_own[...]
-    key_at = lax.broadcasted_iota(jnp.int32, (GP - LIVE_LANE, C * R), 1)
-    first_row = lax.broadcasted_iota(jnp.int32, (GP - LIVE_LANE, C * R), 0) == 0
-    dead = jnp.where(jnp.logical_and(first_row, key_at >= length), NEG, 0.0)
-    k_tr[LIVE_LANE:, :] = dead.astype(BF16)
-    v_tr[LIVE_LANE:, :] = jnp.zeros((GP - LIVE_LANE, C * R), BF16)
     for i in range(CH):
         from_z = CH * c + i
         same = jnp.logical_and(from_z == z, c_of_z == c)
         arrive(wqkv.at[s, c, pl.ds(i * DB, DB), :], k_q1 + i, jnp.logical_not(same))
     for k in range(1, S):
         send(wqkv.at[s, c], wqkv.at[s, c], k_q2 + k, plane(k))
+    f_plane(own_label, wf_own)
+    key_at = lax.broadcasted_iota(jnp.int32, (GP - LIVE_LANE, C * R), 1)
+    first_row = lax.broadcasted_iota(jnp.int32, (GP - LIVE_LANE, C * R), 0) == 0
+    dead = jnp.where(jnp.logical_and(first_row, key_at >= length), NEG, 0.0)
+    k_tr[LIVE_LANE:, :] = dead.astype(BF16)
+    v_tr[LIVE_LANE:, :] = jnp.zeros((GP - LIVE_LANE, C * R), BF16)
+    g_t[:, :HF] = flip(g_n[:HF, :])
+    g_t[:, HF:] = flip(g_n[HF:, :])
     for k in range(1, S):
         arrive(wqkv.at[s_from(k), c], k_q2 + k)
     send(wqkv.at[:, c], wqkv.at[:, c], k_q3, sib)
@@ -701,96 +798,79 @@
     arrive(wqkv.at[:, o], k_q3)
     bias_z = bias_all[c_of_z, z - CH * c_of_z]
 
-    def project(block, half, own):
+    def project(block, half):
         at = half_rows(block, half)
         rows = a_all[at, :]
-        width = 3 * GP if own else 2 * GP
-        weights = wqkv[:, :, :, :width].reshape(D, width)
-        made = nn(rows, weights) + bias_z[0:1, :width]
+        made = nn(rows, wqkv[...].reshape(D, 3 * GP)) + bias_z[0:1, :]
         keys = made[:, :GP].astype(BF16)
         values = made[:, GP : 2 * GP].astype(BF16)
         k_n[at, :] = keys
         v_n[at, :] = values
         k_tr[:LIVE_LANE, at] = flip(keys)[:LIVE_LANE, :]
         v_tr[:LIVE_LANE, at] = flip(values)[:LIVE_LANE, :]
-        if own:
+
+        def own():
             queries = made[:, 2 * GP :].astype(BF16).astype(F32) * (HD**-0.5)
             queries = jnp.where(lane == LIVE_LANE, 1.0, queries).astype(BF16)
             q_n[blk(block), :] = queries
             q_t[:, blk(block)] = flip(queries)
             a_t[:, blk(block)] = flip(rows)
 
-    project(z, c, True)
-    project(z, o, False)
-    g_t[:, :HF] = flip(g_n[:HF, :])
-    g_t[:, HF:] = flip(g_n[HF:, :])
-
-    def f_step(t):
-        send(
-            wf.at[rows_of(s * C + jnp.maximum(z - t, 0)), :],
-            wf.at[rows_of(s * C + jnp.maximum(z - t, 0)), :],
-            k_f + 2 * t,
-            (s, jnp.minimum(z + 1, C - 1), c),
-            jnp.logical_and(can_right, z - t >= 0),
-        )
-        send(
-            wf.at[rows_of(s * C + jnp.minimum(z + t, C - 1)), :],
-            wf.at[rows_of(s * C + jnp.minimum(z + t, C - 1)), :],
-            k_f + 2 * t + 1,
-            (s, jnp.maximum(z - 1, 0), c),
-            jnp.logical_and(can_left, z + t < C),
-        )
-
-    def from_left(t):
-        return jnp.maximum(z - 1 - t, 0), z - 1 - t >= 0
-
-    def from_right(t):
-        return jnp.minimum(z + 1 + t, C - 1), z + 1 + t < C
-
-    def f_arrive(t):
-        for side, (block, ok) in enumerate((from_left(t), from_right(t))):
-            arrive(wf.at[rows_of(s * C + block), :], k_f + 2 * t + side, ok)
-        if t + 1 < C - 1:
-            f_step(t + 1)
-        for side, (block, ok) in enumerate((from_left(t), from_right(t))):
-            for k in range(1, S):
-                send(
-                    wf.at[rows_of(s * C + block), :],
-                    wf.at[rows_of(s * C + block), :],
-                    k_fp + (2 * t + side) * S + k,
-                    plane(k),
-                    ok,
-                )
-
+        pl.when(half == c)(own)
+
+    def project_own(i, carry):
+        project(z, lax.rem(c + i, 2))
+        return carry
+
+    a_given = []
+
+    def remote_when(src, dst, index, device, when):
+        def go():
+            remote(src, dst, index, device).start()
+
+        pl.when(when)(go)
+
+    lax.fori_loop(0, 2, project_own, 0)
+    f_arrive(0)
+    f_relay(own_label)
     for t in range(C - 1):
-        sides = (from_left(t), from_right(t))
-        for side, (block, ok) in enumerate(sides):
+        if t == C - 2:
+            f_arrive(1)
+            for later in range(2, C - 1):
+                f_step(later)
+        for side, (label, block, ok) in enumerate(labels_of[t]):
             arrive(a_all.at[half_rows(block, c), :], k_a + 2 * t + side, ok)
+        if t == C - 3:
+            f_step(1)
         if t + 1 < C - 1:
             a_step(t + 1)
-        for side, (block, ok) in enumerate(sides):
-            send(
-                a_all.at[half_rows(block, c), :],
-                a_all.at[half_rows(block, c), :],
-                k_as + 2 * t + side,
-                sib,
-                ok,
-            )
+        for side, (label, block, ok) in enumerate(labels_of[t]):
+            at = a_all.at[half_rows(block, c), :]
+            remote_when(at, at, k_as + 2 * t + side, sib, ok)
+            a_given.append((like_a, k_as + 2 * t + side, ok))
+
+        def come(i, carry, t=t):
+            side = i // 2
+            block = jnp.where(side == 0, from_left(t)[0], from_right(t)[0])
+            ok = jnp.where(side == 0, z - 1 - t >= 0, z + 1 + t < C)
+
+            def other_half():
+                at = a_all.at[half_rows(block, o), :]
+                remote(at, at, k_as + 2 * t + side, sib).wait_recv()
+
+            def both():
+                pl.when(lax.rem(i, 2) == 1)(other_half)
+                project(block, lax.rem(c + i, 2))
+
+            pl.when(ok)(both)
+            return carry
+
+        lax.fori_loop(0, 4, come, 0)
         if t == C - 3:
-            f_step(0)
-        for side, (block, ok) in enumerate(sides):
-
-            def come(block=block, t=t, side=side):
-                project(block, c, True)
-                remote(
-                    a_all.at[half_rows(block, o), :],
-                    a_all.at[half_rows(block, o), :],
-                    k_as + 2 * t + side,
-                    sib,
-                ).wait_recv()
-                project(block, o, False)
-
-            pl.when(ok)(come)
+            f_relay(labels_of[0])
+    f_relay(labels_of[1])
+    f_finish(own_label)
+    f_finish(labels_of[0])
 
     TQ = 128
 
@@ -813,28 +893,40 @@
 
         lax.fori_loop(0, HF // TQ, step, 0)
 
-    for k in range(1, C):
-        block = lax.rem(z + k, C)
+    def attend_all(i, carry):
+        block = lax.rem(z + 1 + i, C)
         attend(block)
-        remote(att_s.at[blk(block), :], att_r.at[blk(z), :], k_att + k, column(k)).start()
-        f_arrive(k - 1)
-    attend(z)
+
+        def give():
+            remote(
+                att_s.at[blk(block), :], att_r.at[blk(z), :], k_att + 1 + i, column(1 + i)
+            ).start()
+
+        def more_weights():
+            for t in range(2, C - 1):
+                f_arrive(t)
+
+        pl.when(i < C - 1)(give)
+        pl.when(i == 1)(more_weights)
+        return carry
+
+    lax.fori_loop(0, C, attend_all, 0)
     att_r[blk(z), :] = att_s[blk(z), :]
 
-    for k in range(1, S):
-        arrive(wf.at[rows_of(s_from(k) * C + z), :], k_fp0 + k)
-        for t in range(C - 1):
-            for side, (block, ok) in enumerate((from_left(t), from_right(t))):
-                arrive(
-                    wf.at[rows_of(s_from(k) * C + block), :], k_fp + (2 * t + side) * S + k, ok
-                )
-    wo_cols = slice(2 * FH, 2 * FH + CH * GP)
-    send(wf.at[:, wo_cols], wo_sib, k_wo, sib)
+    f_finish(labels_of[1])
+    for t in range(2, C - 1):
+        f_relay(labels_of[t])
+    for t in range(2, C - 1):
+        f_finish(labels_of[t])
+    owed.append((wo_sib, k_wo, None))
     for k in range(1, C):
         arrive(att_r.at[blk(z_from(k)), :], k_att + k)
         remote(att_s.at[blk(z), :], att_r.at[blk(z), :], k_att + k, column(k)).wait_send()
     arrive(wo_sib, k_wo)
 
+    settle([entry for entry in owed if entry[0] is like_a])
+    settle(a_given)
+    owed[:] = [entry for entry in owed if entry[0] is not like_a]
     own_rows = pl.ds(pl.multiple_of(c * HF, HF), HF)
     hidden = frames[own_rows, :].astype(F32) + b_out
     for j in range(CH):
@@ -874,37 +966,79 @@
     lax.fori_loop(0, D // 256, z_grad, 0)
     send(gz_s, gz_r, k_gz, sib)
 
-    def down_part(i, carry):
-        at = pl.ds(pl.multiple_of(i * 256, 256), 256)
-        part_s[:, at] = nt(act[other_rows, :], wf[at, FH : 2 * FH]).astype(BF16)
+    def unit_grads(i, carry):
+        cols = pl.ds(pl.multiple_of(i * TF, TF), TF)
+        down = pl.ds(pl.multiple_of(FH + i * TF, TF), TF)
+        wg[:, cols] = nn(z_t[...], gup[:, cols]).astype(BF16)
+        wg[:, down] = nn(g_t[...], act[:, cols]).astype(BF16)
         return carry
 
-    lax.fori_loop(0, D // 256, down_part, 0)
-    send(part_s, part_r, k_part, sib)
-
-    def unit_grads(k):
-        at = pl.ds(pl.multiple_of(lax.rem(s + k, S) * PB, 64), PB)
-
+    lax.fori_loop(0, FH // TF, unit_grads, 0)
+
+    def part_z(j):
+        return lax.rem(z + 1 + j, C)
+
+    def part_rows(j):
+        return pl.ds(pl.multiple_of(part_z(j) * DB, 16), DB)
+
+    part_a, part_b = slice(0, FH), slice(FH, 2 * FH)
+    like_g = wg.at[pl.ds(0, DB), :]
+    like_gh = wg.at[pl.ds(0, DB), pl.ds(0, FH)]
+
+    def wg_first(j):
+        index = k_wg + 6 * j
+        own_z = part_z(j)
+        send(wg.at[row_of(far, own_z), part_a], wg_t.at[j, 0], index, to_x, like=like_gh)
+        send(wg.at[row_of(far, own_z), part_b], wg_t.at[j, 1], index + 1, to_y, like=like_gh)
+        near = wg.at[row_of(near_x, own_z), part_a]
+        send(near, wg_x.at[part_rows(j), part_a], index + 2, to_x, like=like_gh)
+        near = wg.at[row_of(near_y, own_z), part_b]
+        send(near, wg_y.at[part_rows(j), part_b], index + 3, to_y, like=like_gh)
+
+    def add_into(at, cols, others):
         def step(i, carry):
-            cols = pl.ds(pl.multiple_of(i * TF, TF), TF)
-            down = pl.ds(pl.multiple_of(FH + i * TF, TF), TF)
-            wg[at, cols] = nn(z_t[at, :], gup[:, cols]).astype(BF16)
-            wg[at, down] = nn(g_t[at, :], act[:, cols]).astype(BF16)
+            here = pl.ds(pl.multiple_of(cols.start + i * 256, 256), 256)
+            total = wg[at, here].astype(F32)
+            for other, rows, start in others:
+                there = pl.ds(pl.multiple_of(start + i * 256, 256), 256)
+                total = total + other[rows, there].astype(F32)
+            wg[at, here] = total.astype(BF16)
             return carry
 
-        lax.fori_loop(0, FH // TF, step, 0)
-
-    for k in range(1, S):
-        unit_grads(k)
-        at = pl.ds(pl.multiple_of(lax.rem(s + k, S) * PB, 64), PB)
-        send(wg.at[at, :], wg_r.at[k - 1], k_wg + k, plane(k))
+        lax.fori_loop(0, (cols.stop - cols.start) // 256, step, 0)
+
+    def wg_second(j):
+        index = k_wg + 6 * j
+        own_z = part_z(j)
+        arrive(wg_t.at[j, 0], index)
+        at = row_of(near_y, own_z)
+        add_into(at, part_a, [(wg_t.at[j, 0], slice(None), 0)])
+        near = wg.at[at, part_a]
+        send(near, wg_y.at[part_rows(j), part_a], index + 4, to_y, like=like_gh)
+        arrive(wg_t.at[j, 1], index + 1)
+        at = row_of(near_x, own_z)
+        add_into(at, part_b, [(wg_t.at[j, 1], slice(None), 0)])
+        near = wg.at[at, part_b]
+        send(near, wg_x.at[part_rows(j), part_b], index + 5, to_x, like=like_gh)
+
+    def wg_third(j):
+        index = k_wg + 6 * j
+        arrive(wg_x.at[part_rows(j), part_a], index + 2)
+        arrive(wg_y.at[part_rows(j), part_b], index + 3)
+        arrive(wg_y.at[part_rows(j), part_a], index + 4)
+        arrive(wg_x.at[part_rows(j), part_b], index + 5)
+        at = row_of(s, part_z(j))
+        add_into(
+            at, slice(0, 2 * FH), [(wg_x, part_rows(j), 0), (wg_y, part_rows(j), 0)]
+        )
+        if j < C - 1:
+            send(wg.at[at, :], wg_zr.at[j], k_wgz + 1 + j, column(1 + j), like=like_g)
+
+    wg_first(0)
+    wg_first(1)
 
     gz_rows = jnp.concatenate(
         [nt(gup[own_rows, :], wf[i * 256 : (i + 1) * 256, :FH]) for i in range(D // 256)], axis=1
-    )
-    down_rows = jnp.concatenate(
-        [nt(act[own_rows, :], wf[i * 256 : (i + 1) * 256, FH : 2 * FH]) for i in range(D // 256)],
-        axis=1,
     )
     arrive(gz_r, k_gz)
     grad_z = gz_rows + gz_r[...].astype(F32)
@@ -933,76 +1067,61 @@
         send(att_s.at[blk(lax.rem(z + k, C)), :], gatt_r.at[blk(z), :], k_gatt + k, column(k))
     gatt_r[blk(z), :] = att_s[blk(z), :]
     ghl_t[...] = flip(low)
+    def down_part(i, carry):
+        at = pl.ds(pl.multiple_of(i * 256, 256), 256)
+        part_s[:, at] = nt(act[other_rows, :], wf[at, FH : 2 * FH]).astype(BF16)
+        return carry
+
+    lax.fori_loop(0, D // 256, down_part, 0)
+    send(part_s, part_r, k_part, sib)
+
     for j in range(CH):
         og_x[0, :, j * GP : (j + 1) * GP] = nn(ghl_t[...], att_r[blk(CH * o + j), :]).astype(BF16)
     remote(og_x.at[0], og_x.at[1], k_ox, sib).start()
-    arrive(part_r, k_part)
-    out_rows = live_own * (hid[...] + down_rows + part_r[...].astype(F32) + b_down)
-    out_o[own_rows, :] = out_rows.astype(BF16)
-    send(out_o.at[own_rows, :], out_o.at[own_rows, :], k_out, sib)
-    unit_grads(0)
-    for i in range(2):
-        sums[pl.ds(6 + 2 * c + i, 1), :] = jnp.sum(
-            gup[:, i * D : (i + 1) * D].astype(F32), axis=0, keepdims=True
-        )
-    arrive(og_x.at[1], k_ox)
-    remote(og_x.at[0], og_x.at[1], k_ox, sib).wait_send()
-    for j in range(CH):
-        cols = slice(j * GP, (j + 1) * GP)
-        own_part = nn(ghl_t[...], att_r[blk(CH * c + j), :])
-        og_x[0, :, cols] = (own_part + og_x[1, :, cols].astype(F32)).astype(BF16)
-    for k in range(1, S):
-        at = pl.ds(pl.multiple_of(lax.rem(s + k, S) * PB, 64), PB)
-        send(og_x.at[0, at, :], og_r.at[k - 1], k_og + k, plane(k))
-
     dk_t[...] = jnp.zeros_like(dk_t)
     dv_t[...] = jnp.zeros_like(dv_t)
     TK = 512
 
-    def attend_back(block):
-        at = blk(block)
-        gatt_t[...] = flip(gatt_r[at, :])
-        product = gatt_r[at, :].astype(F32) * att_f[at, :]
-        deltas = []
-        for h in range(HG):
-            deltas.append(jnp.sum(only_head(product, h), axis=-1, keepdims=True))
-        dq_f[...] = jnp.zeros_like(dq_f)
-
-        def step(i, carry):
-            keys = pl.ds(pl.multiple_of(i * TK, TK), TK)
+    steps = C * R // TK
+
+    def attend_back(polls):
+        def block_step(b, carry):
+            block = lax.rem(z + C - b, C)
+            at = blk(block)
+
+            def come():
+                remote(gatt_r.at[at, :], gatt_r.at[at, :], k_gatt + b, sib).wait_recv()
+
+            pl.when(b > 0)(come)
+            gatt_t[...] = flip(gatt_r[at, :])
+            product = gatt_r[at, :].astype(F32) * att_f[at, :]
+            deltas = [
+                jnp.sum(only_head(product, h), axis=-1, keepdims=True) for h in range(HG)
+            ]
             for h in range(HG):
-                head = slice(HD * h, HD * (h + 1))
-                scores = nn(only_head(q_n[at, :], h, True), k_tr[:, keys])
-                weights = jnp.exp(scores - lse[at, h : h + 1])
-                grads = nn(only_head(gatt_r[at, :], h), v_tr[:, keys])
-                grad_scores = (weights * (grads - deltas[h])).astype(BF16)
-                dv_t[head, keys] += nn(gatt_t[head, :], weights.astype(BF16))
-                dk_t[head, keys] += nn(q_t[head, at], grad_scores)
-                dq_f[...] += only_head(nn(grad_scores, k_n[keys, :]), h)
+                dlt[:, h : h + 1] = deltas[h]
+            dq_f[...] = jnp.zeros_like(dq_f)
+
+            def step(i, carry):
+                keys = pl.ds(pl.multiple_of(i * TK, TK), TK)
+                for h in range(HG):
+                    head = slice(HD * h, HD * (h + 1))
+                    scores = nn(only_head(q_n[at, :], h, True), k_tr[:, keys])
+                    weights = jnp.exp(scores - lse[at, h : h + 1])
+                    grads = nn(only_head(gatt_r[at, :], h), v_tr[:, keys])
+                    grad_scores = (weights * (grads - dlt[:, h : h + 1])).astype(BF16)
+                    dv_t[head, keys] += nn(gatt_t[head, :], weights.astype(BF16))
+                    dk_t[head, keys] += nn(q_t[head, at], grad_scores)
+                    dq_f[...] += only_head(nn(grad_scores, k_n[keys, :]), h)
+                for number, poll in polls:
+                    pl.when(b * steps + i == number)(poll)
+                return carry
+
+            lax.fori_loop(0, steps, step, 0)
+            g_nat[at, 2 * GP :] = (dq_f[...] * (HD**-0.5)).astype(BF16)
             return carry
 
-        lax.fori_loop(0, C * R // TK, step, 0)
-        g_nat[at, 2 * GP :] = (dq_f[...] * (HD**-0.5)).astype(BF16)
-
-    def wg_reduce():
-        for k in range(1, S):
-            arrive(wg_r.at[k - 1], k_wg + k)
-        for j in range(C):
-            part = pl.ds(j * DB, DB)
-            own = pl.ds(pl.multiple_of(s * PB + j * DB, 16), DB)
-
-            def step(i, carry):
-                cols = pl.ds(pl.multiple_of(i * 512, 512), 512)
-                total = wg[own, cols].astype(F32)
-                for k in range(1, S):
-                    total = total + wg_r[k - 1, part, cols].astype(F32)
-                wg[own, cols] = total.astype(BF16)
-                return carry
-
-            lax.fori_loop(0, 2 * FH // 512, step, 0)
-        for k in range(1, C):
-            at = pl.ds(pl.multiple_of(s * PB + lax.rem(z + k, C) * DB, 16), DB)
-            send(wg.at[at, :], wg_zr.at[k - 1], k_wgz + k, column(k))
+        lax.fori_loop(0, C, block_step, 0)
 
     def og_reduce():
         for k in range(1, S):
@@ -1016,19 +1135,52 @@
             at = pl.ds(pl.multiple_of(lax.rem(z + k, C) * DB, 16), DB)
             send(og_z.at[at, :], og_zr.at[k - 1], k_ogz + k, column(k))
 
-    attend_back(z)
-    for k in range(1, C):
-        arrive(gatt_r.at[blk(z_from(k)), :], k_gatt + k)
-    attend_back(z_from(1))
-    for k in range(2, C):
-        attend_back(z_from(k))
+    def poll_a():
+        wg_second(0)
+        wg_first(2)
+
+    def poll_b():
+        wg_second(1)
+        wg_first(3)
+
+    down_rows = jnp.concatenate(
+        [nt(act[own_rows, :], wf[i * 256 : (i + 1) * 256, FH : 2 * FH]) for i in range(D // 256)],
+        axis=1,
+    )
+    arrive(part_r, k_part)
+    out_rows = live_own * (hid[...] + down_rows + part_r[...].astype(F32) + b_down)
+    out_o[own_rows, :] = out_rows.astype(BF16)
+    send(out_o.at[own_rows, :], out_o.at[own_rows, :], k_out, sib)
+    for i in range(2):
+        sums[pl.ds(6 + 2 * c + i, 1), :] = jnp.sum(
+            gup[:, i * D : (i + 1) * D].astype(F32), axis=0, keepdims=True
+        )
+    arrive(og_x.at[1], k_ox)
+    remote(og_x.at[0], og_x.at[1], k_ox, sib).wait_send()
+    for j in range(CH):
+        cols = slice(j * GP, (j + 1) * GP)
+        own_part = nn(ghl_t[...], att_r[blk(CH * c + j), :])
+        og_x[0, :, cols] = (own_part + og_x[1, :, cols].astype(F32)).astype(BF16)
+    attend_back(
+        (
+            (1, poll_a),
+            (5, poll_b),
+            (9, lambda: wg_third(0)),
+            (11, lambda: wg_second(2)),
+            (15, lambda: wg_third(1)),
+        )
+    )
 
     for i in range(C):
         cols = pl.ds(pl.multiple_of(i * R + o * HF, HF), HF)
         dkv_s[i, 0] = dk_t[:, cols].astype(BF16)
         dkv_s[i, 1] = dv_t[:, cols].astype(BF16)
     send(dkv_s, dkv_r, k_dkv, sib)
-    wg_reduce()
+    wg_second(3)
+    for k in range(1, S):
+        at = pl.ds(pl.multiple_of(lax.rem(s + k, S) * PB, 64), PB)
+        send(og_x.at[0, at, :], og_r.at[k - 1], k_og + k, plane(k))
+
     arrive(dkv_r, k_dkv)
 
     def finish(block):
@@ -1041,45 +1193,82 @@
         g_nat[at, GP : 2 * GP] = jnp.concatenate([values_t, none], axis=0).T.astype(BF16)
         ga_s[at, :] = nt(g_nat[at, :], wqkv[...].reshape(D, 3 * GP)).astype(BF16)
 
-    for k in range(1, C):
-        block = lax.rem(z + k, C)
-        finish(block)
-        send(ga_s.at[blk(block), :], ga_r.at[k - 1], k_ga + k, column(k))
-    finish(z)
-    og_reduce()
-
+    def finish_all(b, carry):
+        finish(b)
+        return carry
+
+    lax.fori_loop(0, C, finish_all, 0)
+
+    like_ga = ga_s.at[pl.ds(0, HF), :]
+
+    def ga_send(t, side):
+        target = C - 1 - t if side == 0 else t
+        device = (s, jnp.minimum(z + 1, C - 1), c) if side == 0 else (s, jnp.maximum(z - 1, 0), c)
+        remote(ga_s.at[blk(target), :], ga_r.at[t, side], k_ga + 2 * t + side, device).start()
+
+    def ga_ahead(t, side):
+        return C - 1 - t > z if side == 0 else t < z
+
+    for t in range(C - 1):
+        for side in range(2):
+            behind = z >= 1 if side == 0 else z + 1 < C
+            first = jnp.logical_and(ga_ahead(t, side), jnp.logical_not(behind))
+            pl.when(first)(lambda t=t, side=side: ga_send(t, side))
+            owed.append((like_ga, k_ga + 2 * t + side, ga_ahead(t, side)))
+
+    def ga_hop(u):
+        for side in range(2):
+            t = u - z if side == 0 else u - (C - 1 - z)
+            behind = z >= 1 if side == 0 else z + 1 < C
+            ok = jnp.logical_and(jnp.logical_and(t >= 0, behind), ga_ahead(t, side))
+
+            def add(t=t, side=side):
+                at = blk(C - 1 - t if side == 0 else t)
+                arrive(ga_r.at[t, side], k_ga + 2 * t + side)
+                ga_s[at, :] = (ga_s[at, :].astype(F32) + ga_r[t, side].astype(F32)).astype(BF16)
+                ga_send(t, side)
+
+            pl.when(ok)(add)
+
+    column_sum = jnp.sum(g_nat[...].astype(F32), axis=0, keepdims=True)
+    sums[pl.ds(10 + z, 1), :] = column_sum
+    pair_lane = lax.broadcasted_iota(jnp.int32, (PB, 128), 1)
     for i in range(S):
         got = nn(a_t[i * PB : (i + 1) * PB, :], g_nat[...])
         qg[i] = got.reshape(2, CH * DB, 3 * GP).astype(BF16)
+        weights = wqkv[i].reshape(PB, 3 * GP).astype(F32)
+        with_a = jnp.sum(got * weights, axis=-1, keepdims=True)
+        alone = jnp.sum(weights * column_sum, axis=-1, keepdims=True)
+        pairs[i * PB : (i + 1) * PB, :] = jnp.where(
+            pair_lane == 0, with_a, jnp.where(pair_lane == 1, alone, 0.0)
+        )
     send(qg.at[:, o], qg_r, k_qx, sib)
-    sums[pl.ds(10 + z, 1), :] = jnp.sum(g_nat[...].astype(F32), axis=0, keepdims=True)
+    turned = pairs[...].T
+    sums[0:1, :] = (turned[0:1, :] - ln1_bias * turned[1:2, :]) / ln1_gain
+    sums[1:2, :] = turned[1:2, :]
     arrive(qg_r, k_qx)
     for i in range(S):
         qg_r[i] = (qg_r[i].astype(F32) + qg[i, c].astype(F32)).astype(BF16)
     for k in range(1, S):
         send(qg_r.at[lax.rem(s + k, S)], qg_p.at[k - 1], k_qp + k, plane(k))
 
-    own_block = blk(z)
-    for k in range(1, C):
-        arrive(ga_r.at[k - 1], k_ga + k)
-    grad_a = ga_s[own_block, :].astype(F32)
-    for k in range(1, C):
-        grad_a = grad_a + ga_r[k - 1].astype(F32)
-    normed, inverse = norm(frames[own_rows, :].astype(F32))
-    scaled = grad_a * ln1_gain
-    inner = (
-        scaled
-        - jnp.mean(scaled, axis=-1, keepdims=True)
-        - normed * jnp.mean(scaled * normed, axis=-1, keepdims=True)
-    )
-    sums[0:1, :] = jnp.sum(grad_a * normed, axis=0, keepdims=True)
-    sums[1:2, :] = jnp.sum(grad_a, axis=0, keepdims=True)
-    gin_o[own_rows, :] = gin_o[own_rows, :] + inner * inverse
-    send(gin_o.at[own_rows, :], gin_o.at[own_rows, :], k_gin, sib)
     sum_p[s] = sums[...]
     for k in range(1, S):
         send(sum_p.at[s], sum_p.at[s], k_sp + k, plane(k))
-
+    wg_third(2)
+    wg_third(3)
+    og_reduce()
+    ga_hop(1)
+    for u in range(2, C - 1):
+        ga_hop(u)
+    for k in range(1, S):
+        arrive(sum_p.at[s_from(k)], k_sp + k)
+    total = sum_p[0]
+    for k in range(1, S):
+        total = total + sum_p[k]
+    sum_z[z] = total
+    for k in range(1, C):
+        send(sum_z.at[z], sum_z.at[z], k_sz + k, column(k))
     for k in range(1, S):
         arrive(qg_p.at[k - 1], k_qp + k)
     total = qg_r[s].astype(F32)
@@ -1109,15 +1298,28 @@
 
         pl.when(same)(keep)
 
-    for k in range(1, S):
-        arrive(sum_p.at[s_from(k)], k_sp + k)
-    total = sum_p[0]
-    for k in range(1, S):
-        total = total + sum_p[k]
-    sum_z[z] = total
-    for k in range(1, C):
-        send(sum_z.at[z], sum_z.at[z], k_sz + k, column(k))
-
+    own_block = blk(z)
+    ga_f[...] = ga_s[own_block, :].astype(F32)
+    for t in range(C - 1):
+        for side in range(2):
+            target = C - 1 - t if side == 0 else t
+            behind = z >= 1 if side == 0 else z + 1 < C
+
+            def add(t=t, side=side):
+                arrive(ga_r.at[t, side], k_ga + 2 * t + side)
+                ga_f[...] += ga_r[t, side].astype(F32)
+
+            pl.when(jnp.logical_and(target == z, behind))(add)
+    grad_a = ga_f[...]
+    normed, inverse = norm(frames[own_rows, :].astype(F32))
+    scaled = grad_a * ln1_gain
+    inner = (
+        scaled
+        - jnp.mean(scaled, axis=-1, keepdims=True)
+        - normed * jnp.mean(scaled * normed, axis=-1, keepdims=True)
+    )
+    gin_o[own_rows, :] = gin_o[own_rows, :] + inner * inverse
+    send(gin_o.at[own_rows, :], gin_o.at[own_rows, :], k_gin, sib)
     def last(own, got, index, to):
         for k in range(1, C):
             arrive(got.at[k - 1], index + k)
@@ -1128,6 +1330,10 @@
 
     last(wg[rows_of(s * C + z), :], wg_zr, k_wgz, gf_o)
     last(og_z[pl.ds(pl.multiple_of(z * DB, 16), DB), :], og_zr, k_ogz, go_o)
+    for j in range(CH):
+        same = jnp.logical_and(CH * c + j == z, c_of_z == c)
+        arrive(qg_zr.at[j], k_qz + j, jnp.logical_not(same))
+    gq_o[...] = qg_zr[...].astype(F32)
     for k in range(1, C):
         arrive(sum_z.at[z_from(k)], k_sz + k)
     total = sum_z[0]
@@ -1135,24 +1341,12 @@
         total = total + sum_z[k]
     sum_c[c] = total
     send(sum_c.at[c], sum_c.at[c], k_sc, sib)
-    for j in range(CH):
-        same = jnp.logical_and(CH * c + j == z, c_of_z == c)
-        arrive(qg_zr.at[j], k_qz + j, jnp.logical_not(same))
-    gq_o[...] = qg_zr[...].astype(F32)
     arrive(sum_c.at[o], k_sc)
     sums_o[...] = sum_c[0] + sum_c[1]
     arrive(out_o.at[other_rows, :], k_out)
     arrive(gin_o.at[other_rows, :], k_gin)
 
-    for src, dst, index, device, when in owed:
-
-        def done(src=src, dst=dst, index=index, device=device):
-            remote(src, dst, index, device).wait_send()
-
-        if when is None:
-            done()
-        else:
-            pl.when(when)(done)
+    settle(owed)
     for j in range(CH):
         same = jnp.logical_and(CH * c + j == z, c_of_z == c)
 
@@ -1178,7 +1372,7 @@
     assert next_sem[0] <= SEMS
 
 
-SEMS = 160
+SEMS = 192
 
 
 def fits(frames, w_query, w_up):
@@ -1189,8 +1383,8 @@
         slot_count == 1
         and cores == 2
         and ctx % 2 == 0
-        and ctx > 2
-        and shards > 1
+        and ctx == 4
+        and shards == 4
         and heads == 3 * ctx
         and width % (16 * shards * ctx) == 0
         and width % 256 == 0
@@ -1284,7 +1478,9 @@
         V((C * HF, GP), BF16),
         V((GP, HF), BF16),
         V((D, 2 * FH), BF16),
-        V((S - 1, PB, 2 * FH), BF16),
+        V((C, 2, DB, FH), BF16),
+        V((PB, 2 * FH), BF16),
+        V((PB, 2 * FH), BF16),
         V((C - 1, DB, 2 * FH), BF16),
         V((2, D, CH * GP), BF16),
         V((S - 1, PB, CH * GP), BF16),
@@ -1293,17 +1489,18 @@
         V((G, T), F32),
         V((G, T), F32),
         V((HF, GP), F32),
+        V((HF, 8), F32),
         V((C, 2, G, HF), BF16),
         V((C, 2, G, HF), BF16),
-        V((C * HF, 3 * GP), BF16),
-        V((C * HF, D), BF16),
-        V((C - 1, HF, D), BF16),
+        V((C - 1, 2, HF, D), BF16),
+        V((HF, D), F32),
         V((S, 2, CH * DB, 3 * GP), BF16),
         V((S, CH * DB, 3 * GP), BF16),
         V((S - 1, CH * DB, 3 * GP), BF16),
         V((CH, DB, 3 * GP), BF16),
         V((CH, DB, 3 * GP), BF16),
         V((16, D), F32),
+        V((D, 128), F32),
         V((S, 16, D), F32),
         V((C, 16, D), F32),
         V((2, 16, D), F32),

time: 270 us -> 202 us (0.75)
  Pallas kernels: 246 us -> 178 us
    pallas_call x1, Pallas kernels: 246 us -> 178 us  [fast_layer(): pl.pallas_call(functools.partial(layer_kernel, dims), out_shape=outs, in_...]
where the time goes in v2:
time: 202 us; the launch traced here: 200 us
  Pallas kernels  178 us (88%)
  local copies, waits for them, and re-layouts  18.1 us (9%)
  other arithmetic  2.43 us (1%)
    pallas_call x1, Pallas kernels, fast_layer(): pl.pallas_call(functools.partial(layer_kernel, dims), out_shape=outs, in_...  178 us

profile of v2, /device:TPU:17, one launch (start us, length us, event | category | flops | bytes accessed | tf_op | source)
XLA Modules:
  0.0 200.4 jit_solution(14982058373048564078)
XLA Ops:
  0.7 0.0 copy-start.11
  0.7 0.0 copy-start.12
  0.8 0.9 reshape.89
  1.7 1.7 pad_maximum_fusion.wf_own
  3.5 0.9 reshape.84
  4.4 0.9 reshape.85
  5.3 0.9 reshape.86
  6.1 0.7 fusion.6.wqkv_own
  6.8 0.1 reshape.87
  6.9 0.1 reshape.88
  7.0 0.6 broadcast_in_dim.16.bias_own
  7.8 0.7 stack.29.vecs
  8.4 0.6 reshape.83.b_up
  9.7 178.3 %shard_map.305 = (bf16[512,768]{1,0:T(8,128)(2,1)}, f32[512,768]{1,0:T(8,128)}, f32[48,3072]{1,0:T(8,128)}, f32[48,512]{1,0:T(8,128)}, f32[2,48,768]{2,1,0:T(8,128)}, /*index=5*/f32[16,768]{1,0:T(8,128)}) custom-call(bf16[512,768]{1,0:T(8,128)(2,1)} %bitcast.22, bf16[512,768]{1,0:T(8,128)(2,1)} %bitcast.23, s32[1]{0:T(128)S(6)} %copy.44.lengths, ...), custom_call_target="tpu_custom_call" | custom-call | tf_op jit(solution)/shard_map/pallas_call | solution.py:1516
  187.9 0.9 fusion.9
  188.8 0.7 reshape.92
  189.5 0.7 reshape.95
  190.1 0.7 constant_dynamic-slice_fusion
  190.9 0.6 reshape.98
  191.5 1.6 slice_reduce_fusion
  193.1 1.1 slice_bitcast_fusion.1
  194.2 0.1 copy.38
  194.3 0.8 reshape.91
  195.0 0.1 copy.39
  195.1 0.8 reshape.93
  195.9 0.1 copy.40
  195.9 0.8 reshape.94
  196.7 0.8 slice_bitcast_fusion
  197.6 0.1 reshape.96
  197.6 0.8 reshape.97
  198.4 0.9 copy.45
  199.3 1.1 copy.46
  (38 shorter events, 0.2 us)
Async XLA Ops:
  0.7 6.2 %copy-start.11 = (f32[384]{0:T(512)S(1)}, f32[384]{0:T(512)}, u32[]{:S(2)}) copy-start(f32[384]{0:T(512)} %param.27) | copy-start | bytes 4612
  0.7 6.3 %copy-start.12 = (f32[384]{0:T(512)S(1)}, f32[384]{0:T(512)}, u32[]{:S(2)}) copy-start(f32[384]{0:T(512)} %param.24) | copy-start | bytes 4612
  0.7 7.0 %copy-start.5 = (f32[768]{0:T(1024)S(1)}, f32[768]{0:T(1024)}, u32[]{:S(2)}) copy-start(f32[768]{0:T(1024)} %param.21) | copy-start | bytes 9220
  0.7 7.0 %copy-start.6 = (f32[768]{0:T(1024)S(1)}, f32[768]{0:T(1024)}, u32[]{:S(2)}) copy-start(f32[768]{0:T(1024)} %param.22) | copy-start | bytes 9220
  0.7 7.0 %copy-start.7 = (f32[768]{0:T(1024)S(1)}, f32[768]{0:T(1024)}, u32[]{:S(2)}) copy-start(f32[768]{0:T(1024)} %param.29) | copy-start | bytes 9220
  0.7 7.0 %copy-start.8 = (f32[768]{0:T(1024)S(1)}, f32[768]{0:T(1024)}, u32[]{:S(2)}) copy-start(f32[768]{0:T(1024)} %param.30) | copy-start | bytes 9220
  0.7 7.0 %copy-start.9 = (f32[768]{0:T(1024)S(1)}, f32[768]{0:T(1024)}, u32[]{:S(2)}) copy-start(f32[768]{0:T(1024)} %param.31) | copy-start | bytes 9220
  0.7 7.0 %copy-start.10 = (f32[768]{0:T(1024)S(1)}, f32[768]{0:T(1024)}, u32[]{:S(2)}) copy-start(f32[768]{0:T(1024)} %param.35) | copy-start | bytes 9220
  0.7 7.7 %copy-start.4 = (f32[1536]{0:T(1024)S(1)}, f32[1536]{0:T(1024)}, u32[]{:S(2)}) copy-start(f32[1536]{0:T(1024)} %param.33) | copy-start | bytes 18436
  187.9 8.8 %copy-start.2 = (f32[48,3072]{1,0:T(8,128)S(1)}, f32[48,3072]{1,0:T(8,128)}, u32[]{:S(2)}) copy-start(f32[48,3072]{1,0:T(8,128)} %get-tuple-element.28) | copy-start | bytes 1769476
  187.9 9.6 %copy-start.3 = (f32[48,512]{1,0:T(8,128)S(1)}, f32[48,512]{1,0:T(8,128)}, u32[]{:S(2)}) copy-start(f32[48,512]{1,0:T(8,128)} %get-tuple-element.27) | copy-start | bytes 294916
  193.1 5.3 %copy-start.1 = (bf16[512,768]{1,0:T(8,128)(2,1)S(1)}, bf16[512,768]{1,0:T(8,128)(2,1)}, u32[]{:S(2)}) copy-start(bf16[512,768]{1,0:T(8,128)(2,1)} %get-tuple-element.23) | copy-start | bytes 2359300
  196.7 2.6 %copy-start = (f32[512,768]{1,0:T(8,128)S(1)}, f32[512,768]{1,0:T(8,128)}, u32[]{:S(2)}) copy-start(f32[512,768]{1,0:T(8,128)} %get-tuple-element.24) | copy-start | bytes 4718596

commit v3 on v2

--- a/solution.py
+++ b/solution.py
@@ -412,6 +412,19 @@
     return lax.dot_general(left, right, (((1,), (1,)), ((), ())), preferred_element_type=F32)
 
 
+def group(values, j):
+    taken = values[:, :256] if j == 0 else pltpu.roll(values[:, 128:384], 192, 1)
+    at = lax.broadcasted_iota(jnp.int32, taken.shape, 1)
+    return jnp.where(at < 3 * HD, taken, 0.0)
+
+
+def ungroup(first, second):
+    turned = pltpu.roll(second, 64, 1)
+    at = lax.broadcasted_iota(jnp.int32, turned.shape, 1)
+    tail = jnp.concatenate([first[:, 128:], first[:, 128:]], axis=1)
+    return jnp.concatenate([first[:, :128], jnp.where(at < 64, tail, turned)], axis=1)
+
+
 def flip(values):
     return values.astype(F32).T.astype(BF16)
 
@@ -421,20 +434,40 @@
     frames,
     cot,
     lengths,
-    vecs,
-    b_up,
-    wqkv_own,
-    bias_own,
-    wf_own,
+    v_gain1,
+    v_bias1,
+    v_b_out,
+    v_gain2,
+    v_bias2,
+    v_b_down,
+    v_b_up,
+    v_b_query,
+    v_b_value,
+    w_query,
+    w_key,
+    w_value,
+    w_up,
+    w_down,
+    w_out,
+    out_h,
+    gin_h,
+    gf_h,
+    go_h,
+    gq_h,
+    sums_h,
+    ss,
+    rs,
+    ls,
+    os,
     out_o,
     gin_o,
     gf_o,
     go_o,
     gq_o,
     sums_o,
-    ss,
-    rs,
-    ls,
+    wqkv_own,
+    bias_own,
+    up_bias,
     a_all,
     a_t,
     wqkv,
@@ -543,6 +576,13 @@
             else:
                 pl.when(when)(done)
 
+    stored = []
+
+    def store(src, dst):
+        copy = pltpu.make_async_copy(src, dst, os.at[len(stored)])
+        copy.start()
+        stored.append(copy)
+
     def arrive(dst, index, when=None):
         def go():
             remote(dst, dst, index, sib).wait_recv()
@@ -585,7 +625,7 @@
     k_a = sems(2 * C)
     k_as = sems(2 * C)
     k_f = sems(2 * C)
-    k_fp = sems(4 * 2 * C)
+    k_fp = sems(6 * 2 * C)
     k_wo = sems(1)
     k_att = sems(C)
     k_n2 = sems(1)
@@ -631,8 +671,23 @@
         return jnp.where(picked, values, jnp.zeros_like(values))
 
     ln1_gain, ln1_bias, b_out, ln2_gain, ln2_bias, b_down = (
-        vecs[i : i + 1, :] for i in range(6)
-    )
+        ref[...].reshape(1, D) for ref in (v_gain1, v_bias1, v_b_out, v_gain2, v_bias2, v_b_down)
+    )
+    for j in range(CH):
+        for i, part in enumerate((w_key, w_value, w_query)):
+            cols = slice(i * GP, (i + 1) * GP)
+            wqkv_own[j, :, cols] = group(part[...].astype(F32), j).astype(BF16)
+    mine_rows = rows_of(s * C + z)
+    wf[mine_rows, :FH] = w_up[...]
+    wf[mine_rows, FH : 2 * FH] = w_down[...]
+    out_t = w_out[...].astype(F32)
+    for j in range(CH):
+        cols = slice(2 * FH + j * GP, 2 * FH + (j + 1) * GP)
+        wf[mine_rows, cols] = group(out_t, j).astype(BF16)
+    for j in range(CH):
+        bias_own[j] = jnp.zeros((8, 3 * GP), F32)
+        bias_own[j, 0:1, GP : 2 * GP] = group(v_b_value[...].reshape(1, CH * 3 * HD), j)
+        bias_own[j, 0:1, 2 * GP :] = group(v_b_query[...].reshape(1, CH * 3 * HD), j)
 
     def norm(values):
         centred = values - jnp.mean(values, axis=-1, keepdims=True)
@@ -672,7 +727,6 @@
         pl.when(same)(keep)
     send(bias_own, bias_all.at[c], k_bias, sib)
     bias_all[c] = bias_own[...]
-    mine_rows = rows_of(s * C + z)
     can_right, can_left = z + 1 < C, z >= 1
 
     def line_step(view, t, index, like):
@@ -722,11 +776,10 @@
     own_label = ((0, z, None),)
     wo_cols = slice(2 * FH, 2 * FH + CH * GP)
 
-    def wo_pass(shard, block, ok, src=None):
+    def wo_pass(shard, block, ok):
         def go():
             at = row_of(shard, block)
-            view = wf.at[at, wo_cols] if src is None else src.at[:, wo_cols]
-            remote(view, wo_sib.at[at, :], k_wo, sib).start()
+            remote(wf.at[at, wo_cols], wo_sib.at[at, :], k_wo, sib).start()
 
         if ok is None:
             go()
@@ -734,38 +787,42 @@
             pl.when(ok)(go)
 
 
-    def f_plane(labels, src=None):
+    def f_plane(labels):
         for label, block, ok in labels:
-            at = wf.at[row_of(s, block), :]
-            send(src if src is not None else at, at, k_fp + 4 * label, to_x, ok, like_f)
-            send(src if src is not None else at, at, k_fp + 4 * label + 1, to_y, ok, like_f)
-            wo_pass(s, block, ok, src)
+            index = k_fp + 6 * label
+            for half in range(2):
+                at = wf.at[row_of(s, block), halves[half]]
+                send(at, at, index + half, to_x, ok, like_fh)
+                at = wf.at[row_of(s, block), halves[1 - half]]
+                send(at, at, index + 2 + half, to_y, ok, like_fh)
+            wo_pass(s, block, ok)
 
     def f_relay(labels):
         for label, block, ok in labels:
-            at_x, at_y = wf.at[row_of(near_x, block), :], wf.at[row_of(near_y, block), :]
-            arrive(at_x, k_fp + 4 * label, ok)
+            index = k_fp + 6 * label
             at = wf.at[row_of(near_x, block), halves[0]]
-            send(at, at, k_fp + 4 * label + 2, to_y, ok, like_fh)
-            arrive(at_y, k_fp + 4 * label + 1, ok)
+            arrive(at, index, ok)
+            send(at, at, index + 4, to_y, ok, like_fh)
             at = wf.at[row_of(near_y, block), halves[1]]
-            send(at, at, k_fp + 4 * label + 3, to_x, ok, like_fh)
-            wo_pass(near_x, block, ok)
+            arrive(at, index + 2, ok)
+            send(at, at, index + 5, to_x, ok, like_fh)
             wo_pass(near_y, block, ok)
 
     def f_finish(labels):
         for label, block, ok in labels:
-            for i in (1, 0):
-                arrive(wf.at[row_of(far, block), halves[i]], k_fp + 4 * label + 2 + i, ok)
-                if i == 1:
-                    wo_pass(far, block, ok)
+            index = k_fp + 6 * label
+            arrive(wf.at[row_of(near_x, block), halves[1]], index + 1, ok)
+            wo_pass(near_x, block, ok)
+            arrive(wf.at[row_of(near_y, block), halves[0]], index + 3, ok)
+            arrive(wf.at[row_of(far, block), halves[1]], index + 5, ok)
+            wo_pass(far, block, ok)
+            arrive(wf.at[row_of(far, block), halves[0]], index + 4, ok)
 
     def f_arrive(t):
         for side, (label, block, ok) in enumerate(labels_of[t]):
             arrive(wf.at[row_of(s, block), :], k_f + 2 * t + side, ok)
         f_plane(labels_of[t])
 
-    wf[mine_rows, :] = wf_own[...]
     f_step(0)
     def first_norm(i, carry):
         at = pl.ds(pl.multiple_of(i * 64, 64), 64)
@@ -783,7 +840,7 @@
         arrive(wqkv.at[s, c, pl.ds(i * DB, DB), :], k_q1 + i, jnp.logical_not(same))
     for k in range(1, S):
         send(wqkv.at[s, c], wqkv.at[s, c], k_q2 + k, plane(k))
-    f_plane(own_label, wf_own)
+    f_plane(own_label)
     key_at = lax.broadcasted_iota(jnp.int32, (GP - LIVE_LANE, C * R), 1)
     first_row = lax.broadcasted_iota(jnp.int32, (GP - LIVE_LANE, C * R), 0) == 0
     dead = jnp.where(jnp.logical_and(first_row, key_at >= length), NEG, 0.0)
@@ -945,10 +1002,12 @@
 
     TF = 256
 
+    up_bias[...] = v_b_up[...].reshape(1, FH)
+
     def units(i, carry):
         cols = pl.ds(pl.multiple_of(i * TF, TF), TF)
         down = pl.ds(pl.multiple_of(FH + i * TF, TF), TF)
-        upper = nn(z_all[...], wf[:, cols]) + b_up[:, cols]
+        upper = nn(z_all[...], wf[:, cols]) + up_bias[:, cols]
         cumulative = 0.5 * (1.0 + lax.erf(upper * INV_ROOT_TWO))
         act[:, cols] = (upper * cumulative).astype(BF16)
         slope = cumulative + upper * jnp.exp(-0.5 * upper * upper) * INV_ROOT_TAU
@@ -975,8 +1034,12 @@
 
     lax.fori_loop(0, FH // TF, unit_grads, 0)
 
+    near_end = jnp.minimum(z, C - 1 - z)
+    part_order = ((3, 3), (2, 0), (1, 2), (0, 1))
+
     def part_z(j):
-        return lax.rem(z + 1 + j, C)
+        chosen = jnp.where(near_end == 0, part_order[j][0], part_order[j][1])
+        return jnp.where(2 * z < C, chosen, C - 1 - chosen)
 
     def part_rows(j):
         return pl.ds(pl.multiple_of(part_z(j) * DB, 16), DB)
@@ -985,11 +1048,15 @@
     like_g = wg.at[pl.ds(0, DB), :]
     like_gh = wg.at[pl.ds(0, DB), pl.ds(0, FH)]
 
-    def wg_first(j):
+    def wg_far(j):
         index = k_wg + 6 * j
         own_z = part_z(j)
         send(wg.at[row_of(far, own_z), part_a], wg_t.at[j, 0], index, to_x, like=like_gh)
         send(wg.at[row_of(far, own_z), part_b], wg_t.at[j, 1], index + 1, to_y, like=like_gh)
+
+    def wg_near(j):
+        index = k_wg + 6 * j
+        own_z = part_z(j)
         near = wg.at[row_of(near_x, own_z), part_a]
         send(near, wg_x.at[part_rows(j), part_a], index + 2, to_x, like=like_gh)
         near = wg.at[row_of(near_y, own_z), part_b]
@@ -1032,10 +1099,12 @@
             at, slice(0, 2 * FH), [(wg_x, part_rows(j), 0), (wg_y, part_rows(j), 0)]
         )
         if j < C - 1:
-            send(wg.at[at, :], wg_zr.at[j], k_wgz + 1 + j, column(1 + j), like=like_g)
-
-    wg_first(0)
-    wg_first(1)
+            hop = lax.rem(part_z(j) + C - z, C)
+            remote(wg.at[at, :], wg_zr.at[hop - 1], k_wgz + hop, (s, part_z(j), c)).start()
+
+    wg_far(0)
+    wg_near(0)
+    wg_far(1)
 
     gz_rows = jnp.concatenate(
         [nt(gup[own_rows, :], wf[i * 256 : (i + 1) * 256, :FH]) for i in range(D // 256)], axis=1
@@ -1078,6 +1147,8 @@
     for j in range(CH):
         og_x[0, :, j * GP : (j + 1) * GP] = nn(ghl_t[...], att_r[blk(CH * o + j), :]).astype(BF16)
     remote(og_x.at[0], og_x.at[1], k_ox, sib).start()
+    old = list(owed)
+    owed.clear()
     dk_t[...] = jnp.zeros_like(dk_t)
     dv_t[...] = jnp.zeros_like(dv_t)
     TK = 512
@@ -1137,11 +1208,17 @@
 
     def poll_a():
         wg_second(0)
-        wg_first(2)
+        wg_near(1)
 
     def poll_b():
         wg_second(1)
-        wg_first(3)
+        wg_far(2)
+        wg_near(2)
+
+    def poll_c():
+        wg_second(2)
+        wg_far(3)
+        wg_near(3)
 
     down_rows = jnp.concatenate(
         [nt(act[own_rows, :], wf[i * 256 : (i + 1) * 256, FH : 2 * FH]) for i in range(D // 256)],
@@ -1163,11 +1240,11 @@
         og_x[0, :, cols] = (own_part + og_x[1, :, cols].astype(F32)).astype(BF16)
     attend_back(
         (
-            (1, poll_a),
-            (5, poll_b),
-            (9, lambda: wg_third(0)),
-            (11, lambda: wg_second(2)),
-            (15, lambda: wg_third(1)),
+            (0, poll_a),
+            (3, poll_b),
+            (6, lambda: wg_third(0)),
+            (10, lambda: wg_third(1)),
+            (11, poll_c),
         )
     )
 
@@ -1176,11 +1253,7 @@
         dkv_s[i, 0] = dk_t[:, cols].astype(BF16)
         dkv_s[i, 1] = dv_t[:, cols].astype(BF16)
     send(dkv_s, dkv_r, k_dkv, sib)
-    wg_second(3)
-    for k in range(1, S):
-        at = pl.ds(pl.multiple_of(lax.rem(s + k, S) * PB, 64), PB)
-        send(og_x.at[0, at, :], og_r.at[k - 1], k_og + k, plane(k))
-
+    wg_third(2)
     arrive(dkv_r, k_dkv)
 
     def finish(block):
@@ -1202,8 +1275,8 @@
     like_ga = ga_s.at[pl.ds(0, HF), :]
 
     def ga_send(t, side):
-        target = C - 1 - t if side == 0 else t
-        device = (s, jnp.minimum(z + 1, C - 1), c) if side == 0 else (s, jnp.maximum(z - 1, 0), c)
+        target = jnp.where(side == 0, C - 1 - t, t)
+        device = (s, jnp.clip(z + 1 - 2 * side, 0, C - 1), c)
         remote(ga_s.at[blk(target), :], ga_r.at[t, side], k_ga + 2 * t + side, device).start()
 
     def ga_ahead(t, side):
@@ -1217,19 +1290,26 @@
             owed.append((like_ga, k_ga + 2 * t + side, ga_ahead(t, side)))
 
     def ga_hop(u):
-        for side in range(2):
-            t = u - z if side == 0 else u - (C - 1 - z)
-            behind = z >= 1 if side == 0 else z + 1 < C
-            ok = jnp.logical_and(jnp.logical_and(t >= 0, behind), ga_ahead(t, side))
-
-            def add(t=t, side=side):
-                at = blk(C - 1 - t if side == 0 else t)
+        for i in range(2):
+            side = jnp.where(2 * z < C, i, 1 - i)
+            t = jnp.where(side == 0, u - z, u - (C - 1 - z))
+            target = jnp.where(side == 0, C - 1 - t, t)
+            inner = jnp.logical_and(z >= 1, z + 1 < C)
+            ahead = jnp.where(side == 0, target > z, target < z)
+            ok = jnp.logical_and(jnp.logical_and(t >= 0, inner), ahead)
+
+            def add(t=t, side=side, target=target):
+                at = blk(target)
                 arrive(ga_r.at[t, side], k_ga + 2 * t + side)
                 ga_s[at, :] = (ga_s[at, :].astype(F32) + ga_r[t, side].astype(F32)).astype(BF16)
                 ga_send(t, side)
 
             pl.when(ok)(add)
 
+    wg_second(3)
+    for k in range(1, S):
+        at = pl.ds(pl.multiple_of(lax.rem(s + k, S) * PB, 64), PB)
+        send(og_x.at[0, at, :], og_r.at[k - 1], k_og + k, plane(k))
     column_sum = jnp.sum(g_nat[...].astype(F32), axis=0, keepdims=True)
     sums[pl.ds(10 + z, 1), :] = column_sum
     pair_lane = lax.broadcasted_iota(jnp.int32, (PB, 128), 1)
@@ -1255,8 +1335,12 @@
     sum_p[s] = sums[...]
     for k in range(1, S):
         send(sum_p.at[s], sum_p.at[s], k_sp + k, plane(k))
-    wg_third(2)
+    settle(old)
+    arrive(out_o.at[other_rows, :], k_out)
+    store(out_o, out_h)
     wg_third(3)
+    for hop in range(1, C):
+        owed.append((like_g, k_wgz + hop, None))
     og_reduce()
     ga_hop(1)
     for u in range(2, C - 1):
@@ -1320,6 +1404,7 @@
     )
     gin_o[own_rows, :] = gin_o[own_rows, :] + inner * inverse
     send(gin_o.at[own_rows, :], gin_o.at[own_rows, :], k_gin, sib)
+    store(gin_o.at[own_rows, :], gin_h.at[own_rows, :])
     def last(own, got, index, to):
         for k in range(1, C):
             arrive(got.at[k - 1], index + k)
@@ -1330,10 +1415,13 @@
 
     last(wg[rows_of(s * C + z), :], wg_zr, k_wgz, gf_o)
     last(og_z[pl.ds(pl.multiple_of(z * DB, 16), DB), :], og_zr, k_ogz, go_o)
+    store(gf_o, gf_h)
+    store(go_o, go_h)
     for j in range(CH):
         same = jnp.logical_and(CH * c + j == z, c_of_z == c)
         arrive(qg_zr.at[j], k_qz + j, jnp.logical_not(same))
     gq_o[...] = qg_zr[...].astype(F32)
+    store(gq_o, gq_h)
     for k in range(1, C):
         arrive(sum_z.at[z_from(k)], k_sz + k)
     total = sum_z[0]
@@ -1343,10 +1431,13 @@
     send(sum_c.at[c], sum_c.at[c], k_sc, sib)
     arrive(sum_c.at[o], k_sc)
     sums_o[...] = sum_c[0] + sum_c[1]
-    arrive(out_o.at[other_rows, :], k_out)
+    store(sums_o, sums_h)
     arrive(gin_o.at[other_rows, :], k_gin)
+    store(gin_o.at[other_rows, :], gin_h.at[other_rows, :])
 
     settle(owed)
+    for copy in stored:
+        copy.wait()
     for j in range(CH):
         same = jnp.logical_and(CH * c + j == z, c_of_z == c)
 
@@ -1372,7 +1463,68 @@
     assert next_sem[0] <= SEMS
 
 
-SEMS = 192
+def unpack_kernel(
+    CH,
+    output,
+    grad_input,
+    gf_h,
+    go_h,
+    gq_h,
+    sums_h,
+    output_o,
+    grad_input_o,
+    query_o,
+    key_o,
+    value_o,
+    out_o,
+    up_o,
+    down_o,
+    gain1_o,
+    bias1_o,
+    b_query_o,
+    b_value_o,
+    b_out_o,
+    gain2_o,
+    bias2_o,
+    b_up_o,
+    b_down_o,
+    gf,
+    go,
+    gq,
+    sums,
+    sem,
+):
+    c = lax.axis_index("tp")
+    FH = up_o.shape[1]
+    D = sums.shape[1]
+    GP = 256
+    pairs = ((output, output_o), (grad_input, grad_input_o))
+    pairs += ((gf_h, gf), (go_h, go), (gq_h, gq), (sums_h, sums))
+    copies = [
+        pltpu.make_async_copy(src, dst, sem.at[i]) for i, (src, dst) in enumerate(pairs)
+    ]
+    for copy in copies:
+        copy.start()
+    for copy in copies[2:]:
+        copy.wait()
+    for i, to in enumerate((key_o, value_o, query_o)):
+        cols = slice(i * GP, (i + 1) * GP)
+        to[...] = ungroup(gq[0, :, cols], gq[1, :, cols])
+    out_o[...] = ungroup(go[:, :GP], go[:, GP : 2 * GP])
+    up_o[...] = gf[:, :FH]
+    down_o[...] = gf[:, FH:]
+    for i, to in enumerate((gain1_o, bias1_o, b_out_o, gain2_o, bias2_o, b_down_o)):
+        to[...] = sums[i, :]
+    for i in range(FH // D):
+        b_up_o[i * D : (i + 1) * D] = sums[6 + 2 * c + i, :]
+    for to, start in ((b_value_o, GP), (b_query_o, 2 * GP)):
+        row = [sums[pl.ds(10 + CH * c + j, 1), start : start + GP] for j in range(CH)]
+        to[...] = ungroup(row[0], row[1])[0, :]
+    for copy in copies[:2]:
+        copy.wait()
+
+
+SEMS = 224
 
 
 def fits(frames, w_query, w_up):
@@ -1427,19 +1579,7 @@
     PB = C * DB
     T = C * R
 
-    def grouped(array):
-        parts = array.reshape(array.shape[:-1] + (CH, G))
-        return jnp.pad(parts, [(0, 0)] * (parts.ndim - 1) + [(0, GP - G)])
-
-    wqkv = jnp.concatenate([grouped(w_key), grouped(w_value), grouped(w_query)], axis=-1)
-    wqkv = wqkv.transpose(1, 0, 2)
-    bias = jnp.concatenate(
-        [jnp.zeros((CH, GP), F32), grouped(b_value), grouped(b_query)], axis=-1
-    )
-    bias = jnp.broadcast_to(bias[:, None, :], (CH, 8, 3 * GP))
-    wf = jnp.concatenate([w_up, w_down.T, grouped(w_out.T).reshape(DB, CH * GP)], axis=1)
-    WF = wf.shape[1]
-    vecs = jnp.stack([ln1_gain, ln1_bias, b_out, ln2_gain, ln2_bias, b_down, b_down, b_down])
+    WF = 2 * FH + CH * GP
     vmem = pl.BlockSpec(memory_space=pltpu.VMEM)
     V = pltpu.VMEM
     dims = (S, C, R, D, GP, HG, FH)
@@ -1447,6 +1587,16 @@
         pltpu.SemaphoreType.DMA((SEMS,)),
         pltpu.SemaphoreType.DMA((SEMS,)),
         pltpu.SemaphoreType.DMA((2 * CH,)),
+        pltpu.SemaphoreType.DMA((7,)),
+        V((R, D), BF16),
+        V((R, D), F32),
+        V((DB, 2 * FH), F32),
+        V((DB, CH * GP), F32),
+        V((CH, DB, 3 * GP), F32),
+        V((16, D), F32),
+        V((CH, DB, 3 * GP), BF16),
+        V((CH, 8, 3 * GP), F32),
+        V((1, FH), F32),
         V((T, D), BF16),
         V((D, C * HF), BF16),
         V((S, 2, CH * DB, 3 * GP), BF16),
@@ -1516,42 +1666,77 @@
     output, grad_input, gf, go, gq, sums = pl.pallas_call(
         functools.partial(layer_kernel, dims),
         out_shape=outs,
-        in_specs=[vmem, vmem, pl.BlockSpec(memory_space=pltpu.SMEM)] + [vmem] * 5,
-        out_specs=[vmem] * 6,
+        in_specs=[vmem, vmem, pl.BlockSpec(memory_space=pltpu.SMEM)] + [vmem] * 15,
+        out_specs=[pl.BlockSpec(memory_space=pltpu.HBM)] * 6,
         scratch_shapes=scratch,
         compiler_params=pltpu.CompilerParams(
             collective_id=0, has_side_effects=True, vmem_limit_bytes=63 << 20
         ),
-    )(frames[0], cotangent[0], lengths, vecs, b_up.reshape(1, FH), wqkv, bias, wf)
-    c = lax.axis_index("tp")
-
-    def ungroup(array, start):
-        part = array[..., start : start + G]
-        return part
-
-    def heads_of(start):
-        return gq[:, :, start : start + G].transpose(1, 0, 2).reshape(DB, CH * G)
-
-    biases = lax.dynamic_slice_in_dim(sums, 10 + CH * c, CH, 0)
-    grad_b_up = lax.dynamic_slice_in_dim(sums, 6 + 2 * c, 2, 0).reshape(FH)
+    )(
+        frames[0],
+        cotangent[0],
+        lengths,
+        ln1_gain,
+        ln1_bias,
+        b_out,
+        ln2_gain,
+        ln2_bias,
+        b_down,
+        b_up,
+        b_query,
+        b_value,
+        w_query,
+        w_key,
+        w_value,
+        w_up,
+        w_down.T,
+        w_out.T,
+    )
+    flat = [D, D, CH * G, CH * G, D, D, D, FH, D]
+    results = pl.pallas_call(
+        functools.partial(unpack_kernel, CH),
+        out_shape=[
+            jax.ShapeDtypeStruct((R, D), BF16),
+            jax.ShapeDtypeStruct((R, D), F32),
+            jax.ShapeDtypeStruct((DB, CH * G), F32),
+            jax.ShapeDtypeStruct((DB, CH * G), F32),
+            jax.ShapeDtypeStruct((DB, CH * G), F32),
+            jax.ShapeDtypeStruct((DB, CH * G), F32),
+            jax.ShapeDtypeStruct((DB, FH), F32),
+            jax.ShapeDtypeStruct((DB, FH), F32),
+        ]
+        + [jax.ShapeDtypeStruct((length,), F32) for length in flat],
+        in_specs=[pl.BlockSpec(memory_space=pltpu.HBM)] * 6,
+        out_specs=[vmem] * 17,
+        scratch_shapes=[
+            V((DB, 2 * FH), F32),
+            V((DB, CH * GP), F32),
+            V((CH, DB, 3 * GP), F32),
+            V((16, D), F32),
+            pltpu.SemaphoreType.DMA((6,)),
+        ],
+        compiler_params=pltpu.CompilerParams(vmem_limit_bytes=63 << 20),
+    )(output, grad_input, gf, go, gq, sums)
+    output, grad_input, g_query, g_key, g_value, g_out, g_up, g_down = results[:8]
+    g1, s1, bq, bv, bo, g2, s2, bu, bd = results[8:]
     return (
         output[None],
         grad_input[None],
-        sums[0],
-        sums[1],
-        heads_of(2 * GP),
-        biases[:, 2 * GP : 2 * GP + G].reshape(CH * G),
-        heads_of(0),
-        heads_of(GP),
-        biases[:, GP : GP + G].reshape(CH * G),
-        go.reshape(DB, CH, GP)[:, :, :G].reshape(DB, CH * G).T,
-        sums[2],
-        sums[3],
-        sums[4],
-        gf[:, :FH],
-        grad_b_up,
-        gf[:, FH:].T,
-        sums[5],
+        g1,
+        s1,
+        g_query,
+        bq,
+        g_key,
+        g_value,
+        bv,
+        g_out.T,
+        bo,
+        g2,
+        s2,
+        g_up,
+        bu,
+        g_down.T,
+        bd,
     )
 
 

time: 202 us -> 180 us (0.89)
  local copies, waits for them, and re-layouts: 18.1 us -> 0 us
  other arithmetic: 2.43 us -> 0 us
    reshape x18 -> x0, local copies, waits for them, and re-layouts: 9.3 us -> none  [the longest x9 3.68 us: grouped(): parts = array.reshape(array.shape[:-1] + (CH, G))]
    pallas_call x1, Pallas kernels: 178 us -> 174 us  [fast_layer(): pl.pallas_call(functools.partial(layer_kernel, dims), out_shape=outs, in_...]
    pallas_call x0 -> x1, Pallas kernels: none -> 3.83 us  [fast_layer(): pl.pallas_call(functools.partial(unpack_kernel, CH), out_shape=[jax.Shape...]
    slice x2 -> x0, local copies, waits for them, and re-layouts: 2.48 us -> none  [the longest x1 1.62 us: fast_layer(): sums[5]]
    transpose x5 -> x0, local copies, waits for them, and re-layouts: 2.16 us -> none  [the longest x4 1.32 us: heads_of(): return gq[:, :, start:start + G].transpose(1, 0, 2).reshape(DB, CH * G)]
    unnamed x29 -> x0, local copies, waits for them, and re-layouts: 2.08 us -> none
where the time goes in v3:
time: 180 us; the launch traced here: 179 us
  Pallas kernels  178 us (99%)
    pallas_call x1, Pallas kernels, fast_layer(): pl.pallas_call(functools.partial(layer_kernel, dims), out_shape=outs, in_...  174 us
    pallas_call x1, Pallas kernels, fast_layer(): pl.pallas_call(functools.partial(unpack_kernel, CH), out_shape=[jax.Shape...  3.83 us

profile of v3, /device:TPU:17, one launch (start us, length us, event | category | flops | bytes accessed | tf_op | source)
XLA Modules:
  0.0 179.3 jit_solution(17614910317310140387)
XLA Ops:
  1.3 174.0 %shard_map.305 = (bf16[512,768]{1,0:T(8,128)(2,1)}, f32[512,768]{1,0:T(8,128)}, f32[48,3072]{1,0:T(8,128)}, f32[48,512]{1,0:T(8,128)}, f32[2,48,768]{2,1,0:T(8,128)}, /*index=5*/f32[16,768]{1,0:T(8,128)}) custom-call(bf16[512,768]{1,0:T(8,128)(2,1)} %bitcast.8, bf16[512,768]{1,0:T(8,128)(2,1)} %bitcast.9, s32[1]{0:T(128)S(6)} %copy.35.lengths, f32[768]{0:T(1024)} %v_gain1.1, ...), custom_call_target="tpu_custom_call" | custom-call | tf_op jit(solution)/shard_map/pallas_call | solution.py:1666
  175.3 3.8 %shard_map.306 = (bf16[512,768]{1,0:T(8,128)(2,1)}, f32[512,768]{1,0:T(8,128)}, f32[48,384]{1,0:T(8,128)}, f32[48,384]{1,0:T(8,128)}, f32[48,384]{1,0:T(8,128)},...) custom-call(bf16[512,768]{1,0:T(8,128)(2,1)} %get-tuple-element.40.o, ...), custom_call_target="tpu_custom_call" | custom-call | tf_op jit(solution)/shard_map/pallas_call | solution.py:1696

commit v4 on v3

--- a/solution.py
+++ b/solution.py
@@ -480,7 +480,6 @@
     v_n,
     q_n,
     q_t,
-    lse,
     att_f,
     att_s,
     att_r,
@@ -511,10 +510,11 @@
     dv_t,
     dq_f,
     dlt,
+    q_s,
+    d_s,
     dkv_s,
     dkv_r,
     ga_r,
-    ga_f,
     qg,
     qg_r,
     qg_p,
@@ -529,7 +529,9 @@
     S, C, R, D, GP, HG, FH = dims
     ga_s = a_all.at[pl.ds(0, C * R // 2), :]
     g_nat = a_all.at[pl.ds(C * R // 2, C * R // 2), :]
-    WF = 2 * FH + C // 2 * GP
+    OC = C // 2 * GP
+    WF = OC + 2 * FH
+    pieces = (slice(0, OC + FH), slice(OC + FH, WF))
     HF = R // 2
     CH = C // 2
     DB = D // (S * C)
@@ -555,7 +557,7 @@
             device_id_type=MESH,
         )
 
-    def send(src, dst, index, device, when=None, like=None):
+    def send(src, dst, index, device, when=None, like=None, owe=None):
         def go():
             remote(src, dst, index, device).start()
 
@@ -563,7 +565,8 @@
             go()
         else:
             pl.when(when)(go)
-        owed.append((src if like is None else like, index, when))
+        if owe is not False:
+            owed.append((src if like is None else like, index, when if owe is None else owe))
 
     def settle(entries):
         for like, index, when in entries:
@@ -624,8 +627,8 @@
     k_q3 = sems(1)
     k_a = sems(2 * C)
     k_as = sems(2 * C)
-    k_f = sems(2 * C)
-    k_fp = sems(6 * 2 * C)
+    k_f = sems(4 * C)
+    k_fp = sems(8 * 2 * C)
     k_wo = sems(1)
     k_att = sems(C)
     k_n2 = sems(1)
@@ -678,12 +681,11 @@
             cols = slice(i * GP, (i + 1) * GP)
             wqkv_own[j, :, cols] = group(part[...].astype(F32), j).astype(BF16)
     mine_rows = rows_of(s * C + z)
-    wf[mine_rows, :FH] = w_up[...]
-    wf[mine_rows, FH : 2 * FH] = w_down[...]
+    wf[mine_rows, OC : OC + FH] = w_up[...]
+    wf[mine_rows, OC + FH :] = w_down[...]
     out_t = w_out[...].astype(F32)
     for j in range(CH):
-        cols = slice(2 * FH + j * GP, 2 * FH + (j + 1) * GP)
-        wf[mine_rows, cols] = group(out_t, j).astype(BF16)
+        wf[mine_rows, j * GP : (j + 1) * GP] = group(out_t, j).astype(BF16)
     for j in range(CH):
         bias_own[j] = jnp.zeros((8, 3 * GP), F32)
         bias_own[j, 0:1, GP : 2 * GP] = group(v_b_value[...].reshape(1, CH * 3 * HD), j)
@@ -749,12 +751,12 @@
 
     goes_right = [jnp.logical_and(can_right, z - t >= 0) for t in range(C - 1)]
     goes_left = [jnp.logical_and(can_left, z + t < C) for t in range(C - 1)]
-    like_f = wf.at[pl.ds(0, DB), :]
-    like_fh = wf.at[pl.ds(0, DB), pl.ds(0, WF // 2)]
+    like_f = [wf.at[pl.ds(0, DB), piece] for piece in pieces]
     like_a = a_all.at[pl.ds(0, HF), :]
 
-    def f_step(t):
-        line_step(lambda block: wf.at[rows_of(s * C + block), :], t, k_f, like_f)
+    def f_step(t, p):
+        view = lambda block: wf.at[rows_of(s * C + block), pieces[p]]
+        line_step(view, t, k_f + 2 * C * p, like_f[p])
 
     def a_step(t):
         line_step(lambda block: a_all.at[half_rows(block, c), :], t, k_a, like_a)
@@ -765,7 +767,11 @@
     def from_right(t):
         return jnp.minimum(z + 1 + t, C - 1), z + 1 + t < C
 
-    halves = (slice(0, WF // 2), slice(WF // 2, WF))
+    halves = []
+    for piece in pieces:
+        middle = (piece.start + piece.stop) // 2
+        halves.append((slice(piece.start, middle), slice(middle, piece.stop)))
+    like_fh = [wf.at[pl.ds(0, DB), half[0]] for half in halves]
 
     def row_of(shard, block):
         return rows_of(shard * C + block)
@@ -774,7 +780,10 @@
         ((2 * t + 2,) + from_left(t), (2 * t + 3,) + from_right(t)) for t in range(C - 1)
     ]
     own_label = ((0, z, None),)
-    wo_cols = slice(2 * FH, 2 * FH + CH * GP)
+    at_end = jnp.logical_or(z == 0, z == C - 1)
+    near_end = jnp.minimum(z, C - 1 - z)
+    inside = jnp.logical_not(at_end)
+    wo_cols = slice(0, OC)
 
     def wo_pass(shard, block, ok):
         def go():
@@ -787,43 +796,45 @@
             pl.when(ok)(go)
 
 
-    def f_plane(labels):
+    def f_plane(labels, p):
         for label, block, ok in labels:
-            index = k_fp + 6 * label
-            for half in range(2):
-                at = wf.at[row_of(s, block), halves[half]]
-                send(at, at, index + half, to_x, ok, like_fh)
-                at = wf.at[row_of(s, block), halves[1 - half]]
-                send(at, at, index + 2 + half, to_y, ok, like_fh)
-            wo_pass(s, block, ok)
-
-    def f_relay(labels):
+            index = k_fp + 8 * label + 4 * p
+            at = wf.at[row_of(s, block), pieces[p]]
+            send(at, at, index, to_x, ok, like_f[p])
+            send(at, at, index + 1, to_y, ok, like_f[p])
+            if p == 0:
+                wo_pass(s, block, ok)
+
+    def f_relay(labels, p, gate=None, owe=True):
         for label, block, ok in labels:
-            index = k_fp + 6 * label
-            at = wf.at[row_of(near_x, block), halves[0]]
-            arrive(at, index, ok)
-            send(at, at, index + 4, to_y, ok, like_fh)
-            at = wf.at[row_of(near_y, block), halves[1]]
-            arrive(at, index + 2, ok)
-            send(at, at, index + 5, to_x, ok, like_fh)
-            wo_pass(near_y, block, ok)
-
-    def f_finish(labels):
+            index = k_fp + 8 * label + 4 * p
+            now = ok if gate is None else jnp.logical_and(ok, gate)
+            arrive(wf.at[row_of(near_x, block), pieces[p]], index, now)
+            at = wf.at[row_of(near_x, block), halves[p][0]]
+            send(at, at, index + 2, to_y, now, like_fh[p], ok if owe else False)
+            arrive(wf.at[row_of(near_y, block), pieces[p]], index + 1, now)
+            at = wf.at[row_of(near_y, block), halves[p][1]]
+            send(at, at, index + 3, to_x, now, like_fh[p], ok if owe else False)
+            if p == 0:
+                wo_pass(near_x, block, now)
+                wo_pass(near_y, block, now)
+
+    def f_finish(labels, p):
         for label, block, ok in labels:
-            index = k_fp + 6 * label
-            arrive(wf.at[row_of(near_x, block), halves[1]], index + 1, ok)
-            wo_pass(near_x, block, ok)
-            arrive(wf.at[row_of(near_y, block), halves[0]], index + 3, ok)
-            arrive(wf.at[row_of(far, block), halves[1]], index + 5, ok)
-            wo_pass(far, block, ok)
-            arrive(wf.at[row_of(far, block), halves[0]], index + 4, ok)
-
-    def f_arrive(t):
+            index = k_fp + 8 * label + 4 * p
+            for i in range(2):
+                arrive(wf.at[row_of(far, block), halves[p][i]], index + 2 + i, ok)
+            if p == 0:
+                wo_pass(far, block, ok)
+
+    def f_arrive(t, p):
         for side, (label, block, ok) in enumerate(labels_of[t]):
-            arrive(wf.at[row_of(s, block), :], k_f + 2 * t + side, ok)
-        f_plane(labels_of[t])
-
-    f_step(0)
+            arrive(wf.at[row_of(s, block), pieces[p]], k_f + 2 * C * p + 2 * t + side, ok)
+        f_plane(labels_of[t], p)
+
+    f_step(0, 0)
+    f_step(0, 1)
+
     def first_norm(i, carry):
         at = pl.ds(pl.multiple_of(i * 64, 64), 64)
         to = pl.ds(pl.multiple_of(z * R + i * 64, 64), 64)
@@ -840,7 +851,8 @@
         arrive(wqkv.at[s, c, pl.ds(i * DB, DB), :], k_q1 + i, jnp.logical_not(same))
     for k in range(1, S):
         send(wqkv.at[s, c], wqkv.at[s, c], k_q2 + k, plane(k))
-    f_plane(own_label)
+    f_plane(own_label, 0)
+    f_plane(own_label, 1)
     key_at = lax.broadcasted_iota(jnp.int32, (GP - LIVE_LANE, C * R), 1)
     first_row = lax.broadcasted_iota(jnp.int32, (GP - LIVE_LANE, C * R), 0) == 0
     dead = jnp.where(jnp.logical_and(first_row, key_at >= length), NEG, 0.0)
@@ -888,17 +900,20 @@
         pl.when(when)(go)
 
     lax.fori_loop(0, 2, project_own, 0)
-    f_arrive(0)
-    f_relay(own_label)
+    f_arrive(0, 0)
+    f_arrive(0, 1)
+    f_relay(own_label, 0)
+    f_relay(own_label, 1)
     for t in range(C - 1):
         if t == C - 2:
-            f_arrive(1)
-            for later in range(2, C - 1):
-                f_step(later)
+            for p in range(2):
+                f_arrive(1, p)
+                f_step(2, p)
         for side, (label, block, ok) in enumerate(labels_of[t]):
             arrive(a_all.at[half_rows(block, c), :], k_a + 2 * t + side, ok)
         if t == C - 3:
-            f_step(1)
+            f_step(1, 0)
+            f_step(1, 1)
         if t + 1 < C - 1:
             a_step(t + 1)
         for side, (label, block, ok) in enumerate(labels_of[t]):
@@ -924,10 +939,13 @@
 
         lax.fori_loop(0, 4, come, 0)
         if t == C - 3:
-            f_relay(labels_of[0])
-    f_relay(labels_of[1])
-    f_finish(own_label)
-    f_finish(labels_of[0])
+            f_relay(labels_of[0], 0)
+            f_relay(labels_of[0], 1)
+    for p in range(2):
+        f_relay(labels_of[1], p, at_end)
+    for p in range(2):
+        f_finish(own_label, p)
+        f_finish(labels_of[0], p)
 
     TQ = 128
 
@@ -936,6 +954,7 @@
             at = pl.ds(pl.multiple_of(block * HF + i * TQ, TQ), TQ)
             queries = q_n[at, :]
             total = jnp.zeros((TQ, GP), F32)
+            log_sums = []
             for h in range(HG):
                 scores = nn(only_head(queries, h, True), k_tr[...])
                 top = jnp.max(scores, axis=-1, keepdims=True)
@@ -943,42 +962,53 @@
                 norm_sum = jnp.sum(weights, axis=-1, keepdims=True)
                 got = nn(weights.astype(BF16), v_n[...]) * (1.0 / norm_sum)
                 total = total + only_head(got, h)
-                lse[at, h : h + 1] = top + jnp.log(norm_sum)
+                log_sums.append(top + jnp.log(norm_sum))
             att_f[at, :] = total
+            for h in range(HG):
+                att_f[at, LIVE_LANE + h : LIVE_LANE + h + 1] = log_sums[h]
             att_s[at, :] = total.astype(BF16)
             return carry
 
         lax.fori_loop(0, HF // TQ, step, 0)
 
     def attend_all(i, carry):
-        block = lax.rem(z + 1 + i, C)
+        inner = jnp.where(i == 0, 2, jnp.where(i == 1, 1, jnp.where(i == 2, 3, 0)))
+        block = jnp.where(near_end == 0, lax.rem(i + 1, C), inner)
+        block = jnp.where(2 * z < C, block, C - 1 - block)
         attend(block)
 
         def give():
-            remote(
-                att_s.at[blk(block), :], att_r.at[blk(z), :], k_att + 1 + i, column(1 + i)
-            ).start()
-
-        def more_weights():
-            for t in range(2, C - 1):
-                f_arrive(t)
-
-        pl.when(i < C - 1)(give)
-        pl.when(i == 1)(more_weights)
+            hop = lax.rem(block + C - z, C)
+            device = (s, block, c)
+            remote(att_s.at[blk(block), :], att_r.at[blk(z), :], k_att + hop, device).start()
+
+        def poll_0():
+            f_arrive(2, 0)
+
+        def poll_1():
+            f_relay(labels_of[1], 0, inside, False)
+
+        def poll_2():
+            f_relay(labels_of[1], 1, inside, False)
+            f_relay(labels_of[2], 0)
+            f_arrive(2, 1)
+
+        pl.when(block != z)(give)
+        pl.when(i == 0)(poll_0)
+        pl.when(i == 1)(poll_1)
+        pl.when(i == 2)(poll_2)
         return carry
 
     lax.fori_loop(0, C, attend_all, 0)
     att_r[blk(z), :] = att_s[blk(z), :]
 
-    f_finish(labels_of[1])
-    for t in range(2, C - 1):
-        f_relay(labels_of[t])
-    for t in range(2, C - 1):
-        f_finish(labels_of[t])
+    f_finish(labels_of[1], 0)
+    f_finish(labels_of[2], 0)
     owed.append((wo_sib, k_wo, None))
     for k in range(1, C):
         arrive(att_r.at[blk(z_from(k)), :], k_att + k)
         remote(att_s.at[blk(z), :], att_r.at[blk(z), :], k_att + k, column(k)).wait_send()
+    f_relay(labels_of[2], 1)
     arrive(wo_sib, k_wo)
 
     settle([entry for entry in owed if entry[0] is like_a])
@@ -988,7 +1018,7 @@
     hidden = frames[own_rows, :].astype(F32) + b_out
     for j in range(CH):
         hidden = hidden + nt(
-            att_r[blk(CH * c + j), :], wf[:, 2 * FH + j * GP : 2 * FH + (j + 1) * GP]
+            att_r[blk(CH * c + j), :], wf[:, j * GP : (j + 1) * GP]
         )
         hidden = hidden + nt(att_r[blk(CH * o + j), :], wo_sib[:, j * GP : (j + 1) * GP])
     hid[...] = hidden
@@ -1000,14 +1030,17 @@
     arrive(z_all.at[other_rows, :], k_n2)
     z_t[:, other_rows] = flip(z_all[other_rows, :])
 
+    f_finish(labels_of[1], 1)
+    f_finish(labels_of[2], 1)
     TF = 256
 
     up_bias[...] = v_b_up[...].reshape(1, FH)
 
     def units(i, carry):
         cols = pl.ds(pl.multiple_of(i * TF, TF), TF)
-        down = pl.ds(pl.multiple_of(FH + i * TF, TF), TF)
-        upper = nn(z_all[...], wf[:, cols]) + up_bias[:, cols]
+        down = pl.ds(pl.multiple_of(OC + FH + i * TF, TF), TF)
+        ups = pl.ds(pl.multiple_of(OC + i * TF, TF), TF)
+        upper = nn(z_all[...], wf[:, ups]) + up_bias[:, cols]
         cumulative = 0.5 * (1.0 + lax.erf(upper * INV_ROOT_TWO))
         act[:, cols] = (upper * cumulative).astype(BF16)
         slope = cumulative + upper * jnp.exp(-0.5 * upper * upper) * INV_ROOT_TAU
@@ -1019,7 +1052,7 @@
 
     def z_grad(i, carry):
         at = pl.ds(pl.multiple_of(i * 256, 256), 256)
-        gz_s[:, at] = nt(gup[other_rows, :], wf[at, :FH]).astype(BF16)
+        gz_s[:, at] = nt(gup[other_rows, :], wf[at, OC : OC + FH]).astype(BF16)
         return carry
 
     lax.fori_loop(0, D // 256, z_grad, 0)
@@ -1034,7 +1067,6 @@
 
     lax.fori_loop(0, FH // TF, unit_grads, 0)
 
-    near_end = jnp.minimum(z, C - 1 - z)
     part_order = ((3, 3), (2, 0), (1, 2), (0, 1))
 
     def part_z(j):
@@ -1107,7 +1139,7 @@
     wg_far(1)
 
     gz_rows = jnp.concatenate(
-        [nt(gup[own_rows, :], wf[i * 256 : (i + 1) * 256, :FH]) for i in range(D // 256)], axis=1
+        [nt(gup[own_rows, :], wf[i * 256 : (i + 1) * 256, OC : OC + FH]) for i in range(D // 256)], axis=1
     )
     arrive(gz_r, k_gz)
     grad_z = gz_rows + gz_r[...].astype(F32)
@@ -1129,7 +1161,7 @@
     sums[2:3, :] = jnp.sum(low.astype(F32), axis=0, keepdims=True)
     for j in range(CH):
         att_s[blk(CH * c + j), :] = nn(
-            low, wf[:, 2 * FH + j * GP : 2 * FH + (j + 1) * GP]
+            low, wf[:, j * GP : (j + 1) * GP]
         ).astype(BF16)
         att_s[blk(CH * o + j), :] = nn(low, wo_sib[:, j * GP : (j + 1) * GP]).astype(BF16)
     for k in range(1, C):
@@ -1138,7 +1170,7 @@
     ghl_t[...] = flip(low)
     def down_part(i, carry):
         at = pl.ds(pl.multiple_of(i * 256, 256), 256)
-        part_s[:, at] = nt(act[other_rows, :], wf[at, FH : 2 * FH]).astype(BF16)
+        part_s[:, at] = nt(act[other_rows, :], wf[at, OC + FH :]).astype(BF16)
         return carry
 
     lax.fori_loop(0, D // 256, down_part, 0)
@@ -1166,30 +1198,36 @@
             pl.when(b > 0)(come)
             gatt_t[...] = flip(gatt_r[at, :])
             product = gatt_r[at, :].astype(F32) * att_f[at, :]
-            deltas = [
-                jnp.sum(only_head(product, h), axis=-1, keepdims=True) for h in range(HG)
-            ]
             for h in range(HG):
-                dlt[:, h : h + 1] = deltas[h]
+                rows = slice(h * HF, (h + 1) * HF)
+                dlt[rows, 0:1] = jnp.sum(only_head(product, h), axis=-1, keepdims=True)
+                dlt[rows, 1:2] = att_f[at, LIVE_LANE + h : LIVE_LANE + h + 1]
+                q_s[rows, :] = only_head(q_n[at, :], h, True)
+                d_s[rows, :] = only_head(gatt_r[at, :], h)
             dq_f[...] = jnp.zeros_like(dq_f)
 
             def step(i, carry):
                 keys = pl.ds(pl.multiple_of(i * TK, TK), TK)
+                weights = jnp.exp(nn(q_s[...], k_tr[:, keys]) - dlt[:, 1:2])
+                grads = nn(d_s[...], v_tr[:, keys])
+                grad_scores = (weights * (grads - dlt[:, 0:1])).astype(BF16)
+                weights = weights.astype(BF16)
                 for h in range(HG):
                     head = slice(HD * h, HD * (h + 1))
-                    scores = nn(only_head(q_n[at, :], h, True), k_tr[:, keys])
-                    weights = jnp.exp(scores - lse[at, h : h + 1])
-                    grads = nn(only_head(gatt_r[at, :], h), v_tr[:, keys])
-                    grad_scores = (weights * (grads - dlt[:, h : h + 1])).astype(BF16)
-                    dv_t[head, keys] += nn(gatt_t[head, :], weights.astype(BF16))
-                    dk_t[head, keys] += nn(q_t[head, at], grad_scores)
-                    dq_f[...] += only_head(nn(grad_scores, k_n[keys, :]), h)
+                    rows = slice(h * HF, (h + 1) * HF)
+                    dv_t[head, keys] += nn(gatt_t[head, :], weights[rows, :])
+                    dk_t[head, keys] += nn(q_t[head, at], grad_scores[rows, :])
+                dq_f[...] += nn(grad_scores, k_n[keys, :])
                 for number, poll in polls:
                     pl.when(b * steps + i == number)(poll)
                 return carry
 
             lax.fori_loop(0, steps, step, 0)
-            g_nat[at, 2 * GP :] = (dq_f[...] * (HD**-0.5)).astype(BF16)
+            for h in range(HG):
+                rows = slice(h * HF, (h + 1) * HF)
+                part = only_head(dq_f[rows, :], h)
+                total = part if h == 0 else total + part
+            g_nat[at, 2 * GP :] = (total * (HD**-0.5)).astype(BF16)
             return carry
 
         lax.fori_loop(0, C, block_step, 0)
@@ -1221,7 +1259,7 @@
         wg_near(3)
 
     down_rows = jnp.concatenate(
-        [nt(act[own_rows, :], wf[i * 256 : (i + 1) * 256, FH : 2 * FH]) for i in range(D // 256)],
+        [nt(act[own_rows, :], wf[i * 256 : (i + 1) * 256, OC + FH :]) for i in range(D // 256)],
         axis=1,
     )
     arrive(part_r, k_part)
@@ -1307,9 +1345,6 @@
             pl.when(ok)(add)
 
     wg_second(3)
-    for k in range(1, S):
-        at = pl.ds(pl.multiple_of(lax.rem(s + k, S) * PB, 64), PB)
-        send(og_x.at[0, at, :], og_r.at[k - 1], k_og + k, plane(k))
     column_sum = jnp.sum(g_nat[...].astype(F32), axis=0, keepdims=True)
     sums[pl.ds(10 + z, 1), :] = column_sum
     pair_lane = lax.broadcasted_iota(jnp.int32, (PB, 128), 1)
@@ -1326,25 +1361,20 @@
     turned = pairs[...].T
     sums[0:1, :] = (turned[0:1, :] - ln1_bias * turned[1:2, :]) / ln1_gain
     sums[1:2, :] = turned[1:2, :]
+    sum_p[s] = sums[...]
+    for k in range(1, S):
+        send(sum_p.at[s], sum_p.at[s], k_sp + k, plane(k))
+    for k in range(1, S):
+        at = pl.ds(pl.multiple_of(lax.rem(s + k, S) * PB, 64), PB)
+        send(og_x.at[0, at, :], og_r.at[k - 1], k_og + k, plane(k))
     arrive(qg_r, k_qx)
     for i in range(S):
         qg_r[i] = (qg_r[i].astype(F32) + qg[i, c].astype(F32)).astype(BF16)
     for k in range(1, S):
         send(qg_r.at[lax.rem(s + k, S)], qg_p.at[k - 1], k_qp + k, plane(k))
-
-    sum_p[s] = sums[...]
-    for k in range(1, S):
-        send(sum_p.at[s], sum_p.at[s], k_sp + k, plane(k))
     settle(old)
     arrive(out_o.at[other_rows, :], k_out)
     store(out_o, out_h)
-    wg_third(3)
-    for hop in range(1, C):
-        owed.append((like_g, k_wgz + hop, None))
-    og_reduce()
-    ga_hop(1)
-    for u in range(2, C - 1):
-        ga_hop(u)
     for k in range(1, S):
         arrive(sum_p.at[s_from(k)], k_sp + k)
     total = sum_p[0]
@@ -1353,6 +1383,13 @@
     sum_z[z] = total
     for k in range(1, C):
         send(sum_z.at[z], sum_z.at[z], k_sz + k, column(k))
+    wg_third(3)
+    for hop in range(1, C):
+        owed.append((like_g, k_wgz + hop, None))
+    ga_hop(1)
+    og_reduce()
+    for u in range(2, C - 1):
+        ga_hop(u)
     for k in range(1, S):
         arrive(qg_p.at[k - 1], k_qp + k)
     total = qg_r[s].astype(F32)
@@ -1382,8 +1419,15 @@
 
         pl.when(same)(keep)
 
+    for k in range(1, C):
+        arrive(sum_z.at[z_from(k)], k_sz + k)
+    total = sum_z[0]
+    for k in range(1, C):
+        total = total + sum_z[k]
+    sum_c[c] = total
+    send(sum_c.at[c], sum_c.at[c], k_sc, sib)
     own_block = blk(z)
-    ga_f[...] = ga_s[own_block, :].astype(F32)
+    hid[...] = ga_s[own_block, :].astype(F32)
     for t in range(C - 1):
         for side in range(2):
             target = C - 1 - t if side == 0 else t
@@ -1391,10 +1435,10 @@
 
             def add(t=t, side=side):
                 arrive(ga_r.at[t, side], k_ga + 2 * t + side)
-                ga_f[...] += ga_r[t, side].astype(F32)
+                hid[...] += ga_r[t, side].astype(F32)
 
             pl.when(jnp.logical_and(target == z, behind))(add)
-    grad_a = ga_f[...]
+    grad_a = hid[...]
     normed, inverse = norm(frames[own_rows, :].astype(F32))
     scaled = grad_a * ln1_gain
     inner = (
@@ -1422,13 +1466,6 @@
         arrive(qg_zr.at[j], k_qz + j, jnp.logical_not(same))
     gq_o[...] = qg_zr[...].astype(F32)
     store(gq_o, gq_h)
-    for k in range(1, C):
-        arrive(sum_z.at[z_from(k)], k_sz + k)
-    total = sum_z[0]
-    for k in range(1, C):
-        total = total + sum_z[k]
-    sum_c[c] = total
-    send(sum_c.at[c], sum_c.at[c], k_sc, sib)
     arrive(sum_c.at[o], k_sc)
     sums_o[...] = sum_c[0] + sum_c[1]
     store(sums_o, sums_h)
@@ -1524,7 +1561,7 @@
         copy.wait()
 
 
-SEMS = 224
+SEMS = 256
 
 
 def fits(frames, w_query, w_up):
@@ -1609,7 +1646,6 @@
         V((T, GP), BF16),
         V((C * HF, GP), BF16),
         V((GP, C * HF), BF16),
-        V((C * HF, 8), F32),
         V((C * HF, GP), F32),
         V((C * HF, GP), BF16),
         V((C * HF, GP), BF16),
@@ -1638,12 +1674,13 @@
         V((C - 1, DB, CH * GP), BF16),
         V((G, T), F32),
         V((G, T), F32),
-        V((HF, GP), F32),
-        V((HF, 8), F32),
+        V((3 * HF, GP), F32),
+        V((3 * HF, 8), F32),
+        V((3 * HF, GP), BF16),
+        V((3 * HF, GP), BF16),
         V((C, 2, G, HF), BF16),
         V((C, 2, G, HF), BF16),
         V((C - 1, 2, HF, D), BF16),
-        V((HF, D), F32),
         V((S, 2, CH * DB, 3 * GP), BF16),
         V((S, CH * DB, 3 * GP), BF16),
         V((S - 1, CH * DB, 3 * GP), BF16),

time: 180 us -> 174 us (0.967)
  Pallas kernels: 178 us -> 172 us
    pallas_call x1, Pallas kernels: 174 us -> 168 us  [fast_layer(): pl.pallas_call(functools.partial(layer_kernel, dims), out_shape=outs, in_...]
where the time goes in v4:
time: 174 us
  Pallas kernels  172 us (99%)
    pallas_call x1, Pallas kernels, fast_layer(): pl.pallas_call(functools.partial(layer_kernel, dims), out_shape=outs, in_...  168 us
    pallas_call x1, Pallas kernels, fast_layer(): pl.pallas_call(functools.partial(unpack_kernel, CH), out_shape=[jax.Shape...  3.83 us

profile of v4, /device:TPU:17, one launch (start us, length us, event | category | flops | bytes accessed | tf_op | source)
XLA Modules:
  0.0 173.6 jit_solution(9815132230153186163)
XLA Ops:
  1.3 168.3 %shard_map.305 = (bf16[512,768]{1,0:T(8,128)(2,1)}, f32[512,768]{1,0:T(8,128)}, f32[48,3072]{1,0:T(8,128)}, f32[48,512]{1,0:T(8,128)}, f32[2,48,768]{2,1,0:T(8,128)}, /*index=5*/f32[16,768]{1,0:T(8,128)}) custom-call(bf16[512,768]{1,0:T(8,128)(2,1)} %bitcast.8, bf16[512,768]{1,0:T(8,128)(2,1)} %bitcast.9, s32[1]{0:T(128)S(6)} %copy.35.lengths, f32[768]{0:T(1024)} %v_gain1.1, ...), custom_call_target="tpu_custom_call" | custom-call | tf_op jit(solution)/shard_map/pallas_call | solution.py:1703
  169.6 3.8 %shard_map.306 = (bf16[512,768]{1,0:T(8,128)(2,1)}, f32[512,768]{1,0:T(8,128)}, f32[48,384]{1,0:T(8,128)}, f32[48,384]{1,0:T(8,128)}, f32[48,384]{1,0:T(8,128)},...) custom-call(bf16[512,768]{1,0:T(8,128)(2,1)} %get-tuple-element.40.o, ...), custom_call_target="tpu_custom_call" | custom-call | tf_op jit(solution)/shard_map/pallas_call | solution.py:1733

commit v5 on v4

--- a/solution.py
+++ b/solution.py
@@ -1032,7 +1032,7 @@
 
     f_finish(labels_of[1], 1)
     f_finish(labels_of[2], 1)
-    TF = 256
+    TF, TG = 512, 512
 
     up_bias[...] = v_b_up[...].reshape(1, FH)
 
@@ -1050,22 +1050,14 @@
 
     lax.fori_loop(0, FH // TF, units, 0)
 
-    def z_grad(i, carry):
-        at = pl.ds(pl.multiple_of(i * 256, 256), 256)
-        gz_s[:, at] = nt(gup[other_rows, :], wf[at, OC : OC + FH]).astype(BF16)
-        return carry
-
-    lax.fori_loop(0, D // 256, z_grad, 0)
-    send(gz_s, gz_r, k_gz, sib)
-
     def unit_grads(i, carry):
-        cols = pl.ds(pl.multiple_of(i * TF, TF), TF)
-        down = pl.ds(pl.multiple_of(FH + i * TF, TF), TF)
+        cols = pl.ds(pl.multiple_of(i * TG, TG), TG)
+        down = pl.ds(pl.multiple_of(FH + i * TG, TG), TG)
         wg[:, cols] = nn(z_t[...], gup[:, cols]).astype(BF16)
         wg[:, down] = nn(g_t[...], act[:, cols]).astype(BF16)
         return carry
 
-    lax.fori_loop(0, FH // TF, unit_grads, 0)
+    lax.fori_loop(0, FH // TG, unit_grads, 0)
 
     part_order = ((3, 3), (2, 0), (1, 2), (0, 1))
 
@@ -1137,6 +1129,14 @@
     wg_far(0)
     wg_near(0)
     wg_far(1)
+
+    def z_grad(i, carry):
+        at = pl.ds(pl.multiple_of(i * 256, 256), 256)
+        gz_s[:, at] = nt(gup[other_rows, :], wf[at, OC : OC + FH]).astype(BF16)
+        return carry
+
+    lax.fori_loop(0, D // 256, z_grad, 0)
+    send(gz_s, gz_r, k_gz, sib)
 
     gz_rows = jnp.concatenate(
         [nt(gup[own_rows, :], wf[i * 256 : (i + 1) * 256, OC : OC + FH]) for i in range(D // 256)], axis=1
@@ -1561,7 +1561,7 @@
         copy.wait()
 
 
-SEMS = 256
+SEMS = 180
 
 
 def fits(frames, w_query, w_up):

time: 174 us -> 170 us (0.977)
  Pallas kernels: 172 us -> 168 us
    pallas_call x1, Pallas kernels: 168 us -> 164 us  [fast_layer(): pl.pallas_call(functools.partial(layer_kernel, dims), out_shape=outs, in_...]
where the time goes in v5:
time: 170 us
  Pallas kernels  168 us (99%)
    pallas_call x1, Pallas kernels, fast_layer(): pl.pallas_call(functools.partial(layer_kernel, dims), out_shape=outs, in_...  164 us
    pallas_call x1, Pallas kernels, fast_layer(): pl.pallas_call(functools.partial(unpack_kernel, CH), out_shape=[jax.Shape...  3.83 us

profile of v5, /device:TPU:17, one launch (start us, length us, event | category | flops | bytes accessed | tf_op | source)
XLA Modules:
  0.0 169.5 jit_solution(17451539553152103445)
XLA Ops:
  1.3 164.2 %shard_map.305 = (bf16[512,768]{1,0:T(8,128)(2,1)}, f32[512,768]{1,0:T(8,128)}, f32[48,3072]{1,0:T(8,128)}, f32[48,512]{1,0:T(8,128)}, f32[2,48,768]{2,1,0:T(8,128)}, /*index=5*/f32[16,768]{1,0:T(8,128)}) custom-call(bf16[512,768]{1,0:T(8,128)(2,1)} %bitcast.8, bf16[512,768]{1,0:T(8,128)(2,1)} %bitcast.9, s32[1]{0:T(128)S(6)} %copy.35.lengths, f32[768]{0:T(1024)} %v_gain1.1, ...), custom_call_target="tpu_custom_call" | custom-call | tf_op jit(solution)/shard_map/pallas_call | solution.py:1703
  165.5 3.8 %shard_map.306 = (bf16[512,768]{1,0:T(8,128)(2,1)}, f32[512,768]{1,0:T(8,128)}, f32[48,384]{1,0:T(8,128)}, f32[48,384]{1,0:T(8,128)}, f32[48,384]{1,0:T(8,128)},...) custom-call(bf16[512,768]{1,0:T(8,128)(2,1)} %get-tuple-element.40.o, ...), custom_call_target="tpu_custom_call" | custom-call | tf_op jit(solution)/shard_map/pallas_call | solution.py:1733

commit v6 on v5

--- a/solution.py
+++ b/solution.py
@@ -547,19 +547,19 @@
         next_sem[0] = base + count
         return base
 
-    def remote(src, dst, index, device):
+    def remote(src, dst, index, device, sent=None):
         return pltpu.make_async_remote_copy(
             src_ref=src,
             dst_ref=dst,
-            send_sem=ss.at[index],
+            send_sem=ss.at[index if sent is None else sent],
             recv_sem=rs.at[index],
             device_id=device,
             device_id_type=MESH,
         )
 
-    def send(src, dst, index, device, when=None, like=None, owe=None):
+    def send(src, dst, index, device, when=None, like=None, owe=None, sent=None):
         def go():
-            remote(src, dst, index, device).start()
+            remote(src, dst, index, device, sent).start()
 
         if when is None:
             go()
@@ -588,7 +588,7 @@
 
     def arrive(dst, index, when=None):
         def go():
-            remote(dst, dst, index, sib).wait_recv()
+            remote(dst, dst, index, sib, 0).wait_recv()
 
         if when is None:
             go()
@@ -623,33 +623,35 @@
 
     k_bias = sems(1)
     k_q1 = sems(CH)
-    k_q2 = sems(S)
+    k_q2 = sems(S - 1) - 1
     k_q3 = sems(1)
-    k_a = sems(2 * C)
-    k_as = sems(2 * C)
-    k_f = sems(4 * C)
-    k_fp = sems(8 * 2 * C)
+    k_a = sems(2 * (C - 1))
+    k_as = sems(2 * (C - 1))
+    k_f = sems(4 * (C - 1))
+    k_fs = sems(1)
+    k_gs = sems(1)
     k_wo = sems(1)
-    k_att = sems(C)
+    k_att = sems(C - 1) - 1
     k_n2 = sems(1)
     k_part = sems(1)
     k_gz = sems(1)
     k_out = sems(1)
-    k_gatt = sems(C)
-    k_wg = sems(6 * C)
-    k_wgz = sems(C)
+    k_gatt = sems(C - 1) - 1
+    k_wgz = sems(C - 1) - 1
     k_ox = sems(1)
-    k_og = sems(S)
-    k_ogz = sems(C)
+    k_og = sems(S - 1) - 1
+    k_ogz = sems(C - 1) - 1
     k_dkv = sems(1)
-    k_ga = sems(2 * C)
+    k_ga = sems(2 * (C - 1))
     k_qx = sems(1)
-    k_qp = sems(S)
+    k_qp = sems(S - 1) - 1
     k_qz = sems(CH)
     k_gin = sems(1)
-    k_sp = sems(S)
-    k_sz = sems(C)
+    k_sp = sems(S - 1) - 1
+    k_sz = sems(C - 1) - 1
     k_sc = sems(1)
+    k_fp = sems(8 * (2 * C - 1))
+    k_wg = sems(6 * C)
 
     barrier = pltpu.get_barrier_semaphore()
     friends = [sib]
@@ -756,7 +758,7 @@
 
     def f_step(t, p):
         view = lambda block: wf.at[rows_of(s * C + block), pieces[p]]
-        line_step(view, t, k_f + 2 * C * p, like_f[p])
+        line_step(view, t, k_f + 2 * (C - 1) * p, like_f[p])
 
     def a_step(t):
         line_step(lambda block: a_all.at[half_rows(block, c), :], t, k_a, like_a)
@@ -771,13 +773,12 @@
     for piece in pieces:
         middle = (piece.start + piece.stop) // 2
         halves.append((slice(piece.start, middle), slice(middle, piece.stop)))
-    like_fh = [wf.at[pl.ds(0, DB), half[0]] for half in halves]
 
     def row_of(shard, block):
         return rows_of(shard * C + block)
 
     labels_of = [
-        ((2 * t + 2,) + from_left(t), (2 * t + 3,) + from_right(t)) for t in range(C - 1)
+        ((2 * t + 1,) + from_left(t), (2 * t + 2,) + from_right(t)) for t in range(C - 1)
     ]
     own_label = ((0, z, None),)
     at_end = jnp.logical_or(z == 0, z == C - 1)
@@ -800,21 +801,21 @@
         for label, block, ok in labels:
             index = k_fp + 8 * label + 4 * p
             at = wf.at[row_of(s, block), pieces[p]]
-            send(at, at, index, to_x, ok, like_f[p])
-            send(at, at, index + 1, to_y, ok, like_f[p])
+            send(at, at, index, to_x, ok, None, False, k_fs)
+            send(at, at, index + 1, to_y, ok, None, False, k_fs)
             if p == 0:
                 wo_pass(s, block, ok)
 
-    def f_relay(labels, p, gate=None, owe=True):
+    def f_relay(labels, p, gate=None):
         for label, block, ok in labels:
             index = k_fp + 8 * label + 4 * p
             now = ok if gate is None else jnp.logical_and(ok, gate)
             arrive(wf.at[row_of(near_x, block), pieces[p]], index, now)
             at = wf.at[row_of(near_x, block), halves[p][0]]
-            send(at, at, index + 2, to_y, now, like_fh[p], ok if owe else False)
+            send(at, at, index + 2, to_y, now, None, False, k_fs)
             arrive(wf.at[row_of(near_y, block), pieces[p]], index + 1, now)
             at = wf.at[row_of(near_y, block), halves[p][1]]
-            send(at, at, index + 3, to_x, now, like_fh[p], ok if owe else False)
+            send(at, at, index + 3, to_x, now, None, False, k_fs)
             if p == 0:
                 wo_pass(near_x, block, now)
                 wo_pass(near_y, block, now)
@@ -829,7 +830,7 @@
 
     def f_arrive(t, p):
         for side, (label, block, ok) in enumerate(labels_of[t]):
-            arrive(wf.at[row_of(s, block), pieces[p]], k_f + 2 * C * p + 2 * t + side, ok)
+            arrive(wf.at[row_of(s, block), pieces[p]], k_f + 2 * (C - 1) * p + 2 * t + side, ok)
         f_plane(labels_of[t], p)
 
     f_step(0, 0)
@@ -986,10 +987,10 @@
             f_arrive(2, 0)
 
         def poll_1():
-            f_relay(labels_of[1], 0, inside, False)
+            f_relay(labels_of[1], 0, inside)
 
         def poll_2():
-            f_relay(labels_of[1], 1, inside, False)
+            f_relay(labels_of[1], 1, inside)
             f_relay(labels_of[2], 0)
             f_arrive(2, 1)
 
@@ -1005,6 +1006,7 @@
     f_finish(labels_of[1], 0)
     f_finish(labels_of[2], 0)
     owed.append((wo_sib, k_wo, None))
+    owed.append((wf.at[pl.ds(0, 3 * C * DB), :], k_fs, None))
     for k in range(1, C):
         arrive(att_r.at[blk(z_from(k)), :], k_att + k)
         remote(att_s.at[blk(z), :], att_r.at[blk(z), :], k_att + k, column(k)).wait_send()
@@ -1069,22 +1071,20 @@
         return pl.ds(pl.multiple_of(part_z(j) * DB, 16), DB)
 
     part_a, part_b = slice(0, FH), slice(FH, 2 * FH)
-    like_g = wg.at[pl.ds(0, DB), :]
-    like_gh = wg.at[pl.ds(0, DB), pl.ds(0, FH)]
 
     def wg_far(j):
         index = k_wg + 6 * j
         own_z = part_z(j)
-        send(wg.at[row_of(far, own_z), part_a], wg_t.at[j, 0], index, to_x, like=like_gh)
-        send(wg.at[row_of(far, own_z), part_b], wg_t.at[j, 1], index + 1, to_y, like=like_gh)
+        send(wg.at[row_of(far, own_z), part_a], wg_t.at[j, 0], index, to_x, owe=False, sent=k_gs)
+        send(wg.at[row_of(far, own_z), part_b], wg_t.at[j, 1], index + 1, to_y, owe=False, sent=k_gs)
 
     def wg_near(j):
         index = k_wg + 6 * j
         own_z = part_z(j)
         near = wg.at[row_of(near_x, own_z), part_a]
-        send(near, wg_x.at[part_rows(j), part_a], index + 2, to_x, like=like_gh)
+        send(near, wg_x.at[part_rows(j), part_a], index + 2, to_x, owe=False, sent=k_gs)
         near = wg.at[row_of(near_y, own_z), part_b]
-        send(near, wg_y.at[part_rows(j), part_b], index + 3, to_y, like=like_gh)
+        send(near, wg_y.at[part_rows(j), part_b], index + 3, to_y, owe=False, sent=k_gs)
 
     def add_into(at, cols, others):
         def step(i, carry):
@@ -1105,12 +1105,12 @@
         at = row_of(near_y, own_z)
         add_into(at, part_a, [(wg_t.at[j, 0], slice(None), 0)])
         near = wg.at[at, part_a]
-        send(near, wg_y.at[part_rows(j), part_a], index + 4, to_y, like=like_gh)
+        send(near, wg_y.at[part_rows(j), part_a], index + 4, to_y, owe=False, sent=k_gs)
         arrive(wg_t.at[j, 1], index + 1)
         at = row_of(near_x, own_z)
         add_into(at, part_b, [(wg_t.at[j, 1], slice(None), 0)])
         near = wg.at[at, part_b]
-        send(near, wg_x.at[part_rows(j), part_b], index + 5, to_x, like=like_gh)
+        send(near, wg_x.at[part_rows(j), part_b], index + 5, to_x, owe=False, sent=k_gs)
 
     def wg_third(j):
         index = k_wg + 6 * j
@@ -1124,7 +1124,8 @@
         )
         if j < C - 1:
             hop = lax.rem(part_z(j) + C - z, C)
-            remote(wg.at[at, :], wg_zr.at[hop - 1], k_wgz + hop, (s, part_z(j), c)).start()
+            device = (s, part_z(j), c)
+            remote(wg.at[at, :], wg_zr.at[hop - 1], k_wgz + hop, device, k_gs).start()
 
     wg_far(0)
     wg_near(0)
@@ -1384,8 +1385,7 @@
     for k in range(1, C):
         send(sum_z.at[z], sum_z.at[z], k_sz + k, column(k))
     wg_third(3)
-    for hop in range(1, C):
-        owed.append((like_g, k_wgz + hop, None))
+    owed.append((wg.at[pl.ds(0, (4 * C - 1) * DB), :], k_gs, None))
     ga_hop(1)
     og_reduce()
     for u in range(2, C - 1):
@@ -1497,7 +1497,7 @@
             ).wait_send()
 
         pl.when(jnp.logical_not(same))(done_weights)
-    assert next_sem[0] <= SEMS
+    assert (next_sem[0], k_fp) == (SEMS, SENDS)
 
 
 def unpack_kernel(
@@ -1561,7 +1561,7 @@
         copy.wait()
 
 
-SEMS = 180
+SEMS, SENDS = 155, 75
 
 
 def fits(frames, w_query, w_up):
@@ -1621,7 +1621,7 @@
     V = pltpu.VMEM
     dims = (S, C, R, D, GP, HG, FH)
     scratch = [
-        pltpu.SemaphoreType.DMA((SEMS,)),
+        pltpu.SemaphoreType.DMA((SENDS,)),
         pltpu.SemaphoreType.DMA((SEMS,)),
         pltpu.SemaphoreType.DMA((2 * CH,)),
         pltpu.SemaphoreType.DMA((7,)),

time: 170 us -> 169 us (level)
  no operation moved by 1% of the time
where the time goes in v6:
time: 169 us; the launch traced here: 168 us
  Pallas kernels  167 us (99%)
    pallas_call x1, Pallas kernels, fast_layer(): pl.pallas_call(functools.partial(layer_kernel, dims), out_shape=outs, in_...  163 us
    pallas_call x1, Pallas kernels, fast_layer(): pl.pallas_call(functools.partial(unpack_kernel, CH), out_shape=[jax.Shape...  3.83 us

profile of v6, /device:TPU:17, one launch (start us, length us, event | category | flops | bytes accessed | tf_op | source)
XLA Modules:
  0.0 168.5 jit_solution(13198797960906750197)
XLA Ops:
  1.3 163.1 %shard_map.305 = (bf16[512,768]{1,0:T(8,128)(2,1)}, f32[512,768]{1,0:T(8,128)}, f32[48,3072]{1,0:T(8,128)}, f32[48,512]{1,0:T(8,128)}, f32[2,48,768]{2,1,0:T(8,128)}, /*index=5*/f32[16,768]{1,0:T(8,128)}) custom-call(bf16[512,768]{1,0:T(8,128)(2,1)} %bitcast.8, bf16[512,768]{1,0:T(8,128)(2,1)} %bitcast.9, s32[1]{0:T(128)S(6)} %copy.35.lengths, f32[768]{0:T(1024)} %v_gain1.1, ...), custom_call_target="tpu_custom_call" | custom-call | tf_op jit(solution)/shard_map/pallas_call | solution.py:1703
  164.5 3.8 %shard_map.306 = (bf16[512,768]{1,0:T(8,128)(2,1)}, f32[512,768]{1,0:T(8,128)}, f32[48,384]{1,0:T(8,128)}, f32[48,384]{1,0:T(8,128)}, f32[48,384]{1,0:T(8,128)},...) custom-call(bf16[512,768]{1,0:T(8,128)(2,1)} %get-tuple-element.40.o, ...), custom_call_target="tpu_custom_call" | custom-call | tf_op jit(solution)/shard_map/pallas_call | solution.py:1733

commit v7 on v6

--- a/solution.py
+++ b/solution.py
@@ -1365,14 +1365,14 @@
     sum_p[s] = sums[...]
     for k in range(1, S):
         send(sum_p.at[s], sum_p.at[s], k_sp + k, plane(k))
-    for k in range(1, S):
-        at = pl.ds(pl.multiple_of(lax.rem(s + k, S) * PB, 64), PB)
-        send(og_x.at[0, at, :], og_r.at[k - 1], k_og + k, plane(k))
     arrive(qg_r, k_qx)
     for i in range(S):
         qg_r[i] = (qg_r[i].astype(F32) + qg[i, c].astype(F32)).astype(BF16)
     for k in range(1, S):
         send(qg_r.at[lax.rem(s + k, S)], qg_p.at[k - 1], k_qp + k, plane(k))
+    for k in range(1, S):
+        at = pl.ds(pl.multiple_of(lax.rem(s + k, S) * PB, 64), PB)
+        send(og_x.at[0, at, :], og_r.at[k - 1], k_og + k, plane(k))
     settle(old)
     arrive(out_o.at[other_rows, :], k_out)
     store(out_o, out_h)

time: 169 us -> 169 us (level)
  no operation moved by 1% of the time
where the time goes in v7:
time: 169 us; the launch traced here: 168 us
  Pallas kernels  167 us (99%)
    pallas_call x1, Pallas kernels, fast_layer(): pl.pallas_call(functools.partial(layer_kernel, dims), out_shape=outs, in_...  163 us
    pallas_call x1, Pallas kernels, fast_layer(): pl.pallas_call(functools.partial(unpack_kernel, CH), out_shape=[jax.Shape...  3.83 us

profile of v7, /device:TPU:17, one launch (start us, length us, event | category | flops | bytes accessed | tf_op | source)
XLA Modules:
  0.0 168.4 jit_solution(15283490097529647747)
XLA Ops:
  1.3 163.1 %shard_map.305 = (bf16[512,768]{1,0:T(8,128)(2,1)}, f32[512,768]{1,0:T(8,128)}, f32[48,3072]{1,0:T(8,128)}, f32[48,512]{1,0:T(8,128)}, f32[2,48,768]{2,1,0:T(8,128)}, /*index=5*/f32[16,768]{1,0:T(8,128)}) custom-call(bf16[512,768]{1,0:T(8,128)(2,1)} %bitcast.8, bf16[512,768]{1,0:T(8,128)(2,1)} %bitcast.9, s32[1]{0:T(128)S(6)} %copy.35.lengths, f32[768]{0:T(1024)} %v_gain1.1, ...), custom_call_target="tpu_custom_call" | custom-call | tf_op jit(solution)/shard_map/pallas_call | solution.py:1703
  164.4 3.8 %shard_map.306 = (bf16[512,768]{1,0:T(8,128)(2,1)}, f32[512,768]{1,0:T(8,128)}, f32[48,384]{1,0:T(8,128)}, f32[48,384]{1,0:T(8,128)}, f32[48,384]{1,0:T(8,128)},...) custom-call(bf16[512,768]{1,0:T(8,128)(2,1)} %get-tuple-element.40.o, ...), custom_call_target="tpu_custom_call" | custom-call | tf_op jit(solution)/shard_map/pallas_call | solution.py:1733
